TPU v7x, 128 devices: a whole 4x4x4 slice. The times are simulated.
128 devices in a mesh: row: 16 (over x, z), col: 8 (over y, core).
Axes of the slice: x: 4, y: 4, z: 4, core: 2. Of those that a mesh axis runs over, the one named last changes fastest.
Arguments:
- trailing: bfloat16 [49152, 16384], P('row', 'col'), may hold values from -6 to 6
- panels: bfloat16 [2, 256, 49152], P(None, 'col', 'row'), as said below
- diag_lower: bfloat16 [2, 256, 256], P(None, 'col'), as said below
- pivot_src: int32 [2, 256], replicated, may hold values from 0 to 49151, as said below
- pivot_dst: int32 [2, 256], replicated, may hold values from 256 to 49152, as said below
Outputs:
- matrix: bfloat16 [49152, 16384], P('row', 'col')
Inputs may be any that keep to these rules, and one draw needn't show every extreme that they name: The entries of pivot_src[k] are distinct rows, none below 256 * k. Entries of pivot_dst[k] under 49152 are distinct, not below 256 * (k + 1), and are exactly the entries of pivot_src[k] that are not below 256 * (k + 1); an entry equal to 49152 marks an old row t + j that is itself one of pivot_src[k]. panels[k, c, r] is zero for r < 256 * (k + 1). diag_lower[k, r, c] is zero for c >= r.
All inputs are finite; a program needn't handle non-finite values.
Results may differ from a plain program's by a relative error of at most 0.0062.
Values may be sent and summed in bfloat16 or wider, within the bound.
No kernel may reach another device: no remote copies, remote signals or barrier semaphores. Data moves between devices by JAX's collectives and lax.ppermute only.
A program may use at most 128 MiB of HBM per device.

v0:
```python
import jax
import jax.numpy as jnp
from jax import lax
from jax.sharding import PartitionSpec as P


def broadcast(x, axis, root):
    mine = lax.axis_index(axis) == root
    return lax.psum(jnp.where(mine, x, jnp.zeros_like(x)), axis)


def per_device(trailing, panels, diag_lower, pivot_src, pivot_dst):
    rows_dev, cols_dev = trailing.shape
    panel_width = diag_lower.shape[2]
    row_index = lax.axis_index("row")
    offset = row_index * rows_dev
    identity = jnp.eye(panel_width, dtype=jnp.float32)
    matrix = trailing
    for panel_step in range(pivot_src.shape[0]):
        start_row = panel_step * panel_width
        sources = pivot_src[panel_step] - offset
        holding = (sources >= 0) & (sources < rows_dev)
        picked = jnp.take(matrix, jnp.clip(sources, 0, rows_dev - 1), axis=0)
        picked = jnp.where(holding[:, None], picked, jnp.zeros((), jnp.bfloat16))
        top_rows = matrix[start_row : start_row + panel_width]
        displaced = broadcast(top_rows, "row", 0)
        targets = pivot_dst[panel_step] - offset
        targets = jnp.where((targets >= 0) & (targets < rows_dev), targets, rows_dev)
        swapped = matrix.at[targets].set(displaced, mode="drop")
        factor = lax.all_gather(diag_lower[panel_step], "col", axis=0, tiled=True)
        unit_lower = factor.astype(jnp.float32) + identity
        block_rows = lax.psum(picked, "row").astype(jnp.float32)
        upper_rows = jax.scipy.linalg.solve_triangular(
            unit_lower, block_rows, lower=True, unit_diagonal=True
        ).astype(jnp.bfloat16)
        product = lax.dot_general(
            lax.all_gather(panels[panel_step], "col", axis=0, tiled=True),
            upper_rows,
            (((0,), (0,)), ((), ())),
            preferred_element_type=jnp.float32,
        )
        result = (swapped.astype(jnp.float32) - product).astype(jnp.bfloat16)
        current = result[start_row : start_row + panel_width]
        matrix = result.at[start_row : start_row + panel_width].set(
            jnp.where(row_index == 0, upper_rows, current)
        )
    return matrix


def solution(mesh):
    placed = (P("row", "col"), P(None, "col", "row"), P(None, "col", None), P(), P())
    return jax.shard_map(
        per_device, mesh=mesh, in_specs=placed, out_specs=P("row", "col"), check_vma=False
    )
```

profile of v0, /device:TPU:0, one launch (start us, length us, event | category | flops | bytes accessed | tf_op | source)
XLA Modules:
  0.0 298.1 jit_solution(11988537814029890667)
XLA Ops:
  7.4 10.7 %copy.35 = bf16[3072,2048]{1,0:T(8,128)(2,1)} copy(bf16[3072,2048]{1,0:T(8,128)(2,1)} %param.13) | data formatting | bytes 25165824
  18.2 8.6 %gather_fusion = bf16[256,2048]{1,0:T(8,128)(2,1)S(1)} fusion(bf16[3072,2048]{1,0:T(8,128)(2,1)} %copy.35, s32[1024]{0:T(1024)S(1)} %pad_clamp_fusion.1), kind=kCustom, calls=%fused_computation.clone | custom fusion | bytes 2098176 | tf_op jit(solution)/shard_map/jit(_take)/gather | solution.py:23
  26.8 2.8 select_select_fusion.1
  30.6 13.4 %all-gather = bf16[1,256,256]{2,1,0:T(8,128)(2,1)S(1)} all-gather(bf16[1,32,256]{2,1,0:T(8,128)(2,1)S(1)} %get-tuple-element.76), channel_id=2, replica_groups=mesh['row'=16,'col'=8] {'col'}, dimensions={1}, use_global_device_ids=true | all-gather | bytes 147456 | tf_op jit(solution)/shard_map/all_gather | solution.py:30
  44.0 13.3 %all-gather.2 = bf16[1,256,256]{2,1,0:T(8,128)(2,1)S(1)} all-gather(bf16[1,32,256]{2,1,0:T(8,128)(2,1)S(1)} %get-tuple-element.75), channel_id=4, replica_groups=mesh['row'=16,'col'=8] {'col'}, dimensions={1}, use_global_device_ids=true | all-gather | bytes 147456 | tf_op jit(solution)/shard_map/all_gather | solution.py:30
  57.5 4.3 %while.6 = (s32[]{:T(128)}, f32[256,256]{1,0:T(8,128)S(1)}, s32[2,2]{1,0:T(2,128)S(1)}, f32[2,128,128]{2,1,0:T(8,128)S(1)}, s32[]{:T(128)}) while((s32[]{:T(128)}, f32[256,256]{1,0:T(8,128)S(1)}, s32[2,2]{1,0:T(2,128)S(1)}, f32[2,128,128]{2,1,0:T(8,128)S(1)}, s32[]{:T(128)}) %tuple.51), condition=%wide.while_cond.2, body=%wide.while_body.2.sunk | while | flops 2 | bytes 131181 | solution.py:33
  58.2 1.5 bitcast_dynamic-update-slice_fusion.4
  60.3 1.5 bitcast_dynamic-update-slice_fusion.4
  61.8 19.7 %custom-call.4 = f32[2,128,128]{1,2,0:T(8,128)S(1)} custom-call(f32[2,128,128]{2,1,0:T(8,128)S(1)} %get-tuple-element.45), custom_call_target="InvertDiagBlocksLowerTriangular" | custom-call | tf_op jit(solution)/shard_map/jit(_solve_triangular)/triangular_solve | solution.py:33
  81.6 41.5 %all-reduce.7.cloned.1.call-done = (bf16[256,2048]{1,0:T(8,128)(2,1)}, bf16[256,2048]{1,0:T(8,128)(2,1)}) async-done(((bf16[256,2048]{1,0:T(8,128)(2,1)}, bf16[256,2048]{1,0:T(8,128)(2,1)}), (bf16[256,2048]{1,0:T(8,128)(2,1)}, bf16[256,2048]{1,0:T(8,128)(2,1)})) %all-reduce.7.cloned.1.call-update) | async-done | bytes 2097168 | tf_op jit(solution)/shard_map/psum | solution.py:9
  123.1 1.5 convert_element_type.38
  124.5 14.9 %scatter_fusion = bf16[3072,2048]{1,0:T(8,128)(2,1)} fusion(bf16[3072,2048]{1,0:T(8,128)(2,1)} %copy.35, s32[256]{0:T(256)S(1)} %bitcast.65, bf16[256,2048]{1,0:T(8,128)(2,1)} %get-tuple-element.67), kind=kCustom, calls=%fused_computation.2 | custom fusion | bytes 3146752 | tf_op jit(solution)/shard_map/scatter | solution.py:29
  140.5 1.8 convolution_subtract_fusion.1
  143.5 9.9 %fusion.1 = bf16[3072,2048]{1,0:T(8,128)(2,1)} fusion(bf16[3072,2048]{1,0:T(8,128)(2,1)} %scatter_fusion, bf16[1,256,3072]{2,1,0:T(8,128)(2,1)} %all-gather.7.cloned.1.call-done, bf16[128,2048]{1,0:T(8,128)(2,1)S(1)} %fusion.15, f32[128,2048]{1,0:T(8,128)S(1)} %fusion.8), kind=kOutput, calls=%fused_computation.11 | convolution fusion | flops 3242196992 | bytes 28311552 | tf_op jit(solution)/shard_map/dot_general | solution.py:36
  153.4 2.5 fusion.7
  155.9 2.3 slice_select_fusion.1
  158.2 8.6 %gather_fusion.1 = bf16[256,2048]{1,0:T(8,128)(2,1)S(1)} fusion(bf16[3072,2048]{1,0:T(8,128)(2,1)} %fusion.7, s32[1024]{0:T(1024)S(1)} %pad_clamp_fusion), kind=kCustom, calls=%fused_computation.1.clone | custom fusion | bytes 2098176 | tf_op jit(solution)/shard_map/jit(_take)/gather | solution.py:23
  168.6 3.8 %while.7 = (s32[]{:T(128)}, f32[256,256]{1,0:T(8,128)S(1)}, s32[2,2]{1,0:T(2,128)S(1)}, f32[2,128,128]{2,1,0:T(8,128)S(1)}, s32[]{:T(128)}) while((s32[]{:T(128)}, f32[256,256]{1,0:T(8,128)S(1)}, s32[2,2]{1,0:T(2,128)S(1)}, f32[2,128,128]{2,1,0:T(8,128)S(1)}, s32[]{:T(128)}) %tuple.67), condition=%wide.while_cond.2.clone, body=%wide.while_body.2.clone.sunk | while | flops 2 | bytes 131181 | solution.py:33
  172.4 19.7 %custom-call.5 = f32[2,128,128]{1,2,0:T(8,128)S(1)} custom-call(f32[2,128,128]{2,1,0:T(8,128)S(1)} %get-tuple-element.46), custom_call_target="InvertDiagBlocksLowerTriangular" | custom-call | tf_op jit(solution)/shard_map/jit(_solve_triangular)/triangular_solve | solution.py:33
  192.1 66.2 %all-reduce.5.cloned.1.call-done = (bf16[256,2048]{1,0:T(8,128)(2,1)}, bf16[256,2048]{1,0:T(8,128)(2,1)}) async-done(((bf16[256,2048]{1,0:T(8,128)(2,1)}, bf16[256,2048]{1,0:T(8,128)(2,1)}), (bf16[256,2048]{1,0:T(8,128)(2,1)}, bf16[256,2048]{1,0:T(8,128)(2,1)})) %all-reduce.5.cloned.1.call-update) | async-done | bytes 2097168 | tf_op jit(solution)/shard_map/psum | solution.py:9
  258.3 1.5 convert_element_type.43
  259.8 15.0 %scatter_fusion.1 = bf16[3072,2048]{1,0:T(8,128)(2,1)} fusion(bf16[3072,2048]{1,0:T(8,128)(2,1)} %fusion.7, s32[256]{0:T(256)S(1)} %bitcast.64, bf16[256,2048]{1,0:T(8,128)(2,1)} %get-tuple-element.65), kind=kCustom, calls=%fused_computation.3 | custom fusion | bytes 3146752 | tf_op jit(solution)/shard_map/scatter | solution.py:29
  278.0 9.9 %fusion = bf16[3072,2048]{1,0:T(8,128)(2,1)} fusion(bf16[3072,2048]{1,0:T(8,128)(2,1)} %scatter_fusion.1, bf16[1,256,3072]{2,1,0:T(8,128)(2,1)} %all-gather.9.cloned.1.call-done, bf16[128,2048]{1,0:T(8,128)(2,1)S(1)} %fusion.13, f32[128,2048]{1,0:T(8,128)S(1)} %fusion.5), kind=kOutput, calls=%fused_computation.9 | convolution fusion | flops 3242196992 | bytes 28311552 | tf_op jit(solution)/shard_map/dot_general | solution.py:36
  287.9 2.5 fusion.4
  (57 shorter events, 13.4 us)
Async XLA Ops:
  7.4 10.7 %copy-start.3 = (s32[2,256]{1,0:T(2,128)S(1)}, s32[2,256]{1,0:T(2,128)}, u32[]{:S(2)}) copy-start(s32[2,256]{1,0:T(2,128)} %param.16) | copy-start | bytes 6148
  7.4 115.7 %all-reduce.7.cloned.1.call-start = ((), (), s32[]{:S(2)}) async-start(), calls=%async_computation.3 | async-start | bytes 4194304 | tf_op jit(solution)/shard_map/psum | solution.py:9
  18.1 11.6 %copy-start.1 = (bf16[2,32,3072]{2,1,0:T(8,128)(2,1)S(1)}, bf16[2,32,3072]{2,1,0:T(8,128)(2,1)}, u32[]{:S(2)}) copy-start(bf16[2,32,3072]{2,1,0:T(8,128)(2,1)} %param.14) | copy-start | bytes 1179652
  18.1 12.5 %copy-start.2 = (bf16[2,32,256]{2,1,0:T(8,128)(2,1)S(1)}, bf16[2,32,256]{2,1,0:T(8,128)(2,1)}, u32[]{:S(2)}) copy-start(bf16[2,32,256]{2,1,0:T(8,128)(2,1)} %param.15) | copy-start | bytes 98308
  18.1 63.4 %copy-start.4 = (s32[2,256]{1,0:T(2,128)S(1)}, s32[2,256]{1,0:T(2,128)}, u32[]{:S(2)}) copy-start(s32[2,256]{1,0:T(2,128)} %param.17) | copy-start | bytes 6148
  29.7 113.8 %all-gather.7.cloned.1.call-start = ((), (), s32[]{:S(2)}) async-start(), calls=%async_computation | async-start | bytes 1769472 | tf_op jit(solution)/shard_map/all_gather | solution.py:37
  30.5 227.8 %all-reduce.5.cloned.1.call-start = ((), (), s32[]{:S(2)}) async-start(), calls=%async_computation.2 | async-start | bytes 4194304 | tf_op jit(solution)/shard_map/psum | solution.py:9
  61.8 61.3 %copy-start = (f32[256,256]{1,0:T(8,128)}, f32[256,256]{1,0:T(8,128)S(1)}, u32[]{:S(2)}) copy-start(f32[256,256]{1,0:T(8,128)S(1)} %get-tuple-element.190) | copy-start | bytes 786436
  61.8 61.3 %copy-start.5 = (s32[2,2]{1,0:T(2,128)}, s32[2,2]{1,0:T(2,128)S(1)}, u32[]{:S(2)}) copy-start(s32[2,2]{1,0:T(2,128)S(1)} %get-tuple-element.203) | copy-start | bytes 52
  153.4 15.2 %copy-start.6 = (s32[2,2]{1,0:T(2,128)S(1)}, s32[2,2]{1,0:T(2,128)}, u32[]{:S(2)}) copy-start(s32[2,2]{1,0:T(2,128)} %copy-done.5) | copy-start | bytes 52
  168.0 110.0 %all-gather.9.cloned.1.call-start = ((), (), s32[]{:S(2)}) async-start(), calls=%async_computation.1 | async-start | bytes 1769472 | tf_op jit(solution)/shard_map/all_gather | solution.py:37
Sparse Core Ops, SparseCore 0:
  29.8 93.2 all-reduce.6
  168.1 90.1 all-reduce.4
Sparse Core Ops, SparseCore 1:
  31.9 27.0 all-gather.6
  170.1 23.9 all-gather.8
where the time goes:
time: 303 us; the launch traced here: 298 us
  waiting for transfers between devices  108 us (36%)
  local copies, waits for them, and re-layouts  66.8 us (22%)
  other arithmetic  53.9 us (18%)
  matrix products  26.8 us (9%)
  blocking collectives  26.6 us (9%)
  between operations  15.4 us (5%)
    psum x2, waiting for transfers between devices, broadcast(): return lax.psum(jnp.where(mine, x, jnp.zeros_like(x)), axis)  108 us
    another operation x5, other arithmetic, per_device(): jax.scipy.linalg.solve_triangular(unit_lower, block_rows, lower=True, uni...  39.5 us
    scatter x2, local copies, waits for them, and re-layouts, per_device(): swapped = matrix.at[targets].set(displaced, mode='drop')  30 us
    all_gather x2, blocking collectives, per_device(): factor = lax.all_gather(diag_lower[panel_step], 'col', axis=0, tiled=True)  26.6 us
    dot_general x2, matrix products, per_device(): lax.dot_general(lax.all_gather(panels[panel_step], 'col', axis=0, tiled=T...  19.8 us
    gather x2, local copies, waits for them, and re-layouts, per_device(): picked = jnp.take(matrix, jnp.clip(sources, 0, rows_dev - 1), axis=0)  17.2 us
    unnamed x15, local copies, waits for them, and re-layouts  10.8 us
    another operation x15, local copies, waits for them, and re-layouts, per_device(): jax.scipy.linalg.solve_triangular(unit_lower, block_rows, lower=True, uni...  8.1 us
  transfers between devices with their start and end apart: 4, of which 2 were waited for; matrix products, arithmetic and copies ran while one was open for 30% of the time, Pallas kernels for 0%

commit v1 on v0

v1 whole, which is shorter than its diff:
```python
import functools

import jax
import jax.numpy as jnp
from jax import lax
from jax.experimental import pallas as pl
from jax.experimental.pallas import tpu as pltpu
from jax.sharding import PartitionSpec as P

F32, BF16 = jnp.float32, jnp.bfloat16
TN = (((0,), (0,)), ((), ()))
NN = (((1,), (0,)), ((), ()))


def dot(a, b, dims=NN):
    return lax.dot_general(a, b, dims, preferred_element_type=F32)


def solve_kernel(inv_ref, sel_ref, c_ref, u_ref):
    width = inv_ref.shape[1]

    def apply(k, rows):
        rest = inv_ref[k]
        total = None
        for _ in range(3):
            part = rest.astype(BF16)
            rest = rest - part.astype(F32)
            term = dot(part, rows)
            total = term if total is None else total + term
        return total.astype(BF16)

    first = apply(0, c_ref[:width, :])
    u_ref[:width, :] = first
    later = c_ref[width : 2 * width, :].astype(F32) - dot(sel_ref[...], first, TN)
    u_ref[width : 2 * width, :] = apply(1, later.astype(BF16))


def solve(inverse, selected, rows, tile=512):
    width, cols = inverse.shape[1], rows.shape[1]
    return pl.pallas_call(
        solve_kernel,
        out_shape=jax.ShapeDtypeStruct((2 * width, cols), BF16),
        grid=(cols // tile,),
        in_specs=[
            pl.BlockSpec(inverse.shape, lambda i: (0, 0, 0)),
            pl.BlockSpec(selected.shape, lambda i: (0, 0)),
            pl.BlockSpec((2 * width, tile), lambda i: (0, i)),
        ],
        out_specs=pl.BlockSpec((2 * width, tile), lambda i: (0, i)),
        compiler_params=pltpu.CompilerParams(vmem_limit_bytes=32 << 20),
    )(inverse, selected, rows)


def update_kernel(width, begin, hole, slot, place, a_ref, l0_ref, l1_ref, u_ref, d_ref, o_ref, x_ref, df_ref):
    step = pl.program_id(0)
    rows = a_ref.shape[0]

    @pl.when(step == 0)
    def _():
        df_ref[...] = d_ref[...].astype(F32)

    x_ref[...] = a_ref[...].astype(F32)

    def fill(j, carry):
        x_ref[pl.ds(hole[j] - step * rows, 1), :] = df_ref[pl.ds(slot[j], 1), :]
        return carry

    lax.fori_loop(begin[step], begin[step + 1], fill, 0)
    mid = (x_ref[...] - dot(l0_ref[...], u_ref[:width, :], TN)).astype(BF16).astype(F32)
    o_ref[...] = (mid - dot(l1_ref[...], u_ref[width:, :], TN)).astype(BF16)

    @pl.when((place[0] == 0) & (step < 2 * width // rows))
    def _():
        o_ref[...] = u_ref[pl.ds(pl.multiple_of(step * rows, rows), rows), :]


def update(slab, l0, l1, upper, displaced, begin, hole, slot, place, rows):
    height, cols = slab.shape
    width, n = l0.shape[0], displaced.shape[0]
    return pl.pallas_call(
        functools.partial(update_kernel, width),
        out_shape=jax.ShapeDtypeStruct(slab.shape, BF16),
        grid_spec=pltpu.PrefetchScalarGridSpec(
            num_scalar_prefetch=4,
            grid=(height // rows,),
            in_specs=[
                pl.BlockSpec((rows, cols), lambda i, *_: (i, 0)),
                pl.BlockSpec((width, rows), lambda i, *_: (0, i)),
                pl.BlockSpec((width, rows), lambda i, *_: (0, i)),
                pl.BlockSpec((2 * width, cols), lambda i, *_: (0, 0)),
                pl.BlockSpec((n, cols), lambda i, *_: (0, 0)),
            ],
            out_specs=pl.BlockSpec((rows, cols), lambda i, *_: (i, 0)),
            scratch_shapes=[pltpu.VMEM((rows, cols), F32), pltpu.VMEM((n, cols), F32)],
        ),
        compiler_params=pltpu.CompilerParams(vmem_limit_bytes=48 << 20),
        cost_estimate=pl.CostEstimate(
            flops=4 * height * cols * width, bytes_accessed=4 * height * cols, transcendentals=0
        ),
    )(begin, hole, slot, place, slab, l0, l1, upper, displaced)


def per_device(trailing, panels, diag_lower, pivot_src, pivot_dst):
    height, cols = trailing.shape
    width = diag_lower.shape[2]
    block = 256
    devices = lax.axis_size("row")
    place = lax.axis_index("row")
    offset = place * height
    count = jnp.arange(width, dtype=jnp.int32)
    here = jnp.arange(height, dtype=jnp.int32)
    src0, src1 = pivot_src[0], pivot_src[1]
    dst0, dst1 = pivot_dst[0], pivot_dst[1]

    def original(position):
        hit = dst0[None, :] == position[:, None]
        return jnp.where(hit.any(1), (hit * count).sum(1), position)

    wanted = jnp.concatenate([src0, original(src1)]) - offset
    onehot = (wanted[:, None] == here[None, :]).astype(BF16)
    picked = dot(onehot, trailing).astype(BF16)
    top = jnp.where(place == 0, trailing[: 2 * width], jnp.zeros((), BF16))
    moved = lax.psum((picked, top), "row")

    whole = lax.all_gather(panels, "col", axis=1, tiled=True)

    position = jnp.concatenate([src1, width + count]) - offset
    chosen = (here[:, None] == position[None, :]).astype(BF16)
    piece = dot(panels[0], chosen).astype(BF16)
    piece = lax.all_to_all(jnp.broadcast_to(piece[None], (devices,) + piece.shape), "row", 0, 0)
    piece = piece.astype(F32).sum(0).astype(BF16)
    small = lax.all_gather(
        jnp.concatenate([piece, diag_lower[0], diag_lower[1]], axis=1), "col", axis=0, tiled=True
    )
    selected, below = small[:, :width], small[:, width : 2 * width]
    unit = jnp.stack([small[:, 2 * width : 3 * width], small[:, 3 * width :]]).astype(F32)
    eye = jnp.eye(width, dtype=F32)
    inverse = jax.scipy.linalg.solve_triangular(
        unit + eye, jnp.broadcast_to(eye, unit.shape), lower=True, unit_diagonal=True
    )

    again = (dst0[:, None] == dst1[None, :]).any(1)
    rest = jnp.concatenate([jnp.where(again, devices * height, dst0), dst1]) - offset
    origin = jnp.concatenate([count, original(width + count)])
    rest = jnp.where((rest >= 0) & (rest < height), rest, height)
    key = rest * (2 * width) + jnp.arange(2 * width, dtype=jnp.int32)
    rank = (key[None, :] < key[:, None]).sum(1)
    place_of = rank[None, :] == jnp.arange(2 * width, dtype=jnp.int32)[:, None]
    hole = jnp.where(place_of, rest[None, :], 0).sum(1)
    slot = jnp.where(place_of, origin[None, :], 0).sum(1)
    edges = jnp.arange(height // block + 1, dtype=jnp.int32) * block
    begin = (rest[None, :] < edges[:, None]).sum(1).astype(jnp.int32)

    landing = (dst1 - offset)[:, None] == here[None, :]
    l0 = jnp.where(landing.any(0)[None, :], dot(below, landing.astype(BF16)).astype(BF16), whole[0])

    upper = solve(inverse, selected, moved[0])
    return update(
        trailing, l0, whole[1], upper, moved[1], begin, hole, slot, place[None].astype(jnp.int32), block
    )


def solution(mesh):
    placed = (P("row", "col"), P(None, "col", "row"), P(None, "col", None), P(), P())
    return jax.shard_map(
        per_device, mesh=mesh, in_specs=placed, out_specs=P("row", "col"), check_vma=False
    )
```

time: 303 us -> 172 us (0.57); the launches traced: 298 us -> 171 us
  waiting for transfers between devices: 108 us -> 41.5 us
  local copies, waits for them, and re-layouts: 66.8 us -> 10.9 us
  Pallas kernels: 0 us -> 22.9 us
  matrix products: 26.8 us -> 14 us
  blocking collectives: 26.6 us -> 13.8 us
  other arithmetic: 53.9 us -> 44.7 us
  starting transfers between devices: 0.34 us -> 8.01 us
    psum x2 -> x1, waiting for transfers between devices: 108 us -> 26.9 us  [per_device(): moved = lax.psum((picked, top), 'row')]
    scatter x2 -> x0, local copies, waits for them, and re-layouts: 30 us -> none  [per_device(): swapped = matrix.at[targets].set(displaced, mode='drop')]
    pallas_call x0 -> x2, Pallas kernels: none -> 22.9 us  [the longest x1 18.9 us: update(): pl.pallas_call(functools.partial(update_kernel, width), out_shape=jax.Sha...]
    gather x2 -> x0, local copies, waits for them, and re-layouts: 17.2 us -> none  [per_device(): picked = jnp.take(matrix, jnp.clip(sources, 0, rows_dev - 1), axis=0)]
    all_to_all x0 -> x1, waiting for transfers between devices: none -> 14.1 us  [per_device(): lax.all_to_all(jnp.broadcast_to(piece[None], (devices,) + piece.shape), '...]
    all_gather x2 -> x1, blocking collectives: 26.6 us -> 13.8 us  [per_device(): lax.all_gather(jnp.concatenate([piece, diag_lower[0], diag_lower[1]], axi...]
    unnamed x15 -> x10, local copies, waits for them, and re-layouts: 10.8 us -> 2.65 us
    all_to_all x0 -> x1, starting transfers between devices: none -> 7.96 us  [per_device(): lax.all_to_all(jnp.broadcast_to(piece[None], (devices,) + piece.shape), '...]
  transfers between devices with their start and end apart: 4 -> 3, of which waited for: 2 -> 2; matrix products, arithmetic and copies ran while one was open for 30% -> 28% of each run, Pallas kernels for 0% -> 2%
where the time goes in v1:
time: 172 us; the launch traced here: 171 us
  other arithmetic  44.7 us (26%)
  waiting for transfers between devices  41.5 us (24%)
  Pallas kernels  22.9 us (13%)
  between operations  15.1 us (9%)
  matrix products  14 us (8%)
  blocking collectives  13.8 us (8%)
  local copies, waits for them, and re-layouts  10.9 us (6%)
  starting transfers between devices  8.01 us (5%)
    another operation x7, other arithmetic, per_device(): jax.scipy.linalg.solve_triangular(unit + eye, jnp.broadcast_to(eye, unit....  39.6 us
    psum x1, waiting for transfers between devices, per_device(): moved = lax.psum((picked, top), 'row')  26.9 us
    pallas_call x1, Pallas kernels, update(): pl.pallas_call(functools.partial(update_kernel, width), out_shape=jax.Sha...  18.9 us
    all_to_all x1, waiting for transfers between devices, per_device(): lax.all_to_all(jnp.broadcast_to(piece[None], (devices,) + piece.shape), '...  14.1 us
    all_gather x1, blocking collectives, per_device(): lax.all_gather(jnp.concatenate([piece, diag_lower[0], diag_lower[1]], axi...  13.8 us
    dot_general x3, matrix products, dot(): return lax.dot_general(a, b, dims, preferred_element_type=F32)  12.7 us
    all_to_all x1, starting transfers between devices, per_device(): lax.all_to_all(jnp.broadcast_to(piece[None], (devices,) + piece.shape), '...  7.96 us
    another operation x6, local copies, waits for them, and re-layouts  4.1 us
  transfers between devices with their start and end apart: 3, of which 2 were waited for; matrix products, arithmetic and copies ran while one was open for 28% of the time, Pallas kernels for 2%

profile of v1, /device:TPU:0, one launch (start us, length us, event | category | flops | bytes accessed | tf_op | source)
XLA Modules:
  0.0 170.9 jit_solution(4464857686320058199)
XLA Ops:
  7.4 0.8 fusion.27
  8.1 0.8 fusion.28
  9.5 10.7 %fusion.6 = bf16[512,2048]{1,0:T(8,128)(2,1)} fusion(bf16[3072,2048]{1,0:T(8,128)(2,1)} %a_ref.1, s32[512]{0:T(512)S(1)} %add_subtract_fusion.1), kind=kOutput, calls=%fused_computation.12 | convolution fusion | flops 6445072384 | bytes 14682112 | tf_op jit(solution)/shard_map/dot_general | solution.py:16
  20.2 3.1 %slice_select_fusion = bf16[512,2048]{1,0:T(8,128)(2,1)} fusion(bf16[3072,2048]{1,0:T(8,128)(2,1)} %a_ref.1, pred[]{:T(512)S(6)} %eq.130), kind=kLoop, calls=%fused_computation.13 | loop fusion | flops 1048576 | bytes 4194305 | tf_op jit(solution)/shard_map/jit(_where)/select_n | solution.py:122
  23.4 0.5 all-gather.2.cloned.1.call-update
  24.3 1.1 fusion.9
  25.4 0.8 broadcast_in_dim.78
  26.3 8.0 %all-to-all-start = ((bf16[16,32,512]{2,1,0:T(8,128)(2,1)}), bf16[16,32,512]{2,1,0:T(8,128)(2,1)S(1)}, u32[]{:S(2)}, u32[]{:S(2)}) async-start(bf16[16,32,512]{2,1,0:T(8,128)(2,1)} %broadcast_in_dim.78), calls=%async_computation | async-start | bytes 1048576 | tf_op jit(solution)/shard_map/all_to_all | solution.py:130
  34.7 0.5 fusion.5
  35.8 14.1 %all-to-all-done = bf16[16,32,512]{2,1,0:T(8,128)(2,1)S(1)} async-done(((bf16[16,32,512]{2,1,0:T(8,128)(2,1)}), bf16[16,32,512]{2,1,0:T(8,128)(2,1)S(1)}, u32[]{:S(2)}, u32[]{:S(2)}) %all-to-all-start) | async-done | bytes 524320 | tf_op jit(solution)/shard_map/all_to_all | solution.py:130
  50.0 13.8 %all_gather.6 = bf16[256,1024]{1,0:T(8,128)(2,1)S(1)} all-gather(bf16[32,1024]{1,0:T(8,128)(2,1)S(1)} %pad_maximum_fusion.1), channel_id=1, replica_groups=mesh['row'=16,'col'=8] {'col'}, dimensions={0}, use_global_device_ids=true | all-gather | bytes 589824 | tf_op jit(solution)/shard_map/all_gather | solution.py:132
  64.0 4.1 %while.1 = (s32[]{:T(128)}, f32[2,256,256]{2,1,0:T(8,128)S(1)}, s32[2,2]{1,0:T(2,128)S(1)}, f32[2,2,128,128]{3,2,0,1:T(8,128)S(1)}, s32[]{:T(128)}) while((s32[]{:T(128)}, f32[2,256,256]{2,1,0:T(8,128)S(1)}, s32[2,2]{1,0:T(2,128)S(1)}, f32[2,2,128,128]{3,2,0,1:T(8,128)S(1)}, s32[]{:T(128)}) %tuple.33), condition=%wide.while_cond, body=%wide.while_body.sunk | while | flops 2 | bytes 262261 | solution.py:138
  64.0 0.6 fusion.33
  64.6 1.4 bitcast_dynamic-update-slice_fusion.2
  66.1 0.6 fusion.33
  66.7 1.4 bitcast_dynamic-update-slice_fusion.2
  68.1 39.3 %custom-call.4 = f32[2,2,128,128]{2,3,1,0:T(8,128)S(1)} custom-call(f32[2,2,128,128]{3,2,1,0:T(8,128)S(1)} %bitcast.59), custom_call_target="InvertDiagBlocksLowerTriangular" | custom-call | tf_op jit(solution)/shard_map/jit(_solve_triangular)/vmap()/triangular_solve | solution.py:138
  108.7 26.9 %all-reduce.3.cloned.1.call-done = (bf16[512,2048]{1,0:T(8,128)(2,1)}, bf16[512,2048]{1,0:T(8,128)(2,1)}) async-done(((bf16[512,2048]{1,0:T(8,128)(2,1)}, bf16[512,2048]{1,0:T(8,128)(2,1)}), (bf16[512,2048]{1,0:T(8,128)(2,1)}, bf16[512,2048]{1,0:T(8,128)(2,1)})) %all-reduce.3.cloned.1.call-update) | async-done | bytes 4194320 | tf_op jit(solution)/shard_map/psum | solution.py:123
  135.6 1.6 copy-done
  137.2 3.9 %shard_map.55.u_ref = bf16[512,2048]{1,0:T(8,128)(2,1)S(1)} custom-call(f32[2,256,256]{2,1,0:T(8,128)S(1)} %pad_maximum_fusion.inv_ref, bf16[256,256]{1,0:T(8,128)(2,1)S(1)} %get-tuple-element.34.sel_ref, bf16[512,2048]{1,0:T(8,128)(2,1)S(1)} %copy-done), custom_call_target="tpu_custom_call" | custom-call | tf_op jit(solution)/shard_map/pallas_call | solution.py:40
  141.2 1.7 slice_bitcast_fusion.l1_ref
  142.9 0.7 copy-done.1
  143.5 1.0 fusion.2.l0_ref
  144.5 18.9 %shard_map.56 = bf16[3072,2048]{1,0:T(8,128)(2,1)} custom-call(s32[13]{0:T(128)S(1)} %convert_reduce_fusion.1.begin, s32[512]{0:T(512)S(1)} %get-tuple-element.14.hole, s32[512]{0:T(512)S(1)} %get-tuple-element.13.slot, s32[1]{0:T(128)} %bitcast.3.place, bf16[3072,2048]{1,0:T(8,128)(2,1)} %a_ref.1, bf16[256,3072]{1,0:T(8,128)(2,1)S(1)} %fusion.2.l0_ref, ...), custom_call_target="tpu_custom_call" | custom-call | flops 6442450944 | bytes 25165824 | tf_op jit(solution)/shard_map/pallas_call | solution.py:80
  (46 shorter events, 3.6 us)
Async XLA Ops:
  7.4 128.2 %all-reduce.3.cloned.1.call-start = ((), (), s32[]{:S(2)}) async-start(), calls=%async_computation.2 | async-start | bytes 8388608 | tf_op jit(solution)/shard_map/psum | solution.py:123
  23.3 0.7 copy-start.4
  23.3 1.0 copy-start.2
  23.3 12.3 %copy-start.3 = (bf16[2,32,256]{2,1,0:T(8,128)(2,1)S(1)}, bf16[2,32,256]{2,1,0:T(8,128)(2,1)}, u32[]{:S(2)}) copy-start(bf16[2,32,256]{2,1,0:T(8,128)(2,1)} %param.7) | copy-start | bytes 98308
  23.3 117.8 %all-gather.2.cloned.1.call-start = ((), (), s32[]{:S(2)}) async-start(), calls=%async_computation.1 | async-start | bytes 3538944 | tf_op jit(solution)/shard_map/all_gather | solution.py:125
  26.3 23.6 %all-to-all-start = ((bf16[16,32,512]{2,1,0:T(8,128)(2,1)}), bf16[16,32,512]{2,1,0:T(8,128)(2,1)S(1)}, u32[]{:S(2)}, u32[]{:S(2)}) async-start(bf16[16,32,512]{2,1,0:T(8,128)(2,1)} %broadcast_in_dim.78), calls=%async_computation | async-start | bytes 1048576 | tf_op jit(solution)/shard_map/all_to_all | solution.py:130
  135.6 1.6 copy-start
  141.2 2.4 %copy-start.1 = (bf16[2,256,3072]{2,1,0:T(8,128)(2,1)S(1)}, bf16[2,256,3072]{2,1,0:T(8,128)(2,1)}, u32[]{:S(2)}) copy-start(bf16[2,256,3072]{2,1,0:T(8,128)(2,1)} %all-gather.2.cloned.1.call-done) | copy-start | bytes 9437188
Sparse Core Ops, SparseCore 0:
  23.4 112.1 all-reduce.2
Sparse Core Ops, SparseCore 1:
  25.5 30.1 all-gather.1

commit v2 on v1

v2 whole, which is shorter than its diff:
```python
import functools

import jax
import jax.numpy as jnp
from jax import lax
from jax.experimental import pallas as pl
from jax.experimental.pallas import tpu as pltpu
from jax.sharding import PartitionSpec as P

F32, BF16, I32 = jnp.float32, jnp.bfloat16, jnp.int32
TN = (((0,), (0,)), ((), ()))
NN = (((1,), (0,)), ((), ()))
CAP = 64
LANES = 128


def dot(a, b, dims=NN, precision=None):
    return lax.dot_general(a, b, dims, preferred_element_type=F32, precision=precision)


def params(mib):
    return pltpu.CompilerParams(vmem_limit_bytes=mib << 20)


def gather_kernel(index_ref, a_ref, o_ref, hot_ref):
    @pl.when(pl.program_id(0) == 0)
    def _():
        here = lax.broadcasted_iota(I32, hot_ref.shape, 1)
        hot_ref[...] = jnp.where(here == index_ref[...], 1.0, 0.0).astype(BF16)

    rows = dot(hot_ref[...], a_ref[...]).astype(BF16)
    part = o_ref.shape[2]
    for b in range(o_ref.shape[0]):
        o_ref[b] = rows[:, b * part : (b + 1) * part]


def gather(slab, index, devices):
    height, cols = slab.shape
    slots, part = index.shape[0], cols // devices
    two = 2
    return pl.pallas_call(
        gather_kernel,
        out_shape=jax.ShapeDtypeStruct((devices, slots, part), BF16),
        grid=(devices // two,),
        in_specs=[
            pl.BlockSpec((slots, 1), lambda i: (0, 0)),
            pl.BlockSpec((height, two * part), lambda i: (0, i)),
        ],
        out_specs=pl.BlockSpec((two, slots, part), lambda i: (i, 0, 0)),
        scratch_shapes=[pltpu.VMEM((slots, height), BF16)],
        compiler_params=params(32),
        cost_estimate=pl.CostEstimate(
            flops=2 * slots * height * cols, bytes_accessed=2 * cols * (height + slots), transcendentals=0
        ),
    )(index[:, None], slab)


def invert_kernel(base, d_ref, o_ref):
    panels, width, _ = d_ref.shape
    count = width // base
    blocks = []
    for k in range(panels):
        for b in range(count):
            at = slice(b * base, (b + 1) * base)
            blocks.append(d_ref[k, at, at].astype(F32))
    lower = jnp.stack(blocks)
    row = lax.broadcasted_iota(I32, lower.shape, 1)
    col = lax.broadcasted_iota(I32, lower.shape, 2)
    x = jnp.where(row == col, 1.0, 0.0).astype(F32)
    for c in range(base - 1):
        x = x - lower[:, :, c : c + 1] * x[:, c : c + 1, :]
    o_ref[...] = jnp.zeros(o_ref.shape, F32)
    for k in range(panels):
        for b in range(count):
            at = slice(b * base, (b + 1) * base)
            o_ref[k, at, at] = x[k * count + b]
    size = base
    while size < width:
        for k in range(panels):
            for o in range(0, width, 2 * size):
                up, down = slice(o, o + size), slice(o + size, o + 2 * size)
                inner = dot(d_ref[k, down, up].astype(F32), o_ref[k, up, up], NN, lax.Precision.HIGHEST)
                o_ref[k, down, up] = -dot(o_ref[k, down, down], inner, NN, lax.Precision.HIGHEST)
        size *= 2


def invert(lower):
    return pl.pallas_call(
        functools.partial(invert_kernel, min(32, lower.shape[1])),
        out_shape=jax.ShapeDtypeStruct(lower.shape, F32),
        compiler_params=params(16),
        cost_estimate=pl.CostEstimate(flops=1 << 31, bytes_accessed=1 << 20, transcendentals=0),
    )(lower)


def apply_inverse(inverse, rows):
    total = None
    for _ in range(3):
        part = inverse.astype(BF16)
        inverse = inverse - part.astype(F32)
        term = dot(part, rows)
        total = term if total is None else total + term
    return total.astype(BF16)


def first_kernel(width, inv_ref, own_ref, key_ref, r_ref, y_ref, u_ref, c_ref):
    devices, slots, part = r_ref.shape
    zero = r_ref[0]
    total = jnp.where(own_ref[...] > 0, zero.astype(F32), 0.0)
    for s in range(1, devices):
        total = total + r_ref[s].astype(F32)
    rows = total.astype(BF16)
    c_ref[...] = rows[width:]
    upper = apply_inverse(inv_ref[0], rows[:width])
    u_ref[...] = upper
    want = lax.broadcasted_iota(I32, (devices * CAP, slots), 0)
    want = (want // CAP) * slots + want % CAP
    hot = jnp.where(want == key_ref[...], 1.0, 0.0).astype(BF16)
    fill = dot(hot, zero).astype(BF16)
    for d in range(devices):
        y_ref[d, :width, :] = upper
        y_ref[d, width:, :] = fill[d * CAP : (d + 1) * CAP]


def first(inverse, own, key, received, width):
    devices, slots, part = received.shape
    return pl.pallas_call(
        functools.partial(first_kernel, width),
        out_shape=(
            jax.ShapeDtypeStruct((devices, width + CAP, part), BF16),
            jax.ShapeDtypeStruct((width, part), BF16),
            jax.ShapeDtypeStruct((slots - width, part), BF16),
        ),
        compiler_params=params(32),
        cost_estimate=pl.CostEstimate(flops=1 << 29, bytes_accessed=4 << 20, transcendentals=0),
    )(inverse, own[:, None], key[None, :], received)


def second_kernel(inv_ref, sel_ref, u_ref, c_ref, y_ref):
    later = c_ref[...].astype(F32) - dot(sel_ref[...], u_ref[...], TN)
    upper = apply_inverse(inv_ref[1], later.astype(BF16))
    for d in range(y_ref.shape[0]):
        y_ref[d] = upper


def second(inverse, selected, upper, rows, devices):
    width, part = rows.shape
    return pl.pallas_call(
        second_kernel,
        out_shape=jax.ShapeDtypeStruct((devices, width, part), BF16),
        compiler_params=params(16),
        cost_estimate=pl.CostEstimate(flops=1 << 28, bytes_accessed=2 << 20, transcendentals=0),
    )(inverse, selected, upper, rows)


def update_kernel(
    width, begin, hole, slot, place, a_ref, l_ref, y0_ref, y1_ref, slab_ref, rest_ref, o_ref, u_ref, d_ref, sem
):
    step = pl.program_id(0)
    rows = a_ref.shape[0]
    devices, _, part = y1_ref.shape
    more = begin[pl.num_programs(0)] > CAP

    @pl.when(step == 0)
    def _():
        for e in range(devices):
            at = slice(e * part, (e + 1) * part)
            u_ref[:width, at] = y0_ref[e, :width, :]
            u_ref[width:, at] = y1_ref[e]
            d_ref[:CAP, at] = y0_ref[e, width:, :]

    @pl.when((step == 0) & (place[0] == 0))
    def _():
        copy = pltpu.make_async_copy(slab_ref.at[: 2 * width], d_ref, sem)
        copy.start()
        copy.wait()

    @pl.when((step == 0) & (place[0] != 0) & more)
    def _():
        copy = pltpu.make_async_copy(rest_ref.at[CAP:], d_ref.at[CAP:], sem)
        copy.start()
        copy.wait()

    group = 16

    def fill(j, carry):
        to, source = hole[j] - step * rows, slot[j]
        taken = d_ref[pl.ds(pl.multiple_of(source // group * group, group), group), :].astype(F32)
        lane = lax.broadcasted_iota(I32, taken.shape, 0)
        row = jnp.where(lane == source % group, taken, 0.0).sum(0, keepdims=True)
        target = pl.ds(pl.multiple_of(to // group * group, group), group)
        a_ref[target, :] = jnp.where(lane == to % group, row, a_ref[target, :].astype(F32)).astype(BF16)
        return carry

    lax.fori_loop(begin[step], begin[step + 1], fill, 0)
    o_ref[...] = (a_ref[...].astype(F32) - dot(l_ref[...], u_ref[...], TN)).astype(BF16)

    @pl.when((place[0] == 0) & (step < 2 * width // rows))
    def _():
        o_ref[...] = u_ref[pl.ds(pl.multiple_of(step * rows, rows), rows), :]


def update(slab, lower, y0, y1, rest, begin, hole, slot, place, rows):
    height, cols = slab.shape
    width = lower.shape[0] // 2
    return pl.pallas_call(
        functools.partial(update_kernel, width),
        out_shape=jax.ShapeDtypeStruct(slab.shape, BF16),
        grid_spec=pltpu.PrefetchScalarGridSpec(
            num_scalar_prefetch=4,
            grid=(height // rows,),
            in_specs=[
                pl.BlockSpec((rows, cols), lambda i, *_: (i, 0)),
                pl.BlockSpec((2 * width, rows), lambda i, *_: (0, i)),
                pl.BlockSpec(y0.shape, lambda i, *_: (0, 0, 0)),
                pl.BlockSpec(y1.shape, lambda i, *_: (0, 0, 0)),
                pl.BlockSpec(memory_space=pl.ANY),
                pl.BlockSpec(memory_space=pl.ANY),
            ],
            out_specs=pl.BlockSpec((rows, cols), lambda i, *_: (i, 0)),
            scratch_shapes=[
                pltpu.VMEM((2 * width, cols), BF16),
                pltpu.VMEM((2 * width, cols), BF16),
                pltpu.SemaphoreType.DMA,
            ],
        ),
        compiler_params=params(48),
        cost_estimate=pl.CostEstimate(
            flops=4 * height * cols * width, bytes_accessed=4 * height * cols, transcendentals=0
        ),
    )(begin, hole, slot, place, slab, lower, y0, y1, slab, rest)


def exchange(x):
    return lax.all_to_all(x, "row", 0, 0)


def per_device(trailing, panels, diag_lower, pivot_src, pivot_dst):
    height, cols = trailing.shape
    width = diag_lower.shape[2]
    slots = 2 * width
    block = min(256, width)
    devices = lax.axis_size("row")
    place = lax.axis_index("row")
    offset = place * height
    count = jnp.arange(width, dtype=I32)
    every = jnp.arange(slots, dtype=I32)
    here = jnp.arange(height, dtype=I32)
    src0, src1 = pivot_src[0], pivot_src[1]
    dst0, dst1 = pivot_dst[0], pivot_dst[1]

    def original(position):
        hit = dst0[None, :] == position[:, None]
        return jnp.where(hit.any(1), jnp.where(hit, count[None, :], 0).sum(1), position)

    source = jnp.concatenate([src0, original(src1)])
    owner = source // height
    hit0 = dst0[None, :] == source[:, None]
    hit1 = dst1[None, :] == source[:, None]
    content = jnp.where(
        hit1.any(1),
        jnp.where(hit1, original(width + count)[None, :], 0).sum(1),
        jnp.where(hit0, count[None, :], 0).sum(1),
    )
    local = owner == place
    wanted = jnp.where(local, source - offset, jnp.where(place == 0, content, -1))
    received = exchange(gather(trailing, wanted.astype(I32), devices))

    whole = lax.all_gather(panels, "col", axis=1, tiled=True)

    position = jnp.concatenate([src1, width + count]) - offset
    chosen = (here[:, None] == position[None, :]).astype(BF16)
    piece = dot(panels[0], chosen).astype(BF16)
    piece = exchange(jnp.broadcast_to(piece[None], (devices,) + piece.shape))
    piece = piece.astype(F32).sum(0).astype(BF16)
    small = lax.all_gather(
        jnp.concatenate([piece, diag_lower[0], diag_lower[1]], axis=1), "col", axis=0, tiled=True
    )
    selected, below = small[:, :width], small[:, width:slots]
    inverse = invert(jnp.stack([small[:, slots : slots + width], small[:, slots + width :]]))

    same = owner[:, None] == owner[None, :]
    rank = (same & (every[None, :] < every[:, None])).sum(1).astype(I32)
    key = jnp.where(owner > 0, owner * slots + rank, -1)
    rounds = (jnp.where(owner > 0, rank, 0).max() + CAP) // CAP
    rest = jnp.where(local & (source >= slots), source - offset, height)
    order = (rest[None, :] * slots + every[None, :] < (rest * slots + every)[:, None]).sum(1)
    sort = order[None, :] == every[:, None]
    hole = jnp.where(sort, rest[None, :], 0).sum(1).astype(I32)
    slot = jnp.where(sort, jnp.where(place == 0, content, rank)[None, :], 0).sum(1).astype(I32)
    edges = jnp.arange(height // block + 1, dtype=I32) * block
    begin = (rest[None, :] < edges[:, None]).sum(1).astype(I32)

    landing = (dst1 - offset)[:, None] == here[None, :]
    moved = dot(below, landing.astype(BF16)).astype(BF16)
    lower = jnp.concatenate([jnp.where(landing.any(0)[None, :], moved, whole[0]), whole[1]])

    y0, upper, rows = first(inverse, (owner == 0).astype(I32), key.astype(I32), received, width)
    y1 = second(inverse, selected, upper, rows, devices)

    def fetch(state):
        r, found = state
        want = jnp.arange(devices * CAP, dtype=I32)
        want = want // CAP * slots + want % CAP + r * CAP
        part = dot((want[:, None] == key[None, :]).astype(BF16), received[0]).astype(BF16)
        part = exchange(part.reshape(devices, CAP, -1)).transpose(1, 0, 2).reshape(CAP, cols)
        return r + 1, lax.dynamic_update_slice(found, part, (r * CAP, 0))

    found = lax.while_loop(
        lambda state: state[0] < rounds, fetch, (jnp.ones((), I32), jnp.zeros((slots, cols), BF16))
    )[1]

    return update(
        trailing, lower, exchange(y0), exchange(y1), found, begin, hole, slot, place[None].astype(I32), block
    )


def solution(mesh):
    placed = (P("row", "col"), P(None, "col", "row"), P(None, "col", None), P(), P())
    return jax.shard_map(
        per_device, mesh=mesh, in_specs=placed, out_specs=P("row", "col"), check_vma=False
    )
```

time: 172 us -> 151 us (0.88)
  other arithmetic: 44.7 us -> 5.69 us
  starting transfers between devices: 8.01 us -> 23.6 us
  Pallas kernels: 22.9 us -> 37.5 us
  matrix products: 14 us -> 4.59 us
  waiting for transfers between devices: 41.5 us -> 39.2 us
    another operation x7 -> x1, other arithmetic: 39.6 us -> 0.03 us  [per_device(): jnp.stack([small[:, slots:slots + width], small[:, slots + width:]])]
    psum x1 -> x0, waiting for transfers between devices: 26.9 us -> none  [per_device(): moved = lax.psum((picked, top), 'row')]
    all_to_all x1 -> x4, waiting for transfers between devices: 14.1 us -> 38.5 us  [exchange(): return lax.all_to_all(x, 'row', 0, 0)]
    all_to_all x1 -> x4, starting transfers between devices: 7.96 us -> 23.6 us  [exchange(): return lax.all_to_all(x, 'row', 0, 0)]
    pallas_call x1 -> x4, Pallas kernels: 3.94 us -> 17.8 us  [the longest x1 11.2 us: gather(): pl.pallas_call(gather_kernel, out_shape=jax.ShapeDtypeStruct((devices, sl...]
    dot_general x3 -> x2, matrix products: 12.7 us -> 4.59 us  [dot(): lax.dot_general(a, b, dims, preferred_element_type=F32, precision=precision)]
    another operation x8 -> x0, local copies, waits for them, and re-layouts: 4.19 us -> none
    unnamed x10 -> x26, local copies, waits for them, and re-layouts: 2.65 us -> 6.6 us
  transfers between devices with their start and end apart: 3 -> 5, of which waited for: 2 -> 3; matrix products, arithmetic and copies ran while one was open for 28% -> 4% of each run, Pallas kernels for 2% -> 12%
where the time goes in v2:
time: 151 us; the launch traced here: 150 us
  waiting for transfers between devices  39.2 us (26%)
  Pallas kernels  37.5 us (25%)
  starting transfers between devices  23.6 us (16%)
  between operations  14.4 us (10%)
  blocking collectives  13.6 us (9%)
  local copies, waits for them, and re-layouts  11.6 us (8%)
  other arithmetic  5.69 us (4%)
  matrix products  4.59 us (3%)
    all_to_all x4, waiting for transfers between devices, exchange(): return lax.all_to_all(x, 'row', 0, 0)  38.5 us
    all_to_all x4, starting transfers between devices, exchange(): return lax.all_to_all(x, 'row', 0, 0)  23.6 us
    pallas_call x1, Pallas kernels, update(): pl.pallas_call(functools.partial(update_kernel, width), out_shape=jax.Sha...  19.6 us
    all_gather x1, blocking collectives, per_device(): lax.all_gather(jnp.concatenate([piece, diag_lower[0], diag_lower[1]], axi...  13.6 us
    pallas_call x1, Pallas kernels, gather(): pl.pallas_call(gather_kernel, out_shape=jax.ShapeDtypeStruct((devices, sl...  11.2 us
    unnamed x26, local copies, waits for them, and re-layouts  6.6 us
    dot_general x2, matrix products, dot(): lax.dot_general(a, b, dims, preferred_element_type=F32, precision=precision)  4.59 us
    pallas_call x1, Pallas kernels, invert(): pl.pallas_call(functools.partial(invert_kernel, min(32, lower.shape[1])),...  3.05 us
  transfers between devices with their start and end apart: 5, of which 3 were waited for; matrix products, arithmetic and copies ran while one was open for 4% of the time, Pallas kernels for 12%

profile of v2, /device:TPU:0, one launch (start us, length us, event | category | flops | bytes accessed | tf_op | source)
XLA Modules:
  0.0 150.2 jit_solution(4807995684302410453)
XLA Ops:
  7.2 0.8 fusion.40
  8.5 0.8 slice_bitcast_fusion.6
  10.3 1.0 convert_reduce_fusion
  11.3 1.3 broadcast_select_fusion
  13.2 2.0 %fusion.25 = bf16[32,512]{1,0:T(8,128)(2,1)S(1)} fusion(s32[512]{0:T(512)S(1)} %add_subtract_fusion, bf16[2,32,3072]{2,1,0:T(8,128)(2,1)} %param.8), kind=kOutput, calls=%fused_computation.34 | convolution fusion | flops 102252544 | bytes 231424 | tf_op jit(solution)/shard_map/dot_general | solution.py:18
  15.4 0.8 broadcast_in_dim.121
  16.2 8.0 %all-to-all-start.1 = ((bf16[16,32,512]{2,1,0:T(8,128)(2,1)}), bf16[16,32,512]{2,1,0:T(8,128)(2,1)S(1)}, u32[]{:S(2)}, u32[]{:S(2)}) async-start(bf16[16,32,512]{2,1,0:T(8,128)(2,1)} %broadcast_in_dim.121), calls=%async_computation.1 | async-start | bytes 1048576 | tf_op jit(solution)/shard_map/all_to_all | solution.py:235
  24.2 4.6 %copy-done = bf16[3072,2048]{1,0:T(8,128)(2,1)S(1)} copy-done((bf16[3072,2048]{1,0:T(8,128)(2,1)S(1)}, bf16[3072,2048]{1,0:T(8,128)(2,1)}, u32[]{:S(2)}) %copy-start) | copy-done | bytes 12582936
  28.8 11.2 %shard_map.56 = bf16[16,512,128]{2,1,0:T(8,128)(2,1)} custom-call(s32[512,1]{1,0:T(8,128)S(1)} %get-tuple-element.101.index_ref, bf16[3072,2048]{1,0:T(8,128)(2,1)S(1)} %copy-done), custom_call_target="tpu_custom_call" | custom-call | flops 6442450944 | bytes 14680064 | tf_op jit(solution)/shard_map/pallas_call | solution.py:41
  40.0 7.2 %all-to-all-start.2 = ((bf16[16,512,128]{2,1,0:T(8,128)(2,1)}), bf16[16,512,128]{2,1,0:T(8,128)(2,1)S(1)}, u32[]{:S(2)}, u32[]{:S(2)}) async-start(bf16[16,512,128]{2,1,0:T(8,128)(2,1)} %shard_map.56), calls=%async_computation.2 | async-start | bytes 4194304 | tf_op jit(solution)/shard_map/all_to_all | solution.py:235
  48.8 13.6 %all_gather.6 = bf16[256,1024]{1,0:T(8,128)(2,1)S(1)} all-gather(bf16[32,1024]{1,0:T(8,128)(2,1)S(1)} %pad_maximum_fusion.2), channel_id=1, replica_groups=mesh['row'=16,'col'=8] {'col'}, dimensions={0}, use_global_device_ids=true | all-gather | bytes 589824 | tf_op jit(solution)/shard_map/all_gather | solution.py:276
  62.5 0.8 copy-done.3
  63.3 3.0 %shard_map.55.inv_ref = f32[2,256,256]{2,1,0:T(8,128)S(1)} custom-call(bf16[2,256,256]{2,1,0:T(8,128)(2,1)S(1)} %pad_maximum_fusion.1.d_ref), custom_call_target="tpu_custom_call" | custom-call | flops 2147483648 | bytes 1048576 | tf_op jit(solution)/shard_map/pallas_call | solution.py:88
  66.3 10.1 %all-to-all-done.2.r_ref = bf16[16,512,128]{2,1,0:T(8,128)(2,1)S(1)} async-done(((bf16[16,512,128]{2,1,0:T(8,128)(2,1)}), bf16[16,512,128]{2,1,0:T(8,128)(2,1)S(1)}, u32[]{:S(2)}, u32[]{:S(2)}) %all-to-all-start.2) | async-done | bytes 2097184 | tf_op jit(solution)/shard_map/all_to_all | solution.py:235
  76.5 2.0 %shard_map.57 = (bf16[16,320,128]{2,1,0:T(8,128)(2,1)}, bf16[256,128]{1,0:T(8,128)(2,1)S(1)}, bf16[256,128]{1,0:T(8,128)(2,1)S(1)}) custom-call(f32[2,256,256]{2,1,0:T(8,128)S(1)} %shard_map.55.inv_ref, s32[512,1]{1,0:T(8,128)S(1)} %compare_convert_fusion.own_ref, s32[1,512]{1,0:T(1,128)S(1)} %compare_select_fusion.4.key_ref, ...), custom_call_target="tpu_custom_call" | custom-call | flops 536870912 | bytes 4194304 | tf_op jit(solution)/shard_map/pallas_call | solution.py:127
  78.5 1.6 %shard_map.58 = bf16[16,256,128]{2,1,0:T(8,128)(2,1)} custom-call(f32[2,256,256]{2,1,0:T(8,128)S(1)} %shard_map.55.inv_ref, bf16[256,256]{1,0:T(8,128)(2,1)S(1)} %get-tuple-element.111.sel_ref, bf16[256,128]{1,0:T(8,128)(2,1)S(1)} %get-tuple-element.80.u_ref, bf16[256,128]{1,0:T(8,128)(2,1)S(1)} %get-tuple-element.81.c_ref), custom_call_target="tpu_custom_call" | custom-call | flops 268435456 | bytes 2097152 | tf_op jit(solution)/shard_map/pallas_call | solution.py:148
  80.0 1.6 %broadcast_in_dim.122 = bf16[512,2048]{1,0:T(8,128)(2,1)} broadcast(bf16[]{:T(256)} %constant.102.clone.1), dimensions={} | broadcast | bytes 2097154 | tf_op jit(solution)/shard_map/broadcast_in_dim | solution.py:310
  81.7 4.0 %all-to-all-start.4 = ((bf16[16,256,128]{2,1,0:T(8,128)(2,1)}), bf16[16,256,128]{2,1,0:T(8,128)(2,1)S(1)}, u32[]{:S(2)}, u32[]{:S(2)}) async-start(bf16[16,256,128]{2,1,0:T(8,128)(2,1)} %shard_map.58), calls=%async_computation.4 | async-start | bytes 2097152 | tf_op jit(solution)/shard_map/all_to_all | solution.py:235
  86.7 13.6 %all-to-all-done.4.y1_ref = bf16[16,256,128]{2,1,0:T(8,128)(2,1)S(1)} async-done(((bf16[16,256,128]{2,1,0:T(8,128)(2,1)}), bf16[16,256,128]{2,1,0:T(8,128)(2,1)S(1)}, u32[]{:S(2)}, u32[]{:S(2)}) %all-to-all-start.4) | async-done | bytes 1048608 | tf_op jit(solution)/shard_map/all_to_all | solution.py:235
  100.3 4.4 %all-to-all-start.3 = ((bf16[16,320,128]{2,1,0:T(8,128)(2,1)}), bf16[16,320,128]{2,1,0:T(8,128)(2,1)}, u32[]{:S(2)}, u32[]{:S(2)}) async-start(bf16[16,320,128]{2,1,0:T(8,128)(2,1)} %get-tuple-element.79), calls=%async_computation.3 | async-start | bytes 2621440 | tf_op jit(solution)/shard_map/all_to_all | solution.py:235
  104.8 2.6 %fusion.20 = bf16[256,3072]{1,0:T(8,128)(2,1)S(1)} fusion(bf16[2,256,3072]{2,1,0:T(8,128)(2,1)} %all-gather.2.cloned.1.call-done, s32[256]{0:T(256)S(1)} %broadcast_subtract_fusion.1, pred[3072]{0:T(1024)(128)(4,1)S(1)} %fusion.22, bf16[256,1024]{1,0:T(8,128)(2,1)} %copy-done.3), kind=kOutput, calls=%fused_computation.25 | convolution fusion | flops 405012480 | bytes 3280896 | tf_op jit(solution)/shard_map/dot_general | solution.py:18
  107.7 14.8 %all-to-all-done.3.y0_ref = bf16[16,320,128]{2,1,0:T(8,128)(2,1)} async-done(((bf16[16,320,128]{2,1,0:T(8,128)(2,1)}), bf16[16,320,128]{2,1,0:T(8,128)(2,1)}, u32[]{:S(2)}, u32[]{:S(2)}) %all-to-all-start.3) | async-done | bytes 1310752 | tf_op jit(solution)/shard_map/all_to_all | solution.py:235
  122.4 1.2 copy-done.2
  123.7 19.6 %shard_map.59 = bf16[3072,2048]{1,0:T(8,128)(2,1)} custom-call(s32[13]{0:T(128)S(1)} %convert_reduce_fusion.2.begin, s32[512]{0:T(512)S(1)} %get-tuple-element.84.hole, s32[512]{0:T(512)S(1)} %get-tuple-element.83.slot, s32[1]{0:T(128)} %bitcast.9.place, bf16[3072,2048]{1,0:T(8,128)(2,1)} %slab_ref.1, bf16[512,3072]{1,0:T(8,128)(2,1)S(1)} %pad_maximum_fusion.l_ref, ...), custom_call_target="tpu_custom_call" | custom-call | flops 6442450944 | bytes 25165824 | tf_op jit(solution)/shard_map/pallas_call | solution.py:206
  (62 shorter events, 5.2 us)
Async XLA Ops:
  9.3 3.9 %copy-start.6 = (s32[1,256]{1,0:T(1,128)}, s32[1,256]{1,0:T(1,128)S(1)}, u32[]{:S(2)}) copy-start(s32[1,256]{1,0:T(1,128)S(1)} %get-tuple-element.123) | copy-start | bytes 3076
  9.3 3.9 %copy-start.8 = (s32[1,256]{1,0:T(1,128)}, s32[1,256]{1,0:T(1,128)S(1)}, u32[]{:S(2)}) copy-start(s32[1,256]{1,0:T(1,128)S(1)} %get-tuple-element.124) | copy-start | bytes 3076
  16.2 23.8 %all-to-all-start.1 = ((bf16[16,32,512]{2,1,0:T(8,128)(2,1)}), bf16[16,32,512]{2,1,0:T(8,128)(2,1)S(1)}, u32[]{:S(2)}, u32[]{:S(2)}) async-start(bf16[16,32,512]{2,1,0:T(8,128)(2,1)} %broadcast_in_dim.121), calls=%async_computation.1 | async-start | bytes 1048576 | tf_op jit(solution)/shard_map/all_to_all | solution.py:235
  24.2 4.6 %copy-start = (bf16[3072,2048]{1,0:T(8,128)(2,1)S(1)}, bf16[3072,2048]{1,0:T(8,128)(2,1)}, u32[]{:S(2)}) copy-start(bf16[3072,2048]{1,0:T(8,128)(2,1)} %slab_ref.1) | copy-start | bytes 37748740
  40.0 8.0 %copy-start.5 = (bf16[2,32,256]{2,1,0:T(8,128)(2,1)S(1)}, bf16[2,32,256]{2,1,0:T(8,128)(2,1)}, u32[]{:S(2)}) copy-start(bf16[2,32,256]{2,1,0:T(8,128)(2,1)} %param.9) | copy-start | bytes 98308
  40.0 8.0 %copy-start.7 = (s32[1,256]{1,0:T(1,128)S(1)}, s32[1,256]{1,0:T(1,128)}, u32[]{:S(2)}) copy-start(s32[1,256]{1,0:T(1,128)} %copy-done.6) | copy-start | bytes 3076
  40.0 8.0 %copy-start.9 = (s32[1,256]{1,0:T(1,128)S(1)}, s32[1,256]{1,0:T(1,128)}, u32[]{:S(2)}) copy-start(s32[1,256]{1,0:T(1,128)} %copy-done.8) | copy-start | bytes 3076
  40.0 36.5 %all-to-all-start.2 = ((bf16[16,512,128]{2,1,0:T(8,128)(2,1)}), bf16[16,512,128]{2,1,0:T(8,128)(2,1)S(1)}, u32[]{:S(2)}, u32[]{:S(2)}) async-start(bf16[16,512,128]{2,1,0:T(8,128)(2,1)} %shard_map.56), calls=%async_computation.2 | async-start | bytes 4194304 | tf_op jit(solution)/shard_map/all_to_all | solution.py:235
  47.2 57.5 %all-gather.2.cloned.1.call-start = ((), (), s32[]{:S(2)}) async-start(), calls=%async_computation.5 | async-start | bytes 3538944 | tf_op jit(solution)/shard_map/all_gather | solution.py:269
  62.4 0.8 copy-start.3
  78.5 3.2 %copy-start.12 = (s32[512]{0:T(512)S(1)}, s32[512]{0:T(512)}, u32[]{:S(2)}) copy-start(s32[512]{0:T(512)} %get-tuple-element.169) | copy-start | bytes 6148
  81.7 4.7 %copy-start.10 = (s32[512]{0:T(512)S(1)}, s32[512]{0:T(512)}, u32[]{:S(2)}) copy-start(s32[512]{0:T(512)} %get-tuple-element.133) | copy-start | bytes 6148
  81.7 4.7 %copy-start.11 = (s32[512]{0:T(512)S(1)}, s32[512]{0:T(512)}, u32[]{:S(2)}) copy-start(s32[512]{0:T(512)} %get-tuple-element.117) | copy-start | bytes 6148
  81.7 18.6 %all-to-all-start.4 = ((bf16[16,256,128]{2,1,0:T(8,128)(2,1)}), bf16[16,256,128]{2,1,0:T(8,128)(2,1)S(1)}, u32[]{:S(2)}, u32[]{:S(2)}) async-start(bf16[16,256,128]{2,1,0:T(8,128)(2,1)} %shard_map.58), calls=%async_computation.4 | async-start | bytes 2097152 | tf_op jit(solution)/shard_map/all_to_all | solution.py:235
  100.3 7.0 %copy-start.1 = (bf16[16,256,128]{2,1,0:T(8,128)(2,1)}, bf16[16,256,128]{2,1,0:T(8,128)(2,1)S(1)}, u32[]{:S(2)}) copy-start(bf16[16,256,128]{2,1,0:T(8,128)(2,1)S(1)} %all-to-all-done.4.y1_ref) | copy-start | bytes 3145732
  100.3 22.1 %all-to-all-start.3 = ((bf16[16,320,128]{2,1,0:T(8,128)(2,1)}), bf16[16,320,128]{2,1,0:T(8,128)(2,1)}, u32[]{:S(2)}, u32[]{:S(2)}) async-start(bf16[16,320,128]{2,1,0:T(8,128)(2,1)} %get-tuple-element.79), calls=%async_computation.3 | async-start | bytes 2621440 | tf_op jit(solution)/shard_map/all_to_all | solution.py:235
  104.8 2.6 %copy-start.4 = (bf16[2,256,3072]{2,1,0:T(8,128)(2,1)S(1)}, bf16[2,256,3072]{2,1,0:T(8,128)(2,1)}, u32[]{:S(2)}) copy-start(bf16[2,256,3072]{2,1,0:T(8,128)(2,1)} %all-gather.2.cloned.1.call-done) | copy-start | bytes 9437188
  122.4 1.2 copy-start.2
Sparse Core Ops, SparseCore 0:
  49.8 29.4 all-gather.1

commit v3 on v2

v3 whole, which is shorter than its diff:
```python
import functools

import jax
import jax.numpy as jnp
from jax import lax
from jax.experimental import pallas as pl
from jax.experimental.pallas import tpu as pltpu
from jax.sharding import PartitionSpec as P

F32, BF16, I32 = jnp.float32, jnp.bfloat16, jnp.int32
TN = (((0,), (0,)), ((), ()))
NN = (((1,), (0,)), ((), ()))
CAP = 64
LANES = 128


def dot(a, b, dims=NN, precision=None):
    return lax.dot_general(a, b, dims, preferred_element_type=F32, precision=precision)


def params(mib):
    return pltpu.CompilerParams(vmem_limit_bytes=mib << 20)


def as_column(row):
    size = row.shape[1]
    eye = lax.broadcasted_iota(I32, (size, size), 0) == lax.broadcasted_iota(I32, (size, size), 1)
    return jnp.where(eye, row, 0.0).sum(1, keepdims=True)


def lookup(keys, table, values, other):
    hit = keys == table
    found = jnp.where(hit, values, 0.0).sum(1, keepdims=True)
    return jnp.where(jnp.where(hit, 1.0, 0.0).sum(1, keepdims=True) > 0, found, other)


def as_row(column):
    size = column.shape[0]
    eye = lax.broadcasted_iota(I32, (size, size), 0) == lax.broadcasted_iota(I32, (size, size), 1)
    return jnp.where(eye, column, 0.0).sum(0, keepdims=True)


def slot_rows(height, me, src_ref, dst_ref):
    width = src_ref.shape[1]
    dst0, dst1 = dst_ref[0:1, :].astype(F32), dst_ref[1:2, :].astype(F32)
    lane = lax.broadcasted_iota(I32, (1, width), 1).astype(F32)
    late = as_column(lane + width)
    late = as_row(lookup(late, dst0, lane, late))
    src1 = as_column(src_ref[1:2, :].astype(F32))
    source = jnp.concatenate([as_column(src_ref[0:1, :].astype(F32)), lookup(src1, dst0, lane, src1)])
    return source, lookup(source, dst1, late, lookup(source, dst0, lane, -1.0))


def owned_first(src_ref, height):
    return src_ref[1:2, :] < height


def table_kernel(height, devices, block, place, src_ref, dst_ref, own_ref, key_ref, table_ref):
    slots = 2 * src_ref.shape[1]
    me = place[0].astype(F32)
    source, content = slot_rows(height, me, src_ref, dst_ref)
    owner = jnp.zeros_like(source)
    for d in range(1, devices):
        owner = owner + jnp.where(source >= float(d * height), 1.0, 0.0)
    own_ref[...] = jnp.where(owner == 0, 1.0, 0.0)
    lane = lax.broadcasted_iota(I32, (slots, slots), 1).astype(F32)
    line = lax.broadcasted_iota(I32, (slots, slots), 0).astype(F32)
    rank = jnp.where((owner == as_row(owner)) & (lane < line), 1.0, 0.0).sum(1, keepdims=True)
    key = as_row(jnp.where(owner > 0, owner * slots + rank, -1.0))
    first = jnp.where(owned_first(src_ref, height), 1.0, 0.0)
    key_ref[...] = jnp.concatenate([key, jnp.concatenate([first, first], 1)] * 4)
    rest = jnp.where((owner == me) & (source >= slots), source - me * height, float(height))
    order = (as_row(rest) * slots + lane < rest * slots + line).astype(F32).sum(1, keepdims=True)
    sort = order == lane
    hole = jnp.where(sort, rest, 0.0).sum(0, keepdims=True)
    slot = jnp.where(sort, jnp.where(me == 0, content, rank), 0.0).sum(0, keepdims=True)
    begin = jnp.where(rest < lane * block, 1.0, 0.0).sum(0, keepdims=True)
    most = jnp.where(owner > 0, rank + 1.0, 0.0).max(0, keepdims=True)
    most = jnp.broadcast_to(most, (1, slots))
    table_ref[...] = jnp.concatenate([hole, slot, begin, most] * 2).astype(I32)


def tables(pivot_src, pivot_dst, place, height, devices, block):
    slots = 2 * pivot_src.shape[1]
    whole = lambda i, *_: (0, 0)
    return pl.pallas_call(
        functools.partial(table_kernel, height, devices, block),
        out_shape=(
            jax.ShapeDtypeStruct((slots, 1), F32),
            jax.ShapeDtypeStruct((8, slots), F32),
            jax.ShapeDtypeStruct((8, slots), I32),
        ),
        grid_spec=pltpu.PrefetchScalarGridSpec(
            num_scalar_prefetch=1,
            grid=(1,),
            in_specs=[pl.BlockSpec(pivot_src.shape, whole), pl.BlockSpec(pivot_dst.shape, whole)],
            out_specs=(
                pl.BlockSpec((slots, 1), whole),
                pl.BlockSpec((8, slots), whole),
                pl.BlockSpec((8, slots), whole),
            ),
        ),
        compiler_params=params(24),
    )(place, pivot_src, pivot_dst)


def gather_kernel(
    height, chunk, place, src_ref, dst_ref, p_ref, a_ref, o_ref, top_ref, low_ref, spread_ref, rounds, acc_ref, extra_ref
):
    slots = 2 * src_ref.shape[1]

    @pl.when(pl.program_id(0) == 0)
    def _():
        me = place[0].astype(F32)
        source, content = slot_rows(height, me, src_ref, dst_ref)
        here = source - me * height
        wanted = jnp.where((here >= 0) & (here < height), here, jnp.where(me == 0, content, -1.0))
        column = lax.broadcasted_iota(I32, (slots, slots), 1).astype(F32)
        top_ref[...] = jnp.where(column == wanted, 1.0, 0.0).astype(BF16)
        low = wanted >= slots
        before = column < lax.broadcasted_iota(I32, (slots, slots), 0).astype(F32)
        flag = jnp.where(low, 1.0, 0.0)
        rank = dot(before.astype(F32).astype(BF16), jnp.broadcast_to(flag, (slots, LANES)).astype(BF16))[:, :1]
        rank = jnp.where(low, rank, -1.0)
        needed = flag.sum().astype(I32)
        rounds[0] = (needed + chunk - 1) // chunk

        def build(r, carry):
            spot = lax.broadcasted_iota(I32, (slots, chunk), 1).astype(F32) + (r * chunk).astype(F32)
            spread = rank == spot
            spread_ref[r] = jnp.where(spread, 1.0, 0.0).astype(BF16)
            row = jnp.where(spread, wanted, 0.0).sum(0, keepdims=True)
            row = as_column(row)
            below = lax.broadcasted_iota(I32, low_ref.shape[1:], 1).astype(F32) + float(slots)
            low_ref[r] = jnp.where(below == row, 1.0, 0.0).astype(BF16)
            return carry

        lax.fori_loop(0, rounds[0], build, 0)

        width, part = src_ref.shape[1], o_ref.shape[2]
        src1 = as_column(src_ref[1:2, :].astype(F32))
        lane = lax.broadcasted_iota(I32, (1, width), 1).astype(F32)
        here = src1 - me * height
        moving = lookup(src1, dst_ref[1:2, :].astype(F32), lane + width, -1.0)
        chosen = jnp.where((here >= 0) & (here < height), here, jnp.where(me == 0, moving, -1.0))
        row = lax.broadcasted_iota(I32, (width, height), 1).astype(F32)
        hot = jnp.where(row == chosen, 1.0, 0.0).astype(BF16)
        taken = dot(p_ref[0], hot, (((1,), (1,)), ((), ()))).astype(BF16)
        piece = taken.shape[0]
        for h in range(extra_ref.shape[0] // piece):
            have = min(part, width - h * part)
            extra_ref[h * piece : (h + 1) * piece, :have] = taken[:, h * part : h * part + have]

    acc_ref[...] = dot(top_ref[...], a_ref[:slots, :])

    def add(r, carry):
        found = dot(low_ref[r], a_ref[slots:, :]).astype(BF16)
        acc_ref[...] += dot(spread_ref[r], found)
        return carry

    lax.fori_loop(0, rounds[0], add, 0)
    part = o_ref.shape[2]
    for b in range(o_ref.shape[0]):
        o_ref[b, : acc_ref.shape[0], :] = acc_ref[:, b * part : (b + 1) * part].astype(BF16)
        o_ref[b, acc_ref.shape[0] :, :] = extra_ref[...]


def gather(slab, panels, pivot_src, pivot_dst, place, devices):
    height, cols = slab.shape
    width = pivot_src.shape[1]
    slots, part = 2 * width, cols // devices
    chunk = min(LANES, slots)
    most = slots // chunk
    many = min(4, devices)
    piece = panels.shape[1]
    extra = piece * pl.cdiv(width, part)
    return pl.pallas_call(
        functools.partial(gather_kernel, height, chunk),
        out_shape=jax.ShapeDtypeStruct((devices, slots + extra, part), BF16),
        grid_spec=pltpu.PrefetchScalarGridSpec(
            num_scalar_prefetch=1,
            grid=(devices // many,),
            in_specs=[
                pl.BlockSpec(pivot_src.shape, lambda i, *_: (0, 0)),
                pl.BlockSpec(pivot_dst.shape, lambda i, *_: (0, 0)),
                pl.BlockSpec((1, piece, height), lambda i, *_: (0, 0, 0)),
                pl.BlockSpec((height, many * part), lambda i, *_: (0, i)),
            ],
            out_specs=pl.BlockSpec((many, slots + extra, part), lambda i, *_: (i, 0, 0)),
            scratch_shapes=[
                pltpu.VMEM((slots, slots), BF16),
                pltpu.VMEM((most, chunk, height - slots), BF16),
                pltpu.VMEM((most, slots, chunk), BF16),
                pltpu.SMEM((1,), I32),
                pltpu.VMEM((slots, many * part), F32),
                pltpu.VMEM((extra, part), BF16),
            ],
        ),
        compiler_params=params(56),
        cost_estimate=pl.CostEstimate(
            flops=slots * height * cols, bytes_accessed=2 * cols * (height + slots), transcendentals=0
        ),
    )(place, pivot_src, pivot_dst, panels, slab)


def invert_kernel(base, d_ref, o_ref):
    panels, width, _ = o_ref.shape
    count = width // base
    blocks = []
    for k in range(panels):
        for b in range(count):
            at = slice(b * base, (b + 1) * base)
            blocks.append(d_ref[at, k * width + b * base : k * width + (b + 1) * base].astype(F32))
    lower = jnp.stack(blocks)
    row = lax.broadcasted_iota(I32, lower.shape, 1)
    col = lax.broadcasted_iota(I32, lower.shape, 2)
    x = jnp.where(row == col, 1.0, 0.0).astype(F32)
    for c in range(base - 1):
        x = x - lower[:, :, c : c + 1] * x[:, c : c + 1, :]
    o_ref[...] = jnp.zeros(o_ref.shape, F32)
    for k in range(panels):
        for b in range(count):
            at = slice(b * base, (b + 1) * base)
            o_ref[k, at, at] = x[k * count + b]
    size = base
    while size < width:
        for k in range(panels):
            for o in range(0, width, 2 * size):
                up, down = slice(o, o + size), slice(o + size, o + 2 * size)
                inner = dot(d_ref[down, k * width + o : k * width + o + size].astype(F32), o_ref[k, up, up], NN, lax.Precision.HIGHEST)
                o_ref[k, down, up] = -dot(o_ref[k, down, down], inner, NN, lax.Precision.HIGHEST)
        size *= 2


def invert(lower):
    width = lower.shape[0]
    return pl.pallas_call(
        functools.partial(invert_kernel, min(32, width)),
        out_shape=jax.ShapeDtypeStruct((lower.shape[1] // width, width, width), F32),
        compiler_params=params(16),
        cost_estimate=pl.CostEstimate(flops=1 << 20, bytes_accessed=1 << 18, transcendentals=0),
    )(lower)


def apply_inverse(inverse, rows):
    total = None
    for _ in range(3):
        part = inverse.astype(BF16)
        inverse = inverse - part.astype(F32)
        term = dot(part, rows)
        total = term if total is None else total + term
    return total.astype(BF16)


def solve_kernel(width, piece, inv_ref, own_ref, key_ref, r_ref, y_ref, small_ref):
    devices, _, part = r_ref.shape
    slots = 2 * width
    zero = r_ref[0, :slots, :]
    total = jnp.where(own_ref[...] > 0, zero.astype(F32), 0.0)
    for s in range(1, devices):
        total = total + r_ref[s, :slots, :].astype(F32)
    rows = total.astype(BF16)
    upper = apply_inverse(inv_ref[0], rows[:width])
    later = apply_inverse(inv_ref[1], rows[width:])
    want = lax.broadcasted_iota(I32, (devices * CAP, slots), 0)
    want = (want // CAP) * slots + want % CAP
    hot = jnp.where(want.astype(F32) == key_ref[0:1, :], 1.0, 0.0).astype(BF16)
    fill = dot(hot, zero).astype(BF16)
    for d in range(devices):
        y_ref[d, :width, :] = upper
        y_ref[d, width:slots, :] = later
        y_ref[d, slots:, :] = fill[d * CAP : (d + 1) * CAP]
    for h in range(pl.cdiv(width, part)):
        have = min(part, width - h * part)
        at = slice(slots + h * piece, slots + (h + 1) * piece)
        moving = r_ref[0, at, :have]
        picked = jnp.where(key_ref[1:2, h * part : h * part + have] > 0, moving.astype(F32), 0.0)
        for s in range(1, devices):
            picked = picked + r_ref[s, at, :have].astype(F32)
        small_ref[:, h * part : h * part + have] = picked.astype(BF16)
        small_ref[:, width + h * part : width + h * part + have] = moving


def solve(inverse, own, key, received, width, piece):
    devices, _, part = received.shape
    return pl.pallas_call(
        functools.partial(solve_kernel, width, piece),
        out_shape=(
            jax.ShapeDtypeStruct((devices, 2 * width + CAP, part), BF16),
            jax.ShapeDtypeStruct((piece, 2 * width), BF16),
        ),
        compiler_params=params(32),
        cost_estimate=pl.CostEstimate(flops=1 << 29, bytes_accessed=4 << 20, transcendentals=0),
    )(inverse, own, key, received)


def arrange_kernel(width, where, inv_ref, sel_ref, below_ref, land_ref, even_ref, odd_ref, l_ref, w_ref, moving_ref):
    shifts, panels, piece, cols = even_ref.shape
    step = pl.program_id(0)
    for s in range(shifts):
        across = lax.rem(where[1] - s + shifts, shifts)
        for k in range(panels):
            for core, ref in enumerate((even_ref, odd_ref)):
                at = pl.multiple_of(k * width + (2 * across + core) * piece, piece)
                l_ref[pl.ds(at, piece), :] = ref[s, k]

    @pl.when((step == 0) & (where[0] == 0))
    def _():
        moving_ref[...] = l_ref[:width, width : 2 * width]

    @pl.when((step == 0) & (where[0] != 0))
    def _():
        moving_ref[...] = below_ref[...]

    here = lax.broadcasted_iota(I32, (width, cols), 1) + where[0] + step * cols
    landing = jnp.where(land_ref[...] == here, 1.0, 0.0)
    moved = dot(moving_ref[...], landing.astype(BF16))
    l_ref[:width, :] = jnp.where(
        landing.sum(0, keepdims=True) > 0, moved, l_ref[:width, :].astype(F32)
    ).astype(BF16)

    @pl.when(step == 0)
    def _():
        coupling = lax.dot_general(
            inv_ref[1], sel_ref[...].astype(F32), (((1,), (1,)), ((), ())),
            preferred_element_type=F32, precision=lax.Precision.HIGHEST,
        )
        w_ref[...] = coupling


def arrange(inverse, selected, below, landing, even, odd, where):
    shifts, panels, piece, height = even.shape
    width = below.shape[0]
    cols = min(512, height)
    pieces = pl.BlockSpec((shifts, panels, piece, cols), lambda i, *_: (0, 0, 0, i))
    return pl.pallas_call(
        functools.partial(arrange_kernel, width),
        out_shape=(
            jax.ShapeDtypeStruct((panels * width, height), BF16),
            jax.ShapeDtypeStruct((width, width), F32),
        ),
        grid_spec=pltpu.PrefetchScalarGridSpec(
            num_scalar_prefetch=1,
            grid=(height // cols,),
            in_specs=[
                pl.BlockSpec(inverse.shape, lambda i, *_: (0, 0, 0)),
                pl.BlockSpec(selected.shape, lambda i, *_: (0, 0)),
                pl.BlockSpec(below.shape, lambda i, *_: (0, 0)),
                pl.BlockSpec((width, 1), lambda i, *_: (0, 0)),
                pieces,
                pieces,
            ],
            out_specs=(
                pl.BlockSpec((panels * width, cols), lambda i, *_: (0, i)),
                pl.BlockSpec((width, width), lambda i, *_: (0, 0)),
            ),
            scratch_shapes=[pltpu.VMEM((width, width), BF16)],
        ),
        compiler_params=params(32),
        cost_estimate=pl.CostEstimate(flops=1 << 24, bytes_accessed=1 << 20, transcendentals=0),
    )(where, inverse, selected, below, landing[:, None], even, odd)


def update_kernel(
    width, table, place, a_ref, l_ref, y_ref, w_ref, slab_ref, rest_ref, o_ref, u_ref, d_ref, sem
):
    step = pl.program_id(0)
    rows = a_ref.shape[0]
    devices, _, part = y_ref.shape
    more = table[2, pl.num_programs(0)] > CAP

    @pl.when(step == 0)
    def _():
        for e in range(devices):
            at = slice(e * part, (e + 1) * part)
            u_ref[:, at] = y_ref[e, : 2 * width, :]
            d_ref[:CAP, at] = y_ref[e, 2 * width :, :]
        high = w_ref[...].astype(BF16)
        rest = (w_ref[...] - high.astype(F32)).astype(BF16)
        for c in range(0, u_ref.shape[1], 512):
            at = slice(c, c + 512)
            upper = u_ref[:width, at]
            later = u_ref[width:, at].astype(F32) - (dot(high, upper) + dot(rest, upper))
            u_ref[width:, at] = later.astype(BF16)

    @pl.when((step == 0) & (place[0] == 0))
    def _():
        copy = pltpu.make_async_copy(slab_ref.at[: 2 * width], d_ref, sem)
        copy.start()
        copy.wait()

    @pl.when((step == 0) & (place[0] != 0) & more)
    def _():
        for e in range(devices):
            copy = pltpu.make_async_copy(
                rest_ref.at[e, CAP : 2 * width], d_ref.at[CAP:, e * part : (e + 1) * part], sem
            )
            copy.start()
            copy.wait()

    group = 16

    def fill(j, carry):
        to, source = table[0, j] - step * rows, table[1, j]
        taken = d_ref[pl.ds(pl.multiple_of(source // group * group, group), group), :].astype(F32)
        lane = lax.broadcasted_iota(I32, taken.shape, 0)
        row = jnp.where(lane == source % group, taken, 0.0).sum(0, keepdims=True)
        target = pl.ds(pl.multiple_of(to // group * group, group), group)
        a_ref[target, :] = jnp.where(lane == to % group, row, a_ref[target, :].astype(F32)).astype(BF16)
        return carry

    lax.fori_loop(table[2, step], table[2, step + 1], fill, 0)
    for c in range(0, o_ref.shape[1], 512):
        at = slice(c, c + 512)
        o_ref[:, at] = (a_ref[:, at].astype(F32) - dot(l_ref[...], u_ref[:, at], TN)).astype(BF16)

    @pl.when((place[0] == 0) & (step < 2 * width // rows))
    def _():
        o_ref[...] = u_ref[pl.ds(pl.multiple_of(step * rows, rows), rows), :]


def update(slab, lower, upper, coupling, rest, table, place, rows):
    height, cols = slab.shape
    width = lower.shape[0] // 2
    return pl.pallas_call(
        functools.partial(update_kernel, width),
        out_shape=jax.ShapeDtypeStruct(slab.shape, BF16),
        grid_spec=pltpu.PrefetchScalarGridSpec(
            num_scalar_prefetch=2,
            grid=(height // rows,),
            in_specs=[
                pl.BlockSpec((rows, cols), lambda i, *_: (i, 0)),
                pl.BlockSpec((2 * width, rows), lambda i, *_: (0, i)),
                pl.BlockSpec(memory_space=pltpu.VMEM),
                pl.BlockSpec(memory_space=pltpu.VMEM),
                pl.BlockSpec(memory_space=pl.ANY),
                pl.BlockSpec(memory_space=pl.ANY),
            ],
            out_specs=pl.BlockSpec((rows, cols), lambda i, *_: (i, 0)),
            scratch_shapes=[
                pltpu.VMEM((2 * width, cols), BF16),
                pltpu.VMEM((2 * width, cols), BF16),
                pltpu.SemaphoreType.DMA,
            ],
        ),
        compiler_params=params(54),
        cost_estimate=pl.CostEstimate(
            flops=4 * height * cols * width, bytes_accessed=4 * height * cols, transcendentals=0
        ),
    )(table, place, slab, lower, upper, coupling, slab, rest)


def exchange(x):
    return lax.all_to_all(x, "row", 0, 0)


def per_device(trailing, panels, diag_lower, pivot_src, pivot_dst):
    height, cols = trailing.shape
    width = diag_lower.shape[2]
    slots = 2 * width
    devices = lax.axis_size("row")
    place = lax.axis_index("row").astype(I32)
    offset = place * height
    received = gather(trailing, panels, pivot_src, pivot_dst, place[None], devices)
    received, diag_lower = lax.optimization_barrier((received, diag_lower))
    received = exchange(received)
    diagonal = lax.all_gather(
        jnp.concatenate([diag_lower[0], diag_lower[1]], axis=1), "col", axis=0, tiled=True
    )
    diagonal, panels, pivot_src, pivot_dst = lax.optimization_barrier(
        (diagonal, panels, pivot_src, pivot_dst)
    )
    inverse = invert(diagonal)
    own, key, table = tables(pivot_src, pivot_dst, place[None], height, devices, slots)

    sent, small = solve(inverse, own, key, received, width, panels.shape[1])

    small = lax.all_gather(small, "col", axis=0, tiled=True)

    columns = lax.axis_size("col")
    chips = columns // 2
    across, core = lax.axis_index("col") // 2, lax.axis_index("col") % 2
    pieces = [panels]
    for s in range(1, chips):
        pieces.append(lax.ppermute(panels, "col", [(i, (i + 2 * s) % columns) for i in range(columns)]))
    pieces = lax.optimization_barrier((pieces, small))[0]
    mine = jnp.stack(pieces)
    other = lax.ppermute(mine, "col", [(i, i ^ 1) for i in range(columns)])
    even, odd = jnp.where(core == 0, mine, other), jnp.where(core == 0, other, mine)

    selected, below = small[:, :width], small[:, width:slots]
    lower, coupling = arrange(
        inverse, selected, below, jnp.where(place == 0, pivot_dst[1], pivot_src[1]), even, odd, jnp.stack([offset, across]).astype(I32)
    )

    fills = received[0, :slots]
    rounds = (table[3, 0] + CAP - 1) // CAP

    def fetch(state):
        r, found = state
        want = jnp.arange(devices * CAP, dtype=I32)
        want = want // CAP * slots + want % CAP + r * CAP
        part = dot((want[:, None] == key[:1].astype(I32)).astype(BF16), fills).astype(BF16)
        part = exchange(part.reshape(devices, CAP, -1))
        return r + 1, lax.dynamic_update_slice(found, part, (0, r * CAP, 0))

    found = lax.while_loop(lambda state: state[0] < rounds, fetch, (jnp.ones((), I32), received))[1]

    return update(trailing, lower, exchange(sent), coupling, found, table, place[None], slots)


def solution(mesh):
    placed = (P("row", "col"), P(None, "col", "row"), P(None, "col", None), P(), P())
    return jax.shard_map(
        per_device, mesh=mesh, in_specs=placed, out_specs=P("row", "col"), check_vma=False
    )
```

time: 151 us -> 130 us (0.86)
  between operations: 14.4 us -> 0.98 us
  blocking collectives: 13.6 us -> 26.7 us
  local copies, waits for them, and re-layouts: 11.6 us -> 3.03 us
  starting transfers between devices: 23.6 us -> 16.4 us
  matrix products: 4.59 us -> 0 us
  Pallas kernels: 37.5 us -> 40.9 us
  waiting for transfers between devices: 39.2 us -> 36 us
    all_gather x1 -> x2, blocking collectives: 13.6 us -> 26.7 us  [the longest x1 13.4 us: per_device(): lax.all_gather(jnp.concatenate([diag_lower[0], diag_lower[1]], axis=1), '...]
    all_to_all x4 -> x2, starting transfers between devices: 23.6 us -> 12.7 us  [exchange(): return lax.all_to_all(x, 'row', 0, 0)]
    pallas_call x4 -> x5, Pallas kernels: 17.8 us -> 22.5 us  [the longest x1 11.5 us: gather(): pl.pallas_call(functools.partial(gather_kernel, height, chunk), out_shape...]
    dot_general x2 -> x0, matrix products: 4.59 us -> none  [dot(): lax.dot_general(a, b, dims, preferred_element_type=F32, precision=precision)]
    unnamed x26 -> x12, local copies, waits for them, and re-layouts: 6.6 us -> 2.35 us
    ppermute x0 -> x4, starting transfers between devices: none -> 3.71 us  [the longest x3 3.37 us: per_device(): lax.ppermute(panels, 'col', [(i, (i + 2 * s) % columns) for i in range(co...]
    another operation x1 -> x2, other arithmetic: 0.03 us -> 2.77 us  [the longest x1 2.69 us: per_device(): mine = jnp.stack(pieces)]
    all_to_all x4 -> x2, waiting for transfers between devices: 38.5 us -> 36 us  [exchange(): return lax.all_to_all(x, 'row', 0, 0)]
  transfers between devices with their start and end apart: 5 -> 6, of which waited for: 3 -> 2; matrix products, arithmetic and copies ran while one was open for 4% -> 2% of each run, Pallas kernels for 12% -> 9%
where the time goes in v3:
time: 130 us; the launch traced here: 129 us
  Pallas kernels  40.9 us (31%)
  waiting for transfers between devices  36 us (28%)
  blocking collectives  26.7 us (21%)
  starting transfers between devices  16.4 us (13%)
  other arithmetic  4.9 us (4%)
  local copies, waits for them, and re-layouts  3.03 us (2%)
    all_to_all x2, waiting for transfers between devices, exchange(): return lax.all_to_all(x, 'row', 0, 0)  36 us
    pallas_call x1, Pallas kernels, update(): pl.pallas_call(functools.partial(update_kernel, width), out_shape=jax.Sha...  18.4 us
    all_gather x1, blocking collectives, per_device(): lax.all_gather(jnp.concatenate([diag_lower[0], diag_lower[1]], axis=1), '...  13.4 us
    all_gather x1, blocking collectives, per_device(): small = lax.all_gather(small, 'col', axis=0, tiled=True)  13.3 us
    all_to_all x2, starting transfers between devices, exchange(): return lax.all_to_all(x, 'row', 0, 0)  12.7 us
    pallas_call x1, Pallas kernels, gather(): pl.pallas_call(functools.partial(gather_kernel, height, chunk), out_shape...  11.5 us
    pallas_call x1, Pallas kernels, arrange(): pl.pallas_call(functools.partial(arrange_kernel, width), out_shape=(jax.S...  3.68 us
    ppermute x3, starting transfers between devices, per_device(): lax.ppermute(panels, 'col', [(i, (i + 2 * s) % columns) for i in range(co...  3.37 us
  transfers between devices with their start and end apart: 6, of which 2 were waited for; matrix products, arithmetic and copies ran while one was open for 2% of the time, Pallas kernels for 9%

profile of v3, /device:TPU:0, one launch (start us, length us, event | category | flops | bytes accessed | tf_op | source)
XLA Modules:
  0.0 129.0 jit_solution(8410270205681895124)
XLA Ops:
  0.0 11.5 %shard_map.55 = bf16[16,576,128]{2,1,0:T(8,128)(2,1)} custom-call(s32[1]{0:T(128)} %bitcast.2.place, s32[2,256]{1,0:T(2,128)} %src_ref.2, s32[2,256]{1,0:T(2,128)} %dst_ref.2, bf16[2,32,3072]{2,1,0:T(8,128)(2,1)} %p_ref.1, bf16[3072,2048]{1,0:T(8,128)(2,1)} %slab_ref.1), custom_call_target="tpu_custom_call" | custom-call | flops 3221225472 | bytes 14680064 | tf_op jit(solution)/shard_map/pallas_call | solution.py:177
  11.5 8.1 %all-to-all-start.1 = ((bf16[16,576,128]{2,1,0:T(8,128)(2,1)}), bf16[16,576,128]{2,1,0:T(8,128)(2,1)S(1)}, u32[]{:S(2)}, u32[]{:S(2)}) async-start(bf16[16,576,128]{2,1,0:T(8,128)(2,1)} %shard_map.55), calls=%async_computation.1 | async-start | bytes 4718592 | tf_op jit(solution)/shard_map/all_to_all | solution.py:454
  19.6 13.4 %all_gather.6.d_ref = bf16[256,512]{1,0:T(8,128)(2,1)S(1)} all-gather(bf16[32,512]{1,0:T(8,128)(2,1)S(1)} %pad_maximum_fusion.1), channel_id=1, replica_groups=mesh['row'=16,'col'=8] {'col'}, dimensions={0}, use_global_device_ids=true | all-gather | bytes 294912 | tf_op jit(solution)/shard_map/all_gather | solution.py:467
  33.0 2.5 %collective-permute-start.2 = (bf16[2,32,3072]{2,1,0:T(8,128)(2,1)}, bf16[2,32,3072]{2,1,0:T(8,128)(2,1)}, u32[]{:S(2)}, u32[]{:S(2)}) collective-permute-start(bf16[2,32,3072]{2,1,0:T(8,128)(2,1)} %p_ref.1), channel_id=1, source_target_pairs={{0,6},{1,7},{2,0},{3,1},{4,2},{5,3},{6,4},{7,5},{8,14},{9,15},{10,... | collective-permute-start | bytes 1179656 | tf_op jit(solution)/shard_map/ppermute | solution.py:485
  35.5 0.9 collective-permute-start.1
  36.3 0.0 collective-permute-start
  36.3 1.9 %shard_map.56 = (f32[512,1]{1,0:T(8,128)S(1)}, f32[8,512]{1,0:T(8,128)S(1)}, s32[8,512]{1,0:T(8,128)S(1)}) custom-call(s32[1]{0:T(128)} %bitcast.2.place, s32[2,256]{1,0:T(2,128)S(1)} %copy-done.3, s32[2,256]{1,0:T(2,128)S(1)} %copy-done.4), custom_call_target="tpu_custom_call" | custom-call | tf_op jit(solution)/shard_map/pallas_call | solution.py:86
  38.2 0.5 slice.35
  39.4 3.0 %shard_map.57.inv_ref = f32[2,256,256]{2,1,0:T(8,128)S(1)} custom-call(bf16[256,512]{1,0:T(8,128)(2,1)S(1)} %all_gather.6.d_ref), custom_call_target="tpu_custom_call" | custom-call | flops 1048576 | bytes 262144 | tf_op jit(solution)/shard_map/pallas_call | solution.py:237
  42.4 10.8 %all-to-all-done.1.r_ref = bf16[16,576,128]{2,1,0:T(8,128)(2,1)S(1)} async-done(((bf16[16,576,128]{2,1,0:T(8,128)(2,1)}), bf16[16,576,128]{2,1,0:T(8,128)(2,1)S(1)}, u32[]{:S(2)}, u32[]{:S(2)}) %all-to-all-start.1) | async-done | bytes 2359328 | tf_op jit(solution)/shard_map/all_to_all | solution.py:454
  53.2 2.4 %shard_map.58 = (bf16[16,576,128]{2,1,0:T(8,128)(2,1)}, bf16[32,512]{1,0:T(8,128)(2,1)S(1)}) custom-call(f32[2,256,256]{2,1,0:T(8,128)S(1)} %shard_map.57.inv_ref, f32[512,1]{1,0:T(8,128)S(1)} %get-tuple-element.100.own_ref, f32[8,512]{1,0:T(8,128)S(1)} %get-tuple-element.101.key_ref, bf16[16,576,128]{2,1,0:T(8,128)(2,1)S(1)} %all-to-all-done.1.r_ref), custom_call_target="tpu_custom_call" | custom-call | flops 536870912 | bytes 4194304 | tf_op jit(solution)/shard_map/pallas_call | solution.py:286
  55.7 13.3 %all_gather.7 = bf16[256,512]{1,0:T(8,128)(2,1)S(1)} all-gather(bf16[32,512]{1,0:T(8,128)(2,1)S(1)} %get-tuple-element.103), channel_id=1, replica_groups=mesh['row'=16,'col'=8] {'col'}, dimensions={0}, use_global_device_ids=true | all-gather | bytes 294912 | tf_op jit(solution)/shard_map/all_gather | solution.py:478
  69.0 0.0 collective-permute-done.1
  69.0 2.7 %pad_maximum_fusion = bf16[4,2,32,3072]{3,2,1,0:T(8,128)(2,1)} fusion(bf16[1,2,32,3072]{3,2,1,0:T(8,128)(2,1)} %bitcast.11, bf16[1,2,32,3072]{3,2,1,0:T(8,128)(2,1)} %bitcast.10, bf16[1,2,32,3072]{3,2,1,0:T(8,128)(2,1)} %bitcast.9, bf16[1,2,32,3072]{3,2,1,0:T(8,128)(2,1)} %bitcast.8), kind=kLoop, calls=%fused_computation.20 | loop fusion | flops 2359296 | bytes 3145728 | tf_op jit(solution)/shard_map/stack | solution.py:487
  71.7 0.3 collective-permute-start.3
  72.1 4.6 %all-to-all-start.2 = ((bf16[16,576,128]{2,1,0:T(8,128)(2,1)}), bf16[16,576,128]{2,1,0:T(8,128)(2,1)}, u32[]{:S(2)}, u32[]{:S(2)}) async-start(bf16[16,576,128]{2,1,0:T(8,128)(2,1)} %get-tuple-element.110), calls=%async_computation.2 | async-start | bytes 4718592 | tf_op jit(solution)/shard_map/all_to_all | solution.py:454
  76.8 0.1 copy.6.land_ref
  76.9 0.1 pad_add_fusion.where
  77.0 2.1 %broadcast_select_fusion = (bf16[4,2,32,3072]{3,2,1,0:T(8,128)(2,1)S(1)}, bf16[4,2,32,3072]{3,2,1,0:T(8,128)(2,1)S(1)}) fusion(bf16[4,2,32,3072]{3,2,1,0:T(8,128)(2,1)} %collective-permute-done.3, pred[]{:T(512)S(6)} %eq.42, bf16[1,2,32,3072]{3,2,1,0:T(8,128)(2,1)} %bitcast.11, bf16[1,2,32,3072]{3,2,1,0:T(8,128)(2,1)} %bitcast.10, ...), kind=kLoop, calls=%fused_computation.21 | loop fusion | flops 3932160 | bytes 6291457 | tf_op jit(solution)/shard_map/jit(_where)/select_n | solution.py:489
  79.2 3.7 %shard_map.59 = (bf16[512,3072]{1,0:T(8,128)(2,1)S(1)}, f32[256,256]{1,0:T(8,128)S(1)}) custom-call(s32[2]{0:T(128)S(1)} %pad_add_fusion.where, f32[2,256,256]{2,1,0:T(8,128)S(1)} %shard_map.57.inv_ref, bf16[256,256]{1,0:T(8,128)(2,1)S(1)} %get-tuple-element.126.sel_ref, bf16[256,256]{1,0:T(8,128)(2,1)S(1)} %get-tuple-element.125.below_ref, ...), custom_call_target="tpu_custom_call" | custom-call | flops 16777216 | bytes 1048576 | tf_op jit(solution)/shard_map/pallas_call | solution.py:336
  82.9 1.6 %copy-done = bf16[512,3072]{1,0:T(8,128)(2,1)} copy-done((bf16[512,3072]{1,0:T(8,128)(2,1)}, bf16[512,3072]{1,0:T(8,128)(2,1)S(1)}, u32[]{:S(2)}) %copy-start) | copy-done | bytes 3145752
  84.5 0.7 copy-done.1
  85.2 25.2 %all-to-all-done.2.y_ref = bf16[16,576,128]{2,1,0:T(8,128)(2,1)} async-done(((bf16[16,576,128]{2,1,0:T(8,128)(2,1)}), bf16[16,576,128]{2,1,0:T(8,128)(2,1)}, u32[]{:S(2)}, u32[]{:S(2)}) %all-to-all-start.2) | async-done | bytes 2359328 | tf_op jit(solution)/shard_map/all_to_all | solution.py:454
  110.4 18.4 %shard_map.60 = bf16[3072,2048]{1,0:T(8,128)(2,1)} custom-call(s32[8,512]{1,0:T(8,128)} %copy-done.2, s32[1]{0:T(128)} %bitcast.2.place, bf16[3072,2048]{1,0:T(8,128)(2,1)} %slab_ref.1, bf16[512,3072]{1,0:T(8,128)(2,1)} %copy-done, bf16[16,576,128]{2,1,0:T(8,128)(2,1)} %all-to-all-done.2.y_ref, f32[256,256]{1,0:T(8,128)} %copy-done.1, ...), custom_call_target="tpu_custom_call" | custom-call | flops 6442450944 | bytes 25165824 | tf_op jit(solution)/shard_map/pallas_call | solution.py:425
  (20 shorter events, 0.1 us)
Async XLA Ops:
  11.5 8.1 %copy-start.5 = (bf16[2,32,256]{2,1,0:T(8,128)(2,1)S(1)}, bf16[2,32,256]{2,1,0:T(8,128)(2,1)}, u32[]{:S(2)}) copy-start(bf16[2,32,256]{2,1,0:T(8,128)(2,1)} %param.9) | copy-start | bytes 98308
  11.5 24.9 %copy-start.3 = (s32[2,256]{1,0:T(2,128)S(1)}, s32[2,256]{1,0:T(2,128)}, u32[]{:S(2)}) copy-start(s32[2,256]{1,0:T(2,128)} %src_ref.2) | copy-start | bytes 6148
  11.5 24.9 %copy-start.4 = (s32[2,256]{1,0:T(2,128)S(1)}, s32[2,256]{1,0:T(2,128)}, u32[]{:S(2)}) copy-start(s32[2,256]{1,0:T(2,128)} %dst_ref.2) | copy-start | bytes 6148
  11.5 41.8 %all-to-all-start.1 = ((bf16[16,576,128]{2,1,0:T(8,128)(2,1)}), bf16[16,576,128]{2,1,0:T(8,128)(2,1)S(1)}, u32[]{:S(2)}, u32[]{:S(2)}) async-start(bf16[16,576,128]{2,1,0:T(8,128)(2,1)} %shard_map.55), calls=%async_computation.1 | async-start | bytes 4718592 | tf_op jit(solution)/shard_map/all_to_all | solution.py:454
  33.0 36.1 %collective-permute-start.2 = (bf16[2,32,3072]{2,1,0:T(8,128)(2,1)}, bf16[2,32,3072]{2,1,0:T(8,128)(2,1)}, u32[]{:S(2)}, u32[]{:S(2)}) collective-permute-start(bf16[2,32,3072]{2,1,0:T(8,128)(2,1)} %p_ref.1), channel_id=1, source_target_pairs={{0,6},{1,7},{2,0},{3,1},{4,2},{5,3},{6,4},{7,5},{8,14},{9,15},{10,... | collective-permute-start | bytes 1179656 | tf_op jit(solution)/shard_map/ppermute | solution.py:485
  35.5 33.6 %collective-permute-start.1 = (bf16[2,32,3072]{2,1,0:T(8,128)(2,1)}, bf16[2,32,3072]{2,1,0:T(8,128)(2,1)}, u32[]{:S(2)}, u32[]{:S(2)}) collective-permute-start(bf16[2,32,3072]{2,1,0:T(8,128)(2,1)} %p_ref.1), channel_id=1, source_target_pairs={{0,4},{1,5},{2,6},{3,7},{4,0},{5,1},{6,2},{7,3},{8,12},{9,13},{10,... | collective-permute-start | bytes 1179656 | tf_op jit(solution)/shard_map/ppermute | solution.py:485
  36.3 32.7 %collective-permute-start = (bf16[2,32,3072]{2,1,0:T(8,128)(2,1)}, bf16[2,32,3072]{2,1,0:T(8,128)(2,1)}, u32[]{:S(2)}, u32[]{:S(2)}) collective-permute-start(bf16[2,32,3072]{2,1,0:T(8,128)(2,1)} %p_ref.1), channel_id=1, source_target_pairs={{0,2},{1,3},{2,4},{3,5},{4,6},{5,7},{6,0},{7,1},{8,10},{9,11},{10,... | collective-permute-start | bytes 1179656 | tf_op jit(solution)/shard_map/ppermute | solution.py:485
  38.2 17.5 %copy-start.2 = (s32[8,512]{1,0:T(8,128)}, s32[8,512]{1,0:T(8,128)S(1)}, u32[]{:S(2)}) copy-start(s32[8,512]{1,0:T(8,128)S(1)} %get-tuple-element.98.table) | copy-start | bytes 49156
  71.7 5.3 %collective-permute-start.3 = (bf16[4,2,32,3072]{3,2,1,0:T(8,128)(2,1)}, bf16[4,2,32,3072]{3,2,1,0:T(8,128)(2,1)}, u32[]{:S(2)}, u32[]{:S(2)}) collective-permute-start(bf16[4,2,32,3072]{3,2,1,0:T(8,128)(2,1)} %pad_maximum_fusion), channel_id=1, source_target_pairs={{0,1},{1,0},{2,3},{3,2},{4,5},{5,4},{6,7},{7,6},{8,9},{9,8},{10,11... | collective-permute-start | bytes 4718600 | tf_op jit(solution)/shard_map/ppermute | solution.py:488
  72.1 38.3 %all-to-all-start.2 = ((bf16[16,576,128]{2,1,0:T(8,128)(2,1)}), bf16[16,576,128]{2,1,0:T(8,128)(2,1)}, u32[]{:S(2)}, u32[]{:S(2)}) async-start(bf16[16,576,128]{2,1,0:T(8,128)(2,1)} %get-tuple-element.110), calls=%async_computation.2 | async-start | bytes 4718592 | tf_op jit(solution)/shard_map/all_to_all | solution.py:454
  82.8 1.6 %copy-start = (bf16[512,3072]{1,0:T(8,128)(2,1)}, bf16[512,3072]{1,0:T(8,128)(2,1)S(1)}, u32[]{:S(2)}) copy-start(bf16[512,3072]{1,0:T(8,128)(2,1)S(1)} %get-tuple-element.109.l_ref) | copy-start | bytes 9437188
  84.5 0.7 copy-start.1

commit v4 on v3

--- a/solution.py
+++ b/solution.py
@@ -105,64 +105,68 @@
 
 
 def gather_kernel(
-    height, chunk, place, src_ref, dst_ref, p_ref, a_ref, o_ref, top_ref, low_ref, spread_ref, rounds, acc_ref, extra_ref
+    height, chunk, place, src_ref, dst_ref, p_ref, slab_ref, o_ref, a_ref, top_ref, low_ref, spread_ref, acc_ref, extra_ref, sems
 ):
-    slots = 2 * src_ref.shape[1]
-
-    @pl.when(pl.program_id(0) == 0)
-    def _():
-        me = place[0].astype(F32)
-        source, content = slot_rows(height, me, src_ref, dst_ref)
-        here = source - me * height
-        wanted = jnp.where((here >= 0) & (here < height), here, jnp.where(me == 0, content, -1.0))
-        column = lax.broadcasted_iota(I32, (slots, slots), 1).astype(F32)
-        top_ref[...] = jnp.where(column == wanted, 1.0, 0.0).astype(BF16)
-        low = wanted >= slots
-        before = column < lax.broadcasted_iota(I32, (slots, slots), 0).astype(F32)
-        flag = jnp.where(low, 1.0, 0.0)
-        rank = dot(before.astype(F32).astype(BF16), jnp.broadcast_to(flag, (slots, LANES)).astype(BF16))[:, :1]
-        rank = jnp.where(low, rank, -1.0)
-        needed = flag.sum().astype(I32)
-        rounds[0] = (needed + chunk - 1) // chunk
-
-        def build(r, carry):
-            spot = lax.broadcasted_iota(I32, (slots, chunk), 1).astype(F32) + (r * chunk).astype(F32)
-            spread = rank == spot
-            spread_ref[r] = jnp.where(spread, 1.0, 0.0).astype(BF16)
-            row = jnp.where(spread, wanted, 0.0).sum(0, keepdims=True)
-            row = as_column(row)
-            below = lax.broadcasted_iota(I32, low_ref.shape[1:], 1).astype(F32) + float(slots)
-            low_ref[r] = jnp.where(below == row, 1.0, 0.0).astype(BF16)
+    width = src_ref.shape[1]
+    slots = 2 * width
+    tiles, _, cols = a_ref.shape
+    part = o_ref.shape[2]
+    copies = [
+        pltpu.make_async_copy(slab_ref.at[:, t * cols : (t + 1) * cols], a_ref.at[t], sems.at[t]) for t in range(tiles)
+    ]
+    for copy in copies:
+        copy.start()
+
+    me = place[0].astype(F32)
+    source, content = slot_rows(height, me, src_ref, dst_ref)
+    here = source - me * height
+    wanted = jnp.where((here >= 0) & (here < height), here, jnp.where(me == 0, content, -1.0))
+    column = lax.broadcasted_iota(I32, (slots, slots), 1).astype(F32)
+    top_ref[...] = jnp.where(column == wanted, 1.0, 0.0).astype(BF16)
+    low = wanted >= slots
+    before = jnp.where(column < lax.broadcasted_iota(I32, (slots, slots), 0).astype(F32), 1.0, 0.0)
+    flag = jnp.where(low, 1.0, 0.0)
+    rank = dot(before.astype(BF16), jnp.broadcast_to(flag, (slots, LANES)).astype(BF16))[:, :1]
+    rank = jnp.where(low, rank, -1.0)
+    rounds = (flag.sum().astype(I32) + chunk - 1) // chunk
+
+    def build(r, carry):
+        spot = lax.broadcasted_iota(I32, (slots, chunk), 1).astype(F32) + (r * chunk).astype(F32)
+        spread = rank == spot
+        spread_ref[r] = jnp.where(spread, 1.0, 0.0).astype(BF16)
+        row = as_column(jnp.where(spread, wanted, 0.0).sum(0, keepdims=True))
+        below = lax.broadcasted_iota(I32, low_ref.shape[1:], 1).astype(F32) + float(slots)
+        low_ref[r] = jnp.where(below == row, 1.0, 0.0).astype(BF16)
+        return carry
+
+    lax.fori_loop(0, rounds, build, 0)
+
+    src1 = as_column(src_ref[1:2, :].astype(F32))
+    lane = lax.broadcasted_iota(I32, (1, width), 1).astype(F32)
+    here = src1 - me * height
+    moving = lookup(src1, dst_ref[1:2, :].astype(F32), lane + width, -1.0)
+    chosen = jnp.where((here >= 0) & (here < height), here, jnp.where(me == 0, moving, -1.0))
+    row = lax.broadcasted_iota(I32, (width, height), 1).astype(F32)
+    hot = jnp.where(row == chosen, 1.0, 0.0).astype(BF16)
+    taken = dot(p_ref[0], hot, (((1,), (1,)), ((), ()))).astype(BF16)
+    piece = taken.shape[0]
+    for h in range(extra_ref.shape[0] // piece):
+        have = min(part, width - h * part)
+        extra_ref[h * piece : (h + 1) * piece, :have] = taken[:, h * part : h * part + have]
+
+    for t in range(tiles):
+        copies[t].wait()
+        acc_ref[...] = dot(top_ref[...], a_ref[t, :slots, :])
+
+        def add(r, carry, t=t):
+            found = dot(low_ref[r], a_ref[t, slots:, :]).astype(BF16)
+            acc_ref[...] += dot(spread_ref[r], found)
             return carry
 
-        lax.fori_loop(0, rounds[0], build, 0)
-
-        width, part = src_ref.shape[1], o_ref.shape[2]
-        src1 = as_column(src_ref[1:2, :].astype(F32))
-        lane = lax.broadcasted_iota(I32, (1, width), 1).astype(F32)
-        here = src1 - me * height
-        moving = lookup(src1, dst_ref[1:2, :].astype(F32), lane + width, -1.0)
-        chosen = jnp.where((here >= 0) & (here < height), here, jnp.where(me == 0, moving, -1.0))
-        row = lax.broadcasted_iota(I32, (width, height), 1).astype(F32)
-        hot = jnp.where(row == chosen, 1.0, 0.0).astype(BF16)
-        taken = dot(p_ref[0], hot, (((1,), (1,)), ((), ()))).astype(BF16)
-        piece = taken.shape[0]
-        for h in range(extra_ref.shape[0] // piece):
-            have = min(part, width - h * part)
-            extra_ref[h * piece : (h + 1) * piece, :have] = taken[:, h * part : h * part + have]
-
-    acc_ref[...] = dot(top_ref[...], a_ref[:slots, :])
-
-    def add(r, carry):
-        found = dot(low_ref[r], a_ref[slots:, :]).astype(BF16)
-        acc_ref[...] += dot(spread_ref[r], found)
-        return carry
-
-    lax.fori_loop(0, rounds[0], add, 0)
-    part = o_ref.shape[2]
-    for b in range(o_ref.shape[0]):
-        o_ref[b, : acc_ref.shape[0], :] = acc_ref[:, b * part : (b + 1) * part].astype(BF16)
-        o_ref[b, acc_ref.shape[0] :, :] = extra_ref[...]
+        lax.fori_loop(0, rounds, add, 0)
+        for b in range(cols // part):
+            o_ref[t * (cols // part) + b, :slots, :] = acc_ref[:, b * part : (b + 1) * part].astype(BF16)
+            o_ref[t * (cols // part) + b, slots:, :] = extra_ref[...]
 
 
 def gather(slab, panels, pivot_src, pivot_dst, place, devices):
@@ -171,7 +175,7 @@
     slots, part = 2 * width, cols // devices
     chunk = min(LANES, slots)
     most = slots // chunk
-    many = min(4, devices)
+    tiles = 4
     piece = panels.shape[1]
     extra = piece * pl.cdiv(width, part)
     return pl.pallas_call(
@@ -179,24 +183,25 @@
         out_shape=jax.ShapeDtypeStruct((devices, slots + extra, part), BF16),
         grid_spec=pltpu.PrefetchScalarGridSpec(
             num_scalar_prefetch=1,
-            grid=(devices // many,),
+            grid=(1,),
             in_specs=[
                 pl.BlockSpec(pivot_src.shape, lambda i, *_: (0, 0)),
                 pl.BlockSpec(pivot_dst.shape, lambda i, *_: (0, 0)),
                 pl.BlockSpec((1, piece, height), lambda i, *_: (0, 0, 0)),
-                pl.BlockSpec((height, many * part), lambda i, *_: (0, i)),
+                pl.BlockSpec(memory_space=pl.ANY),
             ],
-            out_specs=pl.BlockSpec((many, slots + extra, part), lambda i, *_: (i, 0, 0)),
+            out_specs=pl.BlockSpec((devices, slots + extra, part), lambda i, *_: (0, 0, 0)),
             scratch_shapes=[
+                pltpu.VMEM((tiles, height, cols // tiles), BF16),
                 pltpu.VMEM((slots, slots), BF16),
                 pltpu.VMEM((most, chunk, height - slots), BF16),
                 pltpu.VMEM((most, slots, chunk), BF16),
-                pltpu.SMEM((1,), I32),
-                pltpu.VMEM((slots, many * part), F32),
+                pltpu.VMEM((slots, cols // tiles), F32),
                 pltpu.VMEM((extra, part), BF16),
+                pltpu.SemaphoreType.DMA((tiles,)),
             ],
         ),
-        compiler_params=params(56),
+        compiler_params=params(58),
         cost_estimate=pl.CostEstimate(
             flops=slots * height * cols, bytes_accessed=2 * cols * (height + slots), transcendentals=0
         ),
@@ -294,15 +299,17 @@
     )(inverse, own, key, received)
 
 
-def arrange_kernel(width, where, inv_ref, sel_ref, below_ref, land_ref, even_ref, odd_ref, l_ref, w_ref, moving_ref):
-    shifts, panels, piece, cols = even_ref.shape
+def arrange_kernel(width, where, inv_ref, sel_ref, below_ref, land_ref, *refs):
+    *piece_refs, l_ref, w_ref, moving_ref = refs
+    chips = len(piece_refs) // 2
+    panels, piece, cols = piece_refs[0].shape
     step = pl.program_id(0)
-    for s in range(shifts):
-        across = lax.rem(where[1] - s + shifts, shifts)
+    for i, ref in enumerate(piece_refs):
+        across = lax.rem(where[1] - i % chips + chips, chips)
+        column = 2 * across + lax.rem(where[2] + i // chips, 2)
         for k in range(panels):
-            for core, ref in enumerate((even_ref, odd_ref)):
-                at = pl.multiple_of(k * width + (2 * across + core) * piece, piece)
-                l_ref[pl.ds(at, piece), :] = ref[s, k]
+            at = pl.multiple_of(k * width + column * piece, piece)
+            l_ref[pl.ds(at, piece), :] = ref[k]
 
     @pl.when((step == 0) & (where[0] == 0))
     def _():
@@ -328,11 +335,11 @@
         w_ref[...] = coupling
 
 
-def arrange(inverse, selected, below, landing, even, odd, where):
-    shifts, panels, piece, height = even.shape
+def arrange(inverse, selected, below, landing, parts, where):
+    panels, piece, height = parts[0].shape
     width = below.shape[0]
     cols = min(512, height)
-    pieces = pl.BlockSpec((shifts, panels, piece, cols), lambda i, *_: (0, 0, 0, i))
+    pieces = pl.BlockSpec((panels, piece, cols), lambda i, *_: (0, 0, i))
     return pl.pallas_call(
         functools.partial(arrange_kernel, width),
         out_shape=(
@@ -347,9 +354,8 @@
                 pl.BlockSpec(selected.shape, lambda i, *_: (0, 0)),
                 pl.BlockSpec(below.shape, lambda i, *_: (0, 0)),
                 pl.BlockSpec((width, 1), lambda i, *_: (0, 0)),
-                pieces,
-                pieces,
-            ],
+            ]
+            + [pieces] * len(parts),
             out_specs=(
                 pl.BlockSpec((panels * width, cols), lambda i, *_: (0, i)),
                 pl.BlockSpec((width, width), lambda i, *_: (0, 0)),
@@ -358,7 +364,7 @@
         ),
         compiler_params=params(32),
         cost_estimate=pl.CostEstimate(flops=1 << 24, bytes_accessed=1 << 20, transcendentals=0),
-    )(where, inverse, selected, below, landing[:, None], even, odd)
+    )(where, inverse, selected, below, landing[:, None], *parts)
 
 
 def update_kernel(
@@ -462,35 +468,37 @@
     place = lax.axis_index("row").astype(I32)
     offset = place * height
     received = gather(trailing, panels, pivot_src, pivot_dst, place[None], devices)
-    received, diag_lower = lax.optimization_barrier((received, diag_lower))
+    received, diag_lower, panels = lax.optimization_barrier((received, diag_lower, panels))
     received = exchange(received)
+
+    columns = lax.axis_size("col")
+    chips = columns // 2
+    across, core = lax.axis_index("col") // 2, lax.axis_index("col") % 2
+    parts = [panels]
+    for s in range(1, chips):
+        parts.append(lax.ppermute(panels, "col", [(d, (d + 2 * s) % columns) for d in range(columns)]))
     diagonal = lax.all_gather(
         jnp.concatenate([diag_lower[0], diag_lower[1]], axis=1), "col", axis=0, tiled=True
     )
-    diagonal, panels, pivot_src, pivot_dst = lax.optimization_barrier(
-        (diagonal, panels, pivot_src, pivot_dst)
-    )
+    diagonal, pivot_src, pivot_dst = lax.optimization_barrier((diagonal, pivot_src, pivot_dst))
     inverse = invert(diagonal)
     own, key, table = tables(pivot_src, pivot_dst, place[None], height, devices, slots)
 
+    received, parts = lax.optimization_barrier((received, parts))
     sent, small = solve(inverse, own, key, received, width, panels.shape[1])
 
     small = lax.all_gather(small, "col", axis=0, tiled=True)
 
-    columns = lax.axis_size("col")
-    chips = columns // 2
-    across, core = lax.axis_index("col") // 2, lax.axis_index("col") % 2
-    pieces = [panels]
-    for s in range(1, chips):
-        pieces.append(lax.ppermute(panels, "col", [(i, (i + 2 * s) % columns) for i in range(columns)]))
-    pieces = lax.optimization_barrier((pieces, small))[0]
-    mine = jnp.stack(pieces)
-    other = lax.ppermute(mine, "col", [(i, i ^ 1) for i in range(columns)])
-    even, odd = jnp.where(core == 0, mine, other), jnp.where(core == 0, other, mine)
+    parts = parts + [lax.ppermute(part, "col", [(d, d ^ 1) for d in range(columns)]) for part in parts]
 
     selected, below = small[:, :width], small[:, width:slots]
     lower, coupling = arrange(
-        inverse, selected, below, jnp.where(place == 0, pivot_dst[1], pivot_src[1]), even, odd, jnp.stack([offset, across]).astype(I32)
+        inverse,
+        selected,
+        below,
+        jnp.where(place == 0, pivot_dst[1], pivot_src[1]),
+        parts,
+        jnp.stack([offset, across, core]).astype(I32),
     )
 
     fills = received[0, :slots]

time: 130 us -> 121 us (0.931)
  waiting for transfers between devices: 36 us -> 11.4 us
  blocking collectives: 26.7 us -> 39.1 us
  other arithmetic: 4.9 us -> 0.09 us
  starting transfers between devices: 16.4 us -> 20.9 us
  Pallas kernels: 40.9 us -> 43.6 us
    all_to_all x2, waiting for transfers between devices: 36 us -> 11.4 us  [exchange(): return lax.all_to_all(x, 'row', 0, 0)]
    all_gather x1, blocking collectives: 13.4 us -> 26.3 us  [per_device(): lax.all_gather(jnp.concatenate([diag_lower[0], diag_lower[1]], axis=1), '...]
    another operation x2 -> x1, other arithmetic: 2.77 us -> 0.08 us  [per_device(): jnp.stack([offset, across, core]).astype(I32)]
    all_to_all x2, starting transfers between devices: 12.7 us -> 15.1 us  [exchange(): return lax.all_to_all(x, 'row', 0, 0)]
    select_n x1 -> x0, other arithmetic: 2.11 us -> none  [per_device(): jnp.where(core == 0, other, mine)]
    ppermute x4 -> x7, starting transfers between devices: 3.71 us -> 5.77 us  [the longest x3 4.68 us: per_device(): lax.ppermute(panels, 'col', [(d, (d + 2 * s) % columns) for d in range(co...]
    pallas_call x1, Pallas kernels: 3.68 us -> 5.54 us  [arrange(): pl.pallas_call(functools.partial(arrange_kernel, width), out_shape=(jax.S...]
    pallas_call x1, Pallas kernels: 2.44 us -> 4.15 us  [solve(): pl.pallas_call(functools.partial(solve_kernel, width, piece), out_shape=(...]
  transfers between devices with their start and end apart: 6 -> 9, of which waited for: 2 -> 1; matrix products, arithmetic and copies ran while one was open for 2% -> 1% of each run, Pallas kernels for 9% -> 9%
where the time goes in v4:
time: 121 us; the launch traced here: 120 us
  Pallas kernels  43.6 us (36%)
  blocking collectives  39.1 us (32%)
  starting transfers between devices  20.9 us (17%)
  waiting for transfers between devices  11.4 us (9%)
  local copies, waits for them, and re-layouts  4.03 us (3%)
    all_gather x1, blocking collectives, per_device(): lax.all_gather(jnp.concatenate([diag_lower[0], diag_lower[1]], axis=1), '...  26.3 us
    pallas_call x1, Pallas kernels, update(): pl.pallas_call(functools.partial(update_kernel, width), out_shape=jax.Sha...  18.5 us
    all_to_all x2, starting transfers between devices, exchange(): return lax.all_to_all(x, 'row', 0, 0)  15.1 us
    all_gather x1, blocking collectives, per_device(): small = lax.all_gather(small, 'col', axis=0, tiled=True)  12.8 us
    all_to_all x2, waiting for transfers between devices, exchange(): return lax.all_to_all(x, 'row', 0, 0)  11.4 us
    pallas_call x1, Pallas kernels, gather(): pl.pallas_call(functools.partial(gather_kernel, height, chunk), out_shape...  10.5 us
    pallas_call x1, Pallas kernels, arrange(): pl.pallas_call(functools.partial(arrange_kernel, width), out_shape=(jax.S...  5.54 us
    ppermute x3, starting transfers between devices, per_device(): lax.ppermute(panels, 'col', [(d, (d + 2 * s) % columns) for d in range(co...  4.68 us
  transfers between devices with their start and end apart: 9, of which 1 were waited for; matrix products, arithmetic and copies ran while one was open for 1% of the time, Pallas kernels for 9%

profile of v4, /device:TPU:0, one launch (start us, length us, event | category | flops | bytes accessed | tf_op | source)
XLA Modules:
  0.0 120.2 jit_solution(11103259797466398834)
XLA Ops:
  0.0 10.5 %shard_map.55 = bf16[16,576,128]{2,1,0:T(8,128)(2,1)} custom-call(s32[1]{0:T(128)} %bitcast.2.place, s32[2,256]{1,0:T(2,128)} %src_ref.2, s32[2,256]{1,0:T(2,128)} %dst_ref.2, bf16[2,32,3072]{2,1,0:T(8,128)(2,1)} %refs_0_, bf16[3072,2048]{1,0:T(8,128)(2,1)} %slab_ref.3), custom_call_target="tpu_custom_call" | custom-call | flops 3221225472 | bytes 14680064 | tf_op jit(solution)/shard_map/pallas_call | solution.py:181
  10.6 8.2 %all-to-all-start.1 = ((bf16[16,576,128]{2,1,0:T(8,128)(2,1)}), bf16[16,576,128]{2,1,0:T(8,128)(2,1)}, u32[]{:S(2)}, u32[]{:S(2)}) async-start(bf16[16,576,128]{2,1,0:T(8,128)(2,1)} %shard_map.55), calls=%async_computation.1 | async-start | bytes 4718592 | tf_op jit(solution)/shard_map/all_to_all | solution.py:460
  18.8 3.1 %collective-permute-start.2 = (bf16[2,32,3072]{2,1,0:T(8,128)(2,1)S(1)}, bf16[2,32,3072]{2,1,0:T(8,128)(2,1)S(1)}, u32[]{:S(2)}, u32[]{:S(2)}) collective-permute-start(bf16[2,32,3072]{2,1,0:T(8,128)(2,1)S(1)} %copy-done.1), channel_id=1, source_target_pairs={{0,6},{1,7},{2,0},{3,1},{4,2},{5,3},{6,4},{7,5},{8,14},{9,15},{10,... | collective-permute-start | bytes 1179656 | tf_op jit(solution)/shard_map/ppermute | solution.py:479
  21.8 0.6 collective-permute-start.1
  22.5 1.0 collective-permute-start
  23.4 26.3 %all_gather.6.d_ref = bf16[256,512]{1,0:T(8,128)(2,1)S(1)} all-gather(bf16[32,512]{1,0:T(8,128)(2,1)S(1)} %pad_maximum_fusion), channel_id=1, replica_groups=mesh['row'=16,'col'=8] {'col'}, dimensions={0}, use_global_device_ids=true | all-gather | bytes 294912 | tf_op jit(solution)/shard_map/all_gather | solution.py:480
  49.7 1.9 %shard_map.56 = (f32[512,1]{1,0:T(8,128)S(1)}, f32[8,512]{1,0:T(8,128)S(1)}, s32[8,512]{1,0:T(8,128)S(1)}) custom-call(s32[1]{0:T(128)} %bitcast.2.place, s32[2,256]{1,0:T(2,128)S(1)} %copy-done.4, s32[2,256]{1,0:T(2,128)S(1)} %copy-done.5), custom_call_target="tpu_custom_call" | custom-call | tf_op jit(solution)/shard_map/pallas_call | solution.py:86
  51.6 0.6 slice.35
  52.8 3.0 %shard_map.57.inv_ref = f32[2,256,256]{2,1,0:T(8,128)S(1)} custom-call(bf16[256,512]{1,0:T(8,128)(2,1)S(1)} %all_gather.6.d_ref), custom_call_target="tpu_custom_call" | custom-call | flops 1048576 | bytes 262144 | tf_op jit(solution)/shard_map/pallas_call | solution.py:242
  55.9 0.9 slice_bitcast_fusion
  56.9 4.1 %shard_map.58 = (bf16[16,576,128]{2,1,0:T(8,128)(2,1)}, bf16[32,512]{1,0:T(8,128)(2,1)S(1)}) custom-call(f32[2,256,256]{2,1,0:T(8,128)S(1)} %shard_map.57.inv_ref, f32[512,1]{1,0:T(8,128)S(1)} %get-tuple-element.101.own_ref, f32[8,512]{1,0:T(8,128)S(1)} %get-tuple-element.102.key_ref, bf16[16,576,128]{2,1,0:T(8,128)(2,1)} %all-to-all-done.1.r_ref), custom_call_target="tpu_custom_call" | custom-call | flops 536870912 | bytes 4194304 | tf_op jit(solution)/shard_map/pallas_call | solution.py:291
  61.0 6.9 %all-to-all-start.2 = ((bf16[16,576,128]{2,1,0:T(8,128)(2,1)}), bf16[16,576,128]{2,1,0:T(8,128)(2,1)}, u32[]{:S(2)}, u32[]{:S(2)}) async-start(bf16[16,576,128]{2,1,0:T(8,128)(2,1)} %get-tuple-element.112), calls=%async_computation.2 | async-start | bytes 4718592 | tf_op jit(solution)/shard_map/all_to_all | solution.py:460
  68.0 0.1 collective-permute-start.3
  68.1 0.4 collective-permute-start.4
  68.6 0.1 collective-permute-start.5
  68.7 0.4 collective-permute-start.6
  69.1 0.1 pad_add_fusion.where
  69.2 0.1 copy.6.land_ref
  69.3 12.8 %all_gather.7 = bf16[256,512]{1,0:T(8,128)(2,1)S(1)} all-gather(bf16[32,512]{1,0:T(8,128)(2,1)S(1)} %get-tuple-element.106), channel_id=1, replica_groups=mesh['row'=16,'col'=8] {'col'}, dimensions={0}, use_global_device_ids=true | all-gather | bytes 294912 | tf_op jit(solution)/shard_map/all_gather | solution.py:490
  82.2 5.5 %shard_map.59 = (bf16[512,3072]{1,0:T(8,128)(2,1)S(1)}, f32[256,256]{1,0:T(8,128)S(1)}) custom-call(s32[3]{0:T(128)S(1)} %pad_add_fusion.where, f32[2,256,256]{2,1,0:T(8,128)S(1)} %shard_map.57.inv_ref, bf16[256,256]{1,0:T(8,128)(2,1)S(1)} %get-tuple-element.126.sel_ref, bf16[256,256]{1,0:T(8,128)(2,1)S(1)} %get-tuple-element.125.below_ref, ...), custom_call_target="tpu_custom_call" | custom-call | flops 16777216 | bytes 1048576 | tf_op jit(solution)/shard_map/pallas_call | solution.py:343
  87.8 1.6 %copy-done = bf16[512,3072]{1,0:T(8,128)(2,1)} copy-done((bf16[512,3072]{1,0:T(8,128)(2,1)}, bf16[512,3072]{1,0:T(8,128)(2,1)S(1)}, u32[]{:S(2)}) %copy-start) | copy-done | bytes 3145752
  89.4 0.7 copy-done.2
  90.1 11.4 %all-to-all-done.2.y_ref = bf16[16,576,128]{2,1,0:T(8,128)(2,1)} async-done(((bf16[16,576,128]{2,1,0:T(8,128)(2,1)}), bf16[16,576,128]{2,1,0:T(8,128)(2,1)}, u32[]{:S(2)}, u32[]{:S(2)}) %all-to-all-start.2) | async-done | bytes 2359328 | tf_op jit(solution)/shard_map/all_to_all | solution.py:460
  101.5 18.5 %shard_map.60 = bf16[3072,2048]{1,0:T(8,128)(2,1)} custom-call(s32[8,512]{1,0:T(8,128)} %copy-done.3, s32[1]{0:T(128)} %bitcast.2.place, bf16[3072,2048]{1,0:T(8,128)(2,1)} %slab_ref.3, bf16[512,3072]{1,0:T(8,128)(2,1)} %copy-done, bf16[16,576,128]{2,1,0:T(8,128)(2,1)} %all-to-all-done.2.y_ref, f32[256,256]{1,0:T(8,128)} %copy-done.2, ...), custom_call_target="tpu_custom_call" | custom-call | flops 6442450944 | bytes 25165824 | tf_op jit(solution)/shard_map/pallas_call | solution.py:431
  (26 shorter events, 0.1 us)
Async XLA Ops:
  10.5 8.2 %copy-start.1 = (bf16[2,32,3072]{2,1,0:T(8,128)(2,1)S(1)}, bf16[2,32,3072]{2,1,0:T(8,128)(2,1)}, u32[]{:S(2)}) copy-start(bf16[2,32,3072]{2,1,0:T(8,128)(2,1)} %refs_0_) | copy-start | bytes 1179652
  10.5 12.9 %copy-start.6 = (bf16[2,32,256]{2,1,0:T(8,128)(2,1)S(1)}, bf16[2,32,256]{2,1,0:T(8,128)(2,1)}, u32[]{:S(2)}) copy-start(bf16[2,32,256]{2,1,0:T(8,128)(2,1)} %param.9) | copy-start | bytes 98308
  10.5 39.2 %copy-start.4 = (s32[2,256]{1,0:T(2,128)S(1)}, s32[2,256]{1,0:T(2,128)}, u32[]{:S(2)}) copy-start(s32[2,256]{1,0:T(2,128)} %src_ref.2) | copy-start | bytes 6148
  10.5 39.2 %copy-start.5 = (s32[2,256]{1,0:T(2,128)S(1)}, s32[2,256]{1,0:T(2,128)}, u32[]{:S(2)}) copy-start(s32[2,256]{1,0:T(2,128)} %dst_ref.2) | copy-start | bytes 6148
  10.6 45.4 %all-to-all-start.1 = ((bf16[16,576,128]{2,1,0:T(8,128)(2,1)}), bf16[16,576,128]{2,1,0:T(8,128)(2,1)}, u32[]{:S(2)}, u32[]{:S(2)}) async-start(bf16[16,576,128]{2,1,0:T(8,128)(2,1)} %shard_map.55), calls=%async_computation.1 | async-start | bytes 4718592 | tf_op jit(solution)/shard_map/all_to_all | solution.py:460
  18.8 37.2 %collective-permute-start.2 = (bf16[2,32,3072]{2,1,0:T(8,128)(2,1)S(1)}, bf16[2,32,3072]{2,1,0:T(8,128)(2,1)S(1)}, u32[]{:S(2)}, u32[]{:S(2)}) collective-permute-start(bf16[2,32,3072]{2,1,0:T(8,128)(2,1)S(1)} %copy-done.1), channel_id=1, source_target_pairs={{0,6},{1,7},{2,0},{3,1},{4,2},{5,3},{6,4},{7,5},{8,14},{9,15},{10,... | collective-permute-start | bytes 1179656 | tf_op jit(solution)/shard_map/ppermute | solution.py:479
  21.8 34.1 %collective-permute-start.1 = (bf16[2,32,3072]{2,1,0:T(8,128)(2,1)S(1)}, bf16[2,32,3072]{2,1,0:T(8,128)(2,1)S(1)}, u32[]{:S(2)}, u32[]{:S(2)}) collective-permute-start(bf16[2,32,3072]{2,1,0:T(8,128)(2,1)S(1)} %copy-done.1), channel_id=1, source_target_pairs={{0,4},{1,5},{2,6},{3,7},{4,0},{5,1},{6,2},{7,3},{8,12},{9,13},{10,... | collective-permute-start | bytes 1179656 | tf_op jit(solution)/shard_map/ppermute | solution.py:479
  22.5 33.5 %collective-permute-start = (bf16[2,32,3072]{2,1,0:T(8,128)(2,1)S(1)}, bf16[2,32,3072]{2,1,0:T(8,128)(2,1)S(1)}, u32[]{:S(2)}, u32[]{:S(2)}) collective-permute-start(bf16[2,32,3072]{2,1,0:T(8,128)(2,1)S(1)} %copy-done.1), channel_id=1, source_target_pairs={{0,2},{1,3},{2,4},{3,5},{4,6},{5,7},{6,0},{7,1},{8,10},{9,11},{10,... | collective-permute-start | bytes 1179656 | tf_op jit(solution)/shard_map/ppermute | solution.py:479
  51.6 9.4 %copy-start.3 = (s32[8,512]{1,0:T(8,128)}, s32[8,512]{1,0:T(8,128)S(1)}, u32[]{:S(2)}) copy-start(s32[8,512]{1,0:T(8,128)S(1)} %get-tuple-element.99.table) | copy-start | bytes 49156
  61.0 40.5 %all-to-all-start.2 = ((bf16[16,576,128]{2,1,0:T(8,128)(2,1)}), bf16[16,576,128]{2,1,0:T(8,128)(2,1)}, u32[]{:S(2)}, u32[]{:S(2)}) async-start(bf16[16,576,128]{2,1,0:T(8,128)(2,1)} %get-tuple-element.112), calls=%async_computation.2 | async-start | bytes 4718592 | tf_op jit(solution)/shard_map/all_to_all | solution.py:460
  68.0 14.2 %collective-permute-start.3 = (bf16[2,32,3072]{2,1,0:T(8,128)(2,1)S(1)}, bf16[2,32,3072]{2,1,0:T(8,128)(2,1)S(1)}, u32[]{:S(2)}, u32[]{:S(2)}) collective-permute-start(bf16[2,32,3072]{2,1,0:T(8,128)(2,1)S(1)} %copy-done.1), channel_id=1, source_target_pairs={{0,1},{1,0},{2,3},{3,2},{4,5},{5,4},{6,7},{7,6},{8,9},{9,8},{10,11... | collective-permute-start | bytes 1179656 | tf_op jit(solution)/shard_map/ppermute | solution.py:492
  68.1 14.0 %collective-permute-start.4 = (bf16[2,32,3072]{2,1,0:T(8,128)(2,1)S(1)}, bf16[2,32,3072]{2,1,0:T(8,128)(2,1)S(1)}, u32[]{:S(2)}, u32[]{:S(2)}) collective-permute-start(bf16[2,32,3072]{2,1,0:T(8,128)(2,1)S(1)} %collective-permute-done.refs_1_), channel_id=1, source_target_pairs={{0,1},{1,0},{2,3},{3,2},{4,5},{5,4},{6,7},{7,6},{8,9},{9,8},{10,11... | collective-permute-start | bytes 1179656 | tf_op jit(solution)/shard_map/ppermute | solution.py:492
  68.6 13.6 %collective-permute-start.5 = (bf16[2,32,3072]{2,1,0:T(8,128)(2,1)S(1)}, bf16[2,32,3072]{2,1,0:T(8,128)(2,1)S(1)}, u32[]{:S(2)}, u32[]{:S(2)}) collective-permute-start(bf16[2,32,3072]{2,1,0:T(8,128)(2,1)S(1)} %collective-permute-done.1.refs_2_), channel_id=1, source_target_pairs={{0,1},{1,0},{2,3},{3,2},{4,5},{5,4},{6,7},{7,6},{8,9},{9,8},{10,11... | collective-permute-start | bytes 1179656 | tf_op jit(solution)/shard_map/ppermute | solution.py:492
  68.7 13.5 %collective-permute-start.6 = (bf16[2,32,3072]{2,1,0:T(8,128)(2,1)S(1)}, bf16[2,32,3072]{2,1,0:T(8,128)(2,1)}, u32[]{:S(2)}, u32[]{:S(2)}) collective-permute-start(bf16[2,32,3072]{2,1,0:T(8,128)(2,1)S(1)} %collective-permute-done.2.refs_3_), channel_id=1, source_target_pairs={{0,1},{1,0},{2,3},{3,2},{4,5},{5,4},{6,7},{7,6},{8,9},{9,8},{10,11... | collective-permute-start | bytes 1179656 | tf_op jit(solution)/shard_map/ppermute | solution.py:492
  87.8 1.6 %copy-start = (bf16[512,3072]{1,0:T(8,128)(2,1)}, bf16[512,3072]{1,0:T(8,128)(2,1)S(1)}, u32[]{:S(2)}) copy-start(bf16[512,3072]{1,0:T(8,128)(2,1)S(1)} %get-tuple-element.111.l_ref) | copy-start | bytes 9437188
  89.4 0.7 copy-start.2

commit v5 on v4

--- a/solution.py
+++ b/solution.py
@@ -105,16 +105,15 @@
 
 
 def gather_kernel(
-    height, chunk, place, src_ref, dst_ref, p_ref, slab_ref, o_ref, a_ref, top_ref, low_ref, spread_ref, acc_ref, extra_ref, sems
+    height, chunk, tiles, place, src_ref, dst_ref, p_ref, slab_ref, o_ref, a_ref, top_ref, low_ref, spread_ref, acc_ref, extra_ref, sems
 ):
     width = src_ref.shape[1]
     slots = 2 * width
-    tiles, _, cols = a_ref.shape
+    cols = a_ref.shape[1] // tiles
     part = o_ref.shape[2]
-    copies = [
-        pltpu.make_async_copy(slab_ref.at[:, t * cols : (t + 1) * cols], a_ref.at[t], sems.at[t]) for t in range(tiles)
-    ]
-    for copy in copies:
+    tile = [slice(t * cols, (t + 1) * cols) for t in range(tiles)]
+    copies = [pltpu.make_async_copy(slab_ref.at[:, at], a_ref.at[:, at], sems.at[t]) for t, at in enumerate(tile)]
+    for copy in copies[:2]:
         copy.start()
 
     me = place[0].astype(F32)
@@ -156,10 +155,13 @@
 
     for t in range(tiles):
         copies[t].wait()
-        acc_ref[...] = dot(top_ref[...], a_ref[t, :slots, :])
-
-        def add(r, carry, t=t):
-            found = dot(low_ref[r], a_ref[t, slots:, :]).astype(BF16)
+        if t + 2 < tiles:
+            copies[t + 2].start()
+        at = tile[t]
+        acc_ref[...] = dot(top_ref[...], a_ref[:slots, at])
+
+        def add(r, carry, at=at):
+            found = dot(low_ref[r], a_ref[slots:, at]).astype(BF16)
             acc_ref[...] += dot(spread_ref[r], found)
             return carry
 
@@ -175,11 +177,11 @@
     slots, part = 2 * width, cols // devices
     chunk = min(LANES, slots)
     most = slots // chunk
-    tiles = 4
+    tiles = min(4, devices)
     piece = panels.shape[1]
     extra = piece * pl.cdiv(width, part)
     return pl.pallas_call(
-        functools.partial(gather_kernel, height, chunk),
+        functools.partial(gather_kernel, height, chunk, tiles),
         out_shape=jax.ShapeDtypeStruct((devices, slots + extra, part), BF16),
         grid_spec=pltpu.PrefetchScalarGridSpec(
             num_scalar_prefetch=1,
@@ -192,7 +194,7 @@
             ],
             out_specs=pl.BlockSpec((devices, slots + extra, part), lambda i, *_: (0, 0, 0)),
             scratch_shapes=[
-                pltpu.VMEM((tiles, height, cols // tiles), BF16),
+                pltpu.VMEM((height, cols), BF16),
                 pltpu.VMEM((slots, slots), BF16),
                 pltpu.VMEM((most, chunk, height - slots), BF16),
                 pltpu.VMEM((most, slots, chunk), BF16),
@@ -299,16 +301,15 @@
     )(inverse, own, key, received)
 
 
-def arrange_kernel(width, where, inv_ref, sel_ref, below_ref, land_ref, *refs):
-    *piece_refs, l_ref, w_ref, moving_ref = refs
-    chips = len(piece_refs) // 2
-    panels, piece, cols = piece_refs[0].shape
+def arrange_kernel(width, chips, origins, where, inv_ref, sel_ref, below_ref, land_ref, *refs):
+    *piece_refs, o_ref, w_ref, moving_ref, l_ref = refs
+    _, piece, cols = piece_refs[0].shape
     step = pl.program_id(0)
-    for i, ref in enumerate(piece_refs):
-        across = lax.rem(where[1] - i % chips + chips, chips)
-        column = 2 * across + lax.rem(where[2] + i // chips, 2)
-        for k in range(panels):
-            at = pl.multiple_of(k * width + column * piece, piece)
+    for ref, (back, flip, start) in zip(piece_refs, origins):
+        across = lax.rem(where[1] - back + chips, chips)
+        column = 2 * across + lax.rem(where[2] + flip, 2)
+        for k in range(ref.shape[0]):
+            at = pl.multiple_of((start + k) * width + column * piece, piece)
             l_ref[pl.ds(at, piece), :] = ref[k]
 
     @pl.when((step == 0) & (where[0] == 0))
@@ -325,6 +326,7 @@
     l_ref[:width, :] = jnp.where(
         landing.sum(0, keepdims=True) > 0, moved, l_ref[:width, :].astype(F32)
     ).astype(BF16)
+    o_ref[...] = l_ref[...].T
 
     @pl.when(step == 0)
     def _():
@@ -335,15 +337,15 @@
         w_ref[...] = coupling
 
 
-def arrange(inverse, selected, below, landing, parts, where):
+def arrange(inverse, selected, below, landing, chips, origins, parts, where):
     panels, piece, height = parts[0].shape
     width = below.shape[0]
     cols = min(512, height)
-    pieces = pl.BlockSpec((panels, piece, cols), lambda i, *_: (0, 0, i))
+    pieces = [pl.BlockSpec((part.shape[0], piece, cols), lambda i, *_: (0, 0, i)) for part in parts]
     return pl.pallas_call(
-        functools.partial(arrange_kernel, width),
+        functools.partial(arrange_kernel, width, chips, origins),
         out_shape=(
-            jax.ShapeDtypeStruct((panels * width, height), BF16),
+            jax.ShapeDtypeStruct((height, panels * width), BF16),
             jax.ShapeDtypeStruct((width, width), F32),
         ),
         grid_spec=pltpu.PrefetchScalarGridSpec(
@@ -355,12 +357,12 @@
                 pl.BlockSpec(below.shape, lambda i, *_: (0, 0)),
                 pl.BlockSpec((width, 1), lambda i, *_: (0, 0)),
             ]
-            + [pieces] * len(parts),
+            + pieces,
             out_specs=(
-                pl.BlockSpec((panels * width, cols), lambda i, *_: (0, i)),
+                pl.BlockSpec((cols, panels * width), lambda i, *_: (i, 0)),
                 pl.BlockSpec((width, width), lambda i, *_: (0, 0)),
             ),
-            scratch_shapes=[pltpu.VMEM((width, width), BF16)],
+            scratch_shapes=[pltpu.VMEM((width, width), BF16), pltpu.VMEM((panels * width, cols), BF16)],
         ),
         compiler_params=params(32),
         cost_estimate=pl.CostEstimate(flops=1 << 24, bytes_accessed=1 << 20, transcendentals=0),
@@ -368,38 +370,43 @@
 
 
 def update_kernel(
-    width, table, place, a_ref, l_ref, y_ref, w_ref, slab_ref, rest_ref, o_ref, u_ref, d_ref, sem
+    width, rows, table, place, w_ref, slab_ref, l_hbm, y_ref, rest_ref, o_ref, a_ref, l_ref, u_ref, d_ref, out_ref, ins, sems, load
 ):
-    step = pl.program_id(0)
-    rows = a_ref.shape[0]
     devices, _, part = y_ref.shape
-    more = table[2, pl.num_programs(0)] > CAP
-
-    @pl.when(step == 0)
-    def _():
-        for e in range(devices):
-            at = slice(e * part, (e + 1) * part)
-            u_ref[:, at] = y_ref[e, : 2 * width, :]
-            d_ref[:CAP, at] = y_ref[e, 2 * width :, :]
-        high = w_ref[...].astype(BF16)
-        rest = (w_ref[...] - high.astype(F32)).astype(BF16)
-        for c in range(0, u_ref.shape[1], 512):
-            at = slice(c, c + 512)
-            upper = u_ref[:width, at]
-            later = u_ref[width:, at].astype(F32) - (dot(high, upper) + dot(rest, upper))
-            u_ref[width:, at] = later.astype(BF16)
-
-    @pl.when((step == 0) & (place[0] == 0))
-    def _():
-        copy = pltpu.make_async_copy(slab_ref.at[: 2 * width], d_ref, sem)
+    height, cols = a_ref.shape
+    steps = height // rows
+    wide = min(512, cols)
+    first = place[0] == 0
+    block = [slice(i * rows, (i + 1) * rows) for i in range(steps)]
+    uppers, fills, loads = [], [], []
+    for e in range(devices):
+        at = slice(e * part, (e + 1) * part)
+        uppers.append(pltpu.make_async_copy(y_ref.at[e, : 2 * width], u_ref.at[:, at], load.at[e]))
+        fills.append(pltpu.make_async_copy(y_ref.at[e, 2 * width :], d_ref.at[:CAP, at], load.at[devices + e]))
+    for i, here in enumerate(block):
+        loads.append(
+            (
+                pltpu.make_async_copy(slab_ref.at[here], a_ref.at[here], ins.at[0, i]),
+                pltpu.make_async_copy(l_hbm.at[here], l_ref.at[here], ins.at[1, i]),
+            )
+        )
+    for copy in (*uppers, *fills, *loads[0], *loads[min(1, steps - 1)][: 2 if steps > 1 else 0]):
         copy.start()
+    for copy in uppers:
         copy.wait()
-
-    @pl.when((step == 0) & (place[0] != 0) & more)
+    high = w_ref[...].astype(BF16)
+    rest = (w_ref[...] - high.astype(F32)).astype(BF16)
+    for c in range(0, cols, wide):
+        at = slice(c, c + wide)
+        upper = u_ref[:width, at]
+        later = u_ref[width:, at].astype(F32) - (dot(high, upper) + dot(rest, upper))
+        u_ref[width:, at] = later.astype(BF16)
+
+    @pl.when(jnp.logical_not(first) & (table[2, steps] > CAP))
     def _():
         for e in range(devices):
             copy = pltpu.make_async_copy(
-                rest_ref.at[e, CAP : 2 * width], d_ref.at[CAP:, e * part : (e + 1) * part], sem
+                rest_ref.at[e, CAP : 2 * width], d_ref.at[CAP:, e * part : (e + 1) * part], sems.at[0]
             )
             copy.start()
             copy.wait()
@@ -407,53 +414,71 @@
     group = 16
 
     def fill(j, carry):
-        to, source = table[0, j] - step * rows, table[1, j]
-        taken = d_ref[pl.ds(pl.multiple_of(source // group * group, group), group), :].astype(F32)
+        to, source = table[0, j], table[1, j]
+        at = pl.ds(pl.multiple_of(source // group * group, group), group)
+        taken = jnp.where(first, a_ref[at, :].astype(F32), d_ref[at, :].astype(F32))
         lane = lax.broadcasted_iota(I32, taken.shape, 0)
         row = jnp.where(lane == source % group, taken, 0.0).sum(0, keepdims=True)
         target = pl.ds(pl.multiple_of(to // group * group, group), group)
         a_ref[target, :] = jnp.where(lane == to % group, row, a_ref[target, :].astype(F32)).astype(BF16)
         return carry
 
-    lax.fori_loop(table[2, step], table[2, step + 1], fill, 0)
-    for c in range(0, o_ref.shape[1], 512):
-        at = slice(c, c + 512)
-        o_ref[:, at] = (a_ref[:, at].astype(F32) - dot(l_ref[...], u_ref[:, at], TN)).astype(BF16)
-
-    @pl.when((place[0] == 0) & (step < 2 * width // rows))
-    def _():
-        o_ref[...] = u_ref[pl.ds(pl.multiple_of(step * rows, rows), rows), :]
+    for copy in fills:
+        copy.wait()
+    copies = []
+    for i, here in enumerate(block):
+        for copy in loads[i]:
+            copy.wait()
+        if i + 2 < steps:
+            for copy in loads[i + 2]:
+                copy.start()
+        lax.fori_loop(table[2, i], table[2, i + 1], fill, 0)
+        slot = i % 2
+        if i >= 2:
+            copies[i - 2].wait()
+        for c in range(0, cols, wide):
+            at = slice(c, c + wide)
+            out_ref[slot, :, at] = (a_ref[here, at].astype(F32) - dot(l_ref[here, :], u_ref[:, at])).astype(BF16)
+        if i == 0:
+
+            @pl.when(first)
+            def _():
+                out_ref[0] = u_ref[...]
+
+        copies.append(pltpu.make_async_copy(out_ref.at[slot], o_ref.at[here], sems.at[slot]))
+        copies[i].start()
+    for copy in copies[-2:]:
+        copy.wait()
 
 
 def update(slab, lower, upper, coupling, rest, table, place, rows):
     height, cols = slab.shape
-    width = lower.shape[0] // 2
+    width = lower.shape[1] // 2
+    devices, steps = upper.shape[0], height // rows
     return pl.pallas_call(
-        functools.partial(update_kernel, width),
+        functools.partial(update_kernel, width, rows),
         out_shape=jax.ShapeDtypeStruct(slab.shape, BF16),
         grid_spec=pltpu.PrefetchScalarGridSpec(
             num_scalar_prefetch=2,
-            grid=(height // rows,),
-            in_specs=[
-                pl.BlockSpec((rows, cols), lambda i, *_: (i, 0)),
-                pl.BlockSpec((2 * width, rows), lambda i, *_: (0, i)),
-                pl.BlockSpec(memory_space=pltpu.VMEM),
-                pl.BlockSpec(memory_space=pltpu.VMEM),
-                pl.BlockSpec(memory_space=pl.ANY),
-                pl.BlockSpec(memory_space=pl.ANY),
-            ],
-            out_specs=pl.BlockSpec((rows, cols), lambda i, *_: (i, 0)),
+            grid=(1,),
+            in_specs=[pl.BlockSpec(coupling.shape, lambda i, *_: (0, 0))] + [pl.BlockSpec(memory_space=pl.ANY)] * 4,
+            out_specs=pl.BlockSpec(memory_space=pl.ANY),
             scratch_shapes=[
+                pltpu.VMEM((height, cols), BF16),
+                pltpu.VMEM(lower.shape, BF16),
                 pltpu.VMEM((2 * width, cols), BF16),
                 pltpu.VMEM((2 * width, cols), BF16),
-                pltpu.SemaphoreType.DMA,
+                pltpu.VMEM((2, rows, cols), BF16),
+                pltpu.SemaphoreType.DMA((2, steps)),
+                pltpu.SemaphoreType.DMA((2,)),
+                pltpu.SemaphoreType.DMA((2 * devices,)),
             ],
         ),
         compiler_params=params(54),
         cost_estimate=pl.CostEstimate(
             flops=4 * height * cols * width, bytes_accessed=4 * height * cols, transcendentals=0
         ),
-    )(table, place, slab, lower, upper, coupling, slab, rest)
+    )(table, place, coupling, slab, lower, upper, rest)
 
 
 def exchange(x):
@@ -474,9 +499,11 @@
     columns = lax.axis_size("col")
     chips = columns // 2
     across, core = lax.axis_index("col") // 2, lax.axis_index("col") % 2
-    parts = [panels]
-    for s in range(1, chips):
-        parts.append(lax.ppermute(panels, "col", [(d, (d + 2 * s) % columns) for d in range(columns)]))
+
+    def forward(x, chips_on):
+        return lax.ppermute(x, "col", [(d, (d + 2 * chips_on) % columns) for d in range(columns)])
+
+    near = [forward(panels, s) for s in sorted({1, chips - 1} - {0} if chips > 1 else set())]
     diagonal = lax.all_gather(
         jnp.concatenate([diag_lower[0], diag_lower[1]], axis=1), "col", axis=0, tiled=True
     )
@@ -484,12 +511,18 @@
     inverse = invert(diagonal)
     own, key, table = tables(pivot_src, pivot_dst, place[None], height, devices, slots)
 
-    received, parts = lax.optimization_barrier((received, parts))
+    received, near = lax.optimization_barrier((received, near))
     sent, small = solve(inverse, own, key, received, width, panels.shape[1])
 
     small = lax.all_gather(small, "col", axis=0, tiled=True)
 
-    parts = parts + [lax.ppermute(part, "col", [(d, d ^ 1) for d in range(columns)]) for part in parts]
+    parts = [panels] + near
+    origins = [(0, 0, 0)] + [(s, 0, 0) for s in ((1, chips - 1) if chips > 2 else (1,) if chips > 1 else ())]
+    if chips == 4:
+        parts += [forward(near[0][:1], 1), forward(near[1][1:], 3)]
+        origins += [(2, 0, 0), (2, 0, 1)]
+    parts += [lax.ppermute(part, "col", [(d, d ^ 1) for d in range(columns)]) for part in parts]
+    origins += [(back, 1, start) for back, _, start in origins]
 
     selected, below = small[:, :width], small[:, width:slots]
     lower, coupling = arrange(
@@ -497,6 +530,8 @@
         selected,
         below,
         jnp.where(place == 0, pivot_dst[1], pivot_src[1]),
+        chips,
+        tuple(origins),
         parts,
         jnp.stack([offset, across, core]).astype(I32),
     )

time: 121 us -> 109 us (0.901)
  blocking collectives: 39.1 us -> 35 us
  waiting for transfers between devices: 11.4 us -> 7.59 us
  Pallas kernels: 43.6 us -> 40 us
  local copies, waits for them, and re-layouts: 4.03 us -> 5.35 us
    all_gather x1, blocking collectives: 26.3 us -> 19.2 us  [per_device(): lax.all_gather(jnp.concatenate([diag_lower[0], diag_lower[1]], axis=1), '...]
    all_to_all x2, waiting for transfers between devices: 11.4 us -> 6.35 us  [exchange(): return lax.all_to_all(x, 'row', 0, 0)]
    pallas_call x3, Pallas kernels: 34.5 us -> 30.9 us  [the longest x1 15.9 us: update(): pl.pallas_call(functools.partial(update_kernel, width, rows), out_shape=j...]
    all_gather x1, blocking collectives: 12.8 us -> 15.8 us  [per_device(): small = lax.all_gather(small, 'col', axis=0, tiled=True)]
    all_to_all x2, starting transfers between devices: 15.1 us -> 12.6 us  [exchange(): return lax.all_to_all(x, 'row', 0, 0)]
    ppermute x3 -> x4, starting transfers between devices: 4.68 us -> 6.1 us  [forward(): lax.ppermute(x, 'col', [(d, (d + 2 * chips_on) % columns) for d in range(...]
    slice x0 -> x2, local copies, waits for them, and re-layouts: none -> 1.37 us  [per_device(): parts += [forward(near[0][:1], 1), forward(near[1][1:], 3)]]
    ppermute x4 -> x5, waiting for transfers between devices: 0.01 us -> 1.24 us  [per_device(): lax.ppermute(part, 'col', [(d, d ^ 1) for d in range(columns)])]
  transfers between devices with their start and end apart: 9 -> 11, of which waited for: 1 -> 4; matrix products, arithmetic and copies ran while one was open for 1% -> 2% of each run, Pallas kernels for 9% -> 9%
where the time goes in v5:
time: 109 us
  Pallas kernels  40 us (37%)
  blocking collectives  35 us (32%)
  starting transfers between devices  19.8 us (18%)
  waiting for transfers between devices  7.59 us (7%)
  local copies, waits for them, and re-layouts  5.35 us (5%)
    all_gather x1, blocking collectives, per_device(): lax.all_gather(jnp.concatenate([diag_lower[0], diag_lower[1]], axis=1), '...  19.2 us
    pallas_call x1, Pallas kernels, update(): pl.pallas_call(functools.partial(update_kernel, width, rows), out_shape=j...  15.9 us
    all_gather x1, blocking collectives, per_device(): small = lax.all_gather(small, 'col', axis=0, tiled=True)  15.8 us
    all_to_all x2, starting transfers between devices, exchange(): return lax.all_to_all(x, 'row', 0, 0)  12.6 us
    pallas_call x1, Pallas kernels, gather(): pl.pallas_call(functools.partial(gather_kernel, height, chunk, tiles), ou...  10.6 us
    all_to_all x2, waiting for transfers between devices, exchange(): return lax.all_to_all(x, 'row', 0, 0)  6.35 us
    ppermute x4, starting transfers between devices, forward(): lax.ppermute(x, 'col', [(d, (d + 2 * chips_on) % columns) for d in range(...  6.1 us
    pallas_call x1, Pallas kernels, arrange(): pl.pallas_call(functools.partial(arrange_kernel, width, chips, origins),...  4.42 us
  transfers between devices with their start and end apart: 11, of which 4 were waited for; matrix products, arithmetic and copies ran while one was open for 2% of the time, Pallas kernels for 9%

profile of v5, /device:TPU:0, one launch (start us, length us, event | category | flops | bytes accessed | tf_op | source)
XLA Modules:
  0.0 108.9 jit_solution(2721819724689907337)
XLA Ops:
  0.0 10.6 %shard_map.55 = bf16[16,576,128]{2,1,0:T(8,128)(2,1)} custom-call(s32[1]{0:T(128)} %bitcast.2.place, s32[2,256]{1,0:T(2,128)} %src_ref.2, s32[2,256]{1,0:T(2,128)} %dst_ref.2, bf16[2,32,3072]{2,1,0:T(8,128)(2,1)} %refs_0_, bf16[3072,2048]{1,0:T(8,128)(2,1)} %slab_ref.3), custom_call_target="tpu_custom_call" | custom-call | flops 3221225472 | bytes 14680064 | tf_op jit(solution)/shard_map/pallas_call | solution.py:183
  10.6 8.2 %all-to-all-start.1 = ((bf16[16,576,128]{2,1,0:T(8,128)(2,1)}), bf16[16,576,128]{2,1,0:T(8,128)(2,1)}, u32[]{:S(2)}, u32[]{:S(2)}) async-start(bf16[16,576,128]{2,1,0:T(8,128)(2,1)} %shard_map.55), calls=%async_computation.1 | async-start | bytes 4718592 | tf_op jit(solution)/shard_map/all_to_all | solution.py:485
  18.9 3.1 %collective-permute-start.1 = (bf16[2,32,3072]{2,1,0:T(8,128)(2,1)S(1)}, bf16[2,32,3072]{2,1,0:T(8,128)(2,1)S(1)}, u32[]{:S(2)}, u32[]{:S(2)}) collective-permute-start(bf16[2,32,3072]{2,1,0:T(8,128)(2,1)S(1)} %copy-done.1), channel_id=1, source_target_pairs={{0,6},{1,7},{2,0},{3,1},{4,2},{5,3},{6,4},{7,5},{8,14},{9,15},{10,... | collective-permute-start | bytes 1179656 | tf_op jit(solution)/shard_map/ppermute | solution.py:504
  21.9 19.2 %all_gather.6.d_ref = bf16[256,512]{1,0:T(8,128)(2,1)S(1)} all-gather(bf16[32,512]{1,0:T(8,128)(2,1)S(1)} %pad_maximum_fusion), channel_id=1, replica_groups=mesh['row'=16,'col'=8] {'col'}, dimensions={0}, use_global_device_ids=true | all-gather | bytes 294912 | tf_op jit(solution)/shard_map/all_gather | solution.py:507
  41.2 1.9 %shard_map.56 = (f32[512,1]{1,0:T(8,128)S(1)}, f32[8,512]{1,0:T(8,128)S(1)}, s32[8,512]{1,0:T(8,128)S(1)}) custom-call(s32[1]{0:T(128)} %bitcast.2.place, s32[2,256]{1,0:T(2,128)S(1)} %copy-done.4, s32[2,256]{1,0:T(2,128)S(1)} %copy-done.5), custom_call_target="tpu_custom_call" | custom-call | tf_op jit(solution)/shard_map/pallas_call | solution.py:86
  43.1 0.5 slice.43
  44.2 3.0 %shard_map.57.inv_ref = f32[2,256,256]{2,1,0:T(8,128)S(1)} custom-call(bf16[256,512]{1,0:T(8,128)(2,1)S(1)} %all_gather.6.d_ref), custom_call_target="tpu_custom_call" | custom-call | flops 1048576 | bytes 262144 | tf_op jit(solution)/shard_map/pallas_call | solution.py:244
  47.3 5.3 %all-to-all-done.1.r_ref = bf16[16,576,128]{2,1,0:T(8,128)(2,1)} async-done(((bf16[16,576,128]{2,1,0:T(8,128)(2,1)}), bf16[16,576,128]{2,1,0:T(8,128)(2,1)}, u32[]{:S(2)}, u32[]{:S(2)}) %all-to-all-start.1) | async-done | bytes 2359328 | tf_op jit(solution)/shard_map/all_to_all | solution.py:485
  52.5 0.9 slice_bitcast_fusion
  53.4 4.2 %shard_map.58 = (bf16[16,576,128]{2,1,0:T(8,128)(2,1)}, bf16[32,512]{1,0:T(8,128)(2,1)S(1)}) custom-call(f32[2,256,256]{2,1,0:T(8,128)S(1)} %shard_map.57.inv_ref, f32[512,1]{1,0:T(8,128)S(1)} %get-tuple-element.99.own_ref, f32[8,512]{1,0:T(8,128)S(1)} %get-tuple-element.100.key_ref, bf16[16,576,128]{2,1,0:T(8,128)(2,1)} %all-to-all-done.1.r_ref), custom_call_target="tpu_custom_call" | custom-call | flops 536870912 | bytes 4194304 | tf_op jit(solution)/shard_map/pallas_call | solution.py:293
  57.6 4.4 %all-to-all-start.2 = ((bf16[16,576,128]{2,1,0:T(8,128)(2,1)}), bf16[16,576,128]{2,1,0:T(8,128)(2,1)}, u32[]{:S(2)}, u32[]{:S(2)}) async-start(bf16[16,576,128]{2,1,0:T(8,128)(2,1)} %get-tuple-element.109), calls=%async_computation.2 | async-start | bytes 4718592 | tf_op jit(solution)/shard_map/all_to_all | solution.py:485
  62.2 0.7 slice.41
  62.9 0.5 collective-permute-start.5
  63.3 0.7 slice.42
  64.1 3.0 %collective-permute-start.3 = (bf16[1,32,3072]{2,1,0:T(8,128)(2,1)}, bf16[1,32,3072]{2,1,0:T(8,128)(2,1)S(1)}, u32[]{:S(2)}, u32[]{:S(2)}) collective-permute-start(bf16[1,32,3072]{2,1,0:T(8,128)(2,1)} %slice.42), channel_id=1, source_target_pairs={{0,6},{1,7},{2,0},{3,1},{4,2},{5,3},{6,4},{7,5},{8,14},{9,15},{10,... | collective-permute-start | bytes 589832 | tf_op jit(solution)/shard_map/ppermute | solution.py:504
  67.3 15.8 %all_gather.7 = bf16[256,512]{1,0:T(8,128)(2,1)S(1)} all-gather(bf16[32,512]{1,0:T(8,128)(2,1)S(1)} %get-tuple-element.104), channel_id=1, replica_groups=mesh['row'=16,'col'=8] {'col'}, dimensions={0}, use_global_device_ids=true | all-gather | bytes 294912 | tf_op jit(solution)/shard_map/all_gather | solution.py:517
  83.1 0.4 collective-permute-start.8
  83.7 0.9 collective-permute-done.8.refs_9_
  84.5 0.4 collective-permute-done.7.refs_8_
  84.9 4.4 %shard_map.59 = (bf16[3072,512]{1,0:T(8,128)(2,1)S(1)}, f32[256,256]{1,0:T(8,128)S(1)}) custom-call(s32[3]{0:T(128)S(1)} %pad_add_fusion.where, f32[2,256,256]{2,1,0:T(8,128)S(1)} %shard_map.57.inv_ref, bf16[256,256]{1,0:T(8,128)(2,1)S(1)} %get-tuple-element.122.sel_ref, bf16[256,256]{1,0:T(8,128)(2,1)S(1)} %get-tuple-element.121.below_ref, ...), custom_call_target="tpu_custom_call" | custom-call | flops 16777216 | bytes 1048576 | tf_op jit(solution)/shard_map/pallas_call | solution.py:345
  89.3 1.6 %copy-done = bf16[3072,512]{1,0:T(8,128)(2,1)} copy-done((bf16[3072,512]{1,0:T(8,128)(2,1)}, bf16[3072,512]{1,0:T(8,128)(2,1)S(1)}, u32[]{:S(2)}) %copy-start) | copy-done | bytes 3145752
  91.0 0.7 copy-done.2
  91.7 1.1 all-to-all-done.2.y_ref
  92.8 15.9 %shard_map.60 = bf16[3072,2048]{1,0:T(8,128)(2,1)} custom-call(s32[8,512]{1,0:T(8,128)} %copy-done.3, s32[1]{0:T(128)} %bitcast.2.place, f32[256,256]{1,0:T(8,128)} %copy-done.2, bf16[3072,2048]{1,0:T(8,128)(2,1)} %slab_ref.3, bf16[3072,512]{1,0:T(8,128)(2,1)} %copy-done, bf16[16,576,128]{2,1,0:T(8,128)(2,1)} %all-to-all-done.2.y_ref, ...), custom_call_target="tpu_custom_call" | custom-call | flops 6442450944 | bytes 25165824 | tf_op jit(solution)/shard_map/pallas_call | solution.py:458
  (32 shorter events, 0.6 us)
Async XLA Ops:
  10.6 8.3 %copy-start.1 = (bf16[2,32,3072]{2,1,0:T(8,128)(2,1)S(1)}, bf16[2,32,3072]{2,1,0:T(8,128)(2,1)}, u32[]{:S(2)}) copy-start(bf16[2,32,3072]{2,1,0:T(8,128)(2,1)} %refs_0_) | copy-start | bytes 1179652
  10.6 11.3 %copy-start.6 = (bf16[2,32,256]{2,1,0:T(8,128)(2,1)S(1)}, bf16[2,32,256]{2,1,0:T(8,128)(2,1)}, u32[]{:S(2)}) copy-start(bf16[2,32,256]{2,1,0:T(8,128)(2,1)} %param.9) | copy-start | bytes 98308
  10.6 30.6 %copy-start.4 = (s32[2,256]{1,0:T(2,128)S(1)}, s32[2,256]{1,0:T(2,128)}, u32[]{:S(2)}) copy-start(s32[2,256]{1,0:T(2,128)} %src_ref.2) | copy-start | bytes 6148
  10.6 30.6 %copy-start.5 = (s32[2,256]{1,0:T(2,128)S(1)}, s32[2,256]{1,0:T(2,128)}, u32[]{:S(2)}) copy-start(s32[2,256]{1,0:T(2,128)} %dst_ref.2) | copy-start | bytes 6148
  10.6 41.9 %all-to-all-start.1 = ((bf16[16,576,128]{2,1,0:T(8,128)(2,1)}), bf16[16,576,128]{2,1,0:T(8,128)(2,1)}, u32[]{:S(2)}, u32[]{:S(2)}) async-start(bf16[16,576,128]{2,1,0:T(8,128)(2,1)} %shard_map.55), calls=%async_computation.1 | async-start | bytes 4718592 | tf_op jit(solution)/shard_map/all_to_all | solution.py:485
  18.9 28.4 %collective-permute-start.1 = (bf16[2,32,3072]{2,1,0:T(8,128)(2,1)S(1)}, bf16[2,32,3072]{2,1,0:T(8,128)(2,1)S(1)}, u32[]{:S(2)}, u32[]{:S(2)}) collective-permute-start(bf16[2,32,3072]{2,1,0:T(8,128)(2,1)S(1)} %copy-done.1), channel_id=1, source_target_pairs={{0,6},{1,7},{2,0},{3,1},{4,2},{5,3},{6,4},{7,5},{8,14},{9,15},{10,... | collective-permute-start | bytes 1179656 | tf_op jit(solution)/shard_map/ppermute | solution.py:504
  21.9 25.3 %collective-permute-start = (bf16[2,32,3072]{2,1,0:T(8,128)(2,1)S(1)}, bf16[2,32,3072]{2,1,0:T(8,128)(2,1)S(1)}, u32[]{:S(2)}, u32[]{:S(2)}) collective-permute-start(bf16[2,32,3072]{2,1,0:T(8,128)(2,1)S(1)} %copy-done.1), channel_id=1, source_target_pairs={{0,2},{1,3},{2,4},{3,5},{4,6},{5,7},{6,0},{7,1},{8,10},{9,11},{10,... | collective-permute-start | bytes 1179656 | tf_op jit(solution)/shard_map/ppermute | solution.py:504
  43.1 14.5 %copy-start.3 = (s32[8,512]{1,0:T(8,128)}, s32[8,512]{1,0:T(8,128)S(1)}, u32[]{:S(2)}) copy-start(s32[8,512]{1,0:T(8,128)S(1)} %get-tuple-element.97.table) | copy-start | bytes 49156
  57.6 35.2 %all-to-all-start.2 = ((bf16[16,576,128]{2,1,0:T(8,128)(2,1)}), bf16[16,576,128]{2,1,0:T(8,128)(2,1)}, u32[]{:S(2)}, u32[]{:S(2)}) async-start(bf16[16,576,128]{2,1,0:T(8,128)(2,1)} %get-tuple-element.109), calls=%async_computation.2 | async-start | bytes 4718592 | tf_op jit(solution)/shard_map/all_to_all | solution.py:485
  62.0 21.6 %collective-permute-start.4 = (bf16[2,32,3072]{2,1,0:T(8,128)(2,1)S(1)}, bf16[2,32,3072]{2,1,0:T(8,128)(2,1)S(1)}, u32[]{:S(2)}, u32[]{:S(2)}) collective-permute-start(bf16[2,32,3072]{2,1,0:T(8,128)(2,1)S(1)} %copy-done.1), channel_id=1, source_target_pairs={{0,1},{1,0},{2,3},{3,2},{4,5},{5,4},{6,7},{7,6},{8,9},{9,8},{10,11... | collective-permute-start | bytes 1179656 | tf_op jit(solution)/shard_map/ppermute | solution.py:524
  62.9 20.8 %collective-permute-start.5 = (bf16[2,32,3072]{2,1,0:T(8,128)(2,1)S(1)}, bf16[2,32,3072]{2,1,0:T(8,128)(2,1)S(1)}, u32[]{:S(2)}, u32[]{:S(2)}) collective-permute-start(bf16[2,32,3072]{2,1,0:T(8,128)(2,1)S(1)} %collective-permute-done.refs_1_), channel_id=1, source_target_pairs={{0,1},{1,0},{2,3},{3,2},{4,5},{5,4},{6,7},{7,6},{8,9},{9,8},{10,11... | collective-permute-start | bytes 1179656 | tf_op jit(solution)/shard_map/ppermute | solution.py:524
  64.0 19.6 %collective-permute-start.6 = (bf16[2,32,3072]{2,1,0:T(8,128)(2,1)S(1)}, bf16[2,32,3072]{2,1,0:T(8,128)(2,1)S(1)}, u32[]{:S(2)}, u32[]{:S(2)}) collective-permute-start(bf16[2,32,3072]{2,1,0:T(8,128)(2,1)S(1)} %collective-permute-done.1.refs_2_), channel_id=1, source_target_pairs={{0,1},{1,0},{2,3},{3,2},{4,5},{5,4},{6,7},{7,6},{8,9},{9,8},{10,11... | collective-permute-start | bytes 1179656 | tf_op jit(solution)/shard_map/ppermute | solution.py:524
  64.1 19.0 %collective-permute-start.3 = (bf16[1,32,3072]{2,1,0:T(8,128)(2,1)}, bf16[1,32,3072]{2,1,0:T(8,128)(2,1)S(1)}, u32[]{:S(2)}, u32[]{:S(2)}) collective-permute-start(bf16[1,32,3072]{2,1,0:T(8,128)(2,1)} %slice.42), channel_id=1, source_target_pairs={{0,6},{1,7},{2,0},{3,1},{4,2},{5,3},{6,4},{7,5},{8,14},{9,15},{10,... | collective-permute-start | bytes 589832 | tf_op jit(solution)/shard_map/ppermute | solution.py:504
  67.1 16.4 %collective-permute-start.2 = (bf16[1,32,3072]{2,1,0:T(8,128)(2,1)}, bf16[1,32,3072]{2,1,0:T(8,128)(2,1)S(1)}, u32[]{:S(2)}, u32[]{:S(2)}) collective-permute-start(bf16[1,32,3072]{2,1,0:T(8,128)(2,1)} %slice.41), channel_id=1, source_target_pairs={{0,2},{1,3},{2,4},{3,5},{4,6},{5,7},{6,0},{7,1},{8,10},{9,11},{10,... | collective-permute-start | bytes 589832 | tf_op jit(solution)/shard_map/ppermute | solution.py:504
  83.1 1.4 %collective-permute-start.8 = (bf16[1,32,3072]{2,1,0:T(8,128)(2,1)S(1)}, bf16[1,32,3072]{2,1,0:T(8,128)(2,1)S(1)}, u32[]{:S(2)}, u32[]{:S(2)}) collective-permute-start(bf16[1,32,3072]{2,1,0:T(8,128)(2,1)S(1)} %collective-permute-done.3.refs_4_), channel_id=1, source_target_pairs={{0,1},{1,0},{2,3},{3,2},{4,5},{5,4},{6,7},{7,6},{8,9},{9,8},{10,11... | collective-permute-start | bytes 589832 | tf_op jit(solution)/shard_map/ppermute | solution.py:524
  83.4 1.4 %collective-permute-start.7 = (bf16[1,32,3072]{2,1,0:T(8,128)(2,1)S(1)}, bf16[1,32,3072]{2,1,0:T(8,128)(2,1)S(1)}, u32[]{:S(2)}, u32[]{:S(2)}) collective-permute-start(bf16[1,32,3072]{2,1,0:T(8,128)(2,1)S(1)} %collective-permute-done.2.refs_3_), channel_id=1, source_target_pairs={{0,1},{1,0},{2,3},{3,2},{4,5},{5,4},{6,7},{7,6},{8,9},{9,8},{10,11... | collective-permute-start | bytes 589832 | tf_op jit(solution)/shard_map/ppermute | solution.py:524
  89.3 1.6 %copy-start = (bf16[3072,512]{1,0:T(8,128)(2,1)}, bf16[3072,512]{1,0:T(8,128)(2,1)S(1)}, u32[]{:S(2)}) copy-start(bf16[3072,512]{1,0:T(8,128)(2,1)S(1)} %get-tuple-element.108.l_hbm) | copy-start | bytes 9437188
  90.9 0.7 copy-start.2

commit v6 on v5

--- a/solution.py
+++ b/solution.py
@@ -105,7 +105,7 @@
 
 
 def gather_kernel(
-    height, chunk, tiles, place, src_ref, dst_ref, p_ref, slab_ref, o_ref, a_ref, top_ref, low_ref, spread_ref, acc_ref, extra_ref, sems
+    height, chunk, tiles, place, src_ref, dst_ref, p_ref, slab_ref, o_ref, a_ref, top_ref, low_ref, spread_ref, acc_ref, extra_ref, out_ref, sems, outs
 ):
     width = src_ref.shape[1]
     slots = 2 * width
@@ -145,14 +145,15 @@
     here = src1 - me * height
     moving = lookup(src1, dst_ref[1:2, :].astype(F32), lane + width, -1.0)
     chosen = jnp.where((here >= 0) & (here < height), here, jnp.where(me == 0, moving, -1.0))
-    row = lax.broadcasted_iota(I32, (width, height), 1).astype(F32)
-    hot = jnp.where(row == chosen, 1.0, 0.0).astype(BF16)
-    taken = dot(p_ref[0], hot, (((1,), (1,)), ((), ()))).astype(BF16)
+    row = lax.broadcasted_iota(I32, (height, width), 0).astype(F32)
+    hot = jnp.where(row == as_row(chosen), 1.0, 0.0).astype(BF16)
+    taken = dot(p_ref[0], hot).astype(BF16)
     piece = taken.shape[0]
     for h in range(extra_ref.shape[0] // piece):
         have = min(part, width - h * part)
         extra_ref[h * piece : (h + 1) * piece, :have] = taken[:, h * part : h * part + have]
 
+    sends = []
     for t in range(tiles):
         copies[t].wait()
         if t + 2 < tiles:
@@ -167,8 +168,13 @@
 
         lax.fori_loop(0, rounds, add, 0)
         for b in range(cols // part):
-            o_ref[t * (cols // part) + b, :slots, :] = acc_ref[:, b * part : (b + 1) * part].astype(BF16)
-            o_ref[t * (cols // part) + b, slots:, :] = extra_ref[...]
+            out_ref[t * (cols // part) + b, :slots, :] = acc_ref[:, b * part : (b + 1) * part].astype(BF16)
+            out_ref[t * (cols // part) + b, slots:, :] = extra_ref[...]
+        done = slice(t * (cols // part), (t + 1) * (cols // part))
+        sends.append(pltpu.make_async_copy(out_ref.at[done], o_ref.at[done], outs.at[t]))
+        sends[t].start()
+    for send in sends:
+        send.wait()
 
 
 def gather(slab, panels, pivot_src, pivot_dst, place, devices):
@@ -192,7 +198,7 @@
                 pl.BlockSpec((1, piece, height), lambda i, *_: (0, 0, 0)),
                 pl.BlockSpec(memory_space=pl.ANY),
             ],
-            out_specs=pl.BlockSpec((devices, slots + extra, part), lambda i, *_: (0, 0, 0)),
+            out_specs=pl.BlockSpec(memory_space=pl.ANY),
             scratch_shapes=[
                 pltpu.VMEM((height, cols), BF16),
                 pltpu.VMEM((slots, slots), BF16),
@@ -200,6 +206,8 @@
                 pltpu.VMEM((most, slots, chunk), BF16),
                 pltpu.VMEM((slots, cols // tiles), F32),
                 pltpu.VMEM((extra, part), BF16),
+                pltpu.VMEM((devices, slots + extra, part), BF16),
+                pltpu.SemaphoreType.DMA((tiles,)),
                 pltpu.SemaphoreType.DMA((tiles,)),
             ],
         ),
@@ -259,24 +267,37 @@
     return total.astype(BF16)
 
 
-def solve_kernel(width, piece, inv_ref, own_ref, key_ref, r_ref, y_ref, small_ref):
+def solve_kernel(
+    width, piece, inv_ref, own_ref, key_ref, r_hbm, y_ref, small_ref, zero_ref, r_ref, u_ref, fill_ref, ins, outs
+):
     devices, _, part = r_ref.shape
     slots = 2 * width
-    zero = r_ref[0, :slots, :]
-    total = jnp.where(own_ref[...] > 0, zero.astype(F32), 0.0)
-    for s in range(1, devices):
-        total = total + r_ref[s, :slots, :].astype(F32)
-    rows = total.astype(BF16)
-    upper = apply_inverse(inv_ref[0], rows[:width])
-    later = apply_inverse(inv_ref[1], rows[width:])
+    loads = [pltpu.make_async_copy(r_hbm.at[s], r_ref.at[s], ins.at[s]) for s in range(devices)]
+    for load in loads:
+        load.start()
     want = lax.broadcasted_iota(I32, (devices * CAP, slots), 0)
     want = (want // CAP) * slots + want % CAP
     hot = jnp.where(want.astype(F32) == key_ref[0:1, :], 1.0, 0.0).astype(BF16)
-    fill = dot(hot, zero).astype(BF16)
+    loads[0].wait()
+    zero = r_ref[0, :slots, :]
+    zero_ref[...] = zero
+    fill_ref[...] = dot(hot, zero).astype(BF16)
+    sends = []
     for d in range(devices):
-        y_ref[d, :width, :] = upper
-        y_ref[d, width:slots, :] = later
-        y_ref[d, slots:, :] = fill[d * CAP : (d + 1) * CAP]
+        fills = fill_ref.at[d * CAP : (d + 1) * CAP]
+        sends.append(pltpu.make_async_copy(fills, y_ref.at[d, slots:], outs.at[0, d]))
+        sends[-1].start()
+    total = jnp.where(own_ref[...] > 0, zero.astype(F32), 0.0)
+    for s in range(1, devices):
+        loads[s].wait()
+        total = total + r_ref[s, :slots, :].astype(F32)
+    rows = total.astype(BF16)
+    for k in range(2):
+        here = slice(k * width, (k + 1) * width)
+        u_ref[here, :] = apply_inverse(inv_ref[k], rows[here])
+        for d in range(devices):
+            sends.append(pltpu.make_async_copy(u_ref.at[here], y_ref.at[d, here], outs.at[1 + k, d]))
+            sends[-1].start()
     for h in range(pl.cdiv(width, part)):
         have = min(part, width - h * part)
         at = slice(slots + h * piece, slots + (h + 1) * piece)
@@ -286,17 +307,30 @@
             picked = picked + r_ref[s, at, :have].astype(F32)
         small_ref[:, h * part : h * part + have] = picked.astype(BF16)
         small_ref[:, width + h * part : width + h * part + have] = moving
+    for send in sends:
+        send.wait()
 
 
 def solve(inverse, own, key, received, width, piece):
     devices, _, part = received.shape
+    vmem = pl.BlockSpec(memory_space=pltpu.VMEM)
     return pl.pallas_call(
         functools.partial(solve_kernel, width, piece),
         out_shape=(
             jax.ShapeDtypeStruct((devices, 2 * width + CAP, part), BF16),
             jax.ShapeDtypeStruct((piece, 2 * width), BF16),
-        ),
-        compiler_params=params(32),
+            jax.ShapeDtypeStruct((2 * width, part), BF16),
+        ),
+        in_specs=[vmem, vmem, vmem, pl.BlockSpec(memory_space=pl.ANY)],
+        out_specs=(pl.BlockSpec(memory_space=pl.ANY), vmem, vmem),
+        scratch_shapes=[
+            pltpu.VMEM(received.shape, BF16),
+            pltpu.VMEM((2 * width, part), BF16),
+            pltpu.VMEM((devices * CAP, part), BF16),
+            pltpu.SemaphoreType.DMA((devices,)),
+            pltpu.SemaphoreType.DMA((3, devices)),
+        ],
+        compiler_params=params(24),
         cost_estimate=pl.CostEstimate(flops=1 << 29, bytes_accessed=4 << 20, transcendentals=0),
     )(inverse, own, key, received)
 
@@ -345,8 +379,8 @@
     return pl.pallas_call(
         functools.partial(arrange_kernel, width, chips, origins),
         out_shape=(
-            jax.ShapeDtypeStruct((height, panels * width), BF16),
-            jax.ShapeDtypeStruct((width, width), F32),
+            pltpu.HBM((height, panels * width), BF16),
+            pltpu.HBM((width, width), F32),
         ),
         grid_spec=pltpu.PrefetchScalarGridSpec(
             num_scalar_prefetch=1,
@@ -390,10 +424,13 @@
                 pltpu.make_async_copy(l_hbm.at[here], l_ref.at[here], ins.at[1, i]),
             )
         )
-    for copy in (*uppers, *fills, *loads[0], *loads[min(1, steps - 1)][: 2 if steps > 1 else 0]):
+    for copy in (*uppers, *fills, *loads[0]):
         copy.start()
     for copy in uppers:
         copy.wait()
+    if steps > 1:
+        for copy in loads[1]:
+            copy.start()
     high = w_ref[...].astype(BF16)
     rest = (w_ref[...] - high.astype(F32)).astype(BF16)
     for c in range(0, cols, wide):
@@ -406,22 +443,20 @@
     def _():
         for e in range(devices):
             copy = pltpu.make_async_copy(
-                rest_ref.at[e, CAP : 2 * width], d_ref.at[CAP:, e * part : (e + 1) * part], sems.at[0]
+                rest_ref.at[e, CAP : 2 * width], d_ref.at[CAP:, e * part : (e + 1) * part], sems.at[0, 0]
             )
             copy.start()
             copy.wait()
 
     group = 16
 
-    def fill(j, carry):
+    def put(from_ref, j):
         to, source = table[0, j], table[1, j]
-        at = pl.ds(pl.multiple_of(source // group * group, group), group)
-        taken = jnp.where(first, a_ref[at, :].astype(F32), d_ref[at, :].astype(F32))
+        taken = from_ref[pl.ds(pl.multiple_of(source // group * group, group), group), :].astype(F32)
         lane = lax.broadcasted_iota(I32, taken.shape, 0)
         row = jnp.where(lane == source % group, taken, 0.0).sum(0, keepdims=True)
         target = pl.ds(pl.multiple_of(to // group * group, group), group)
         a_ref[target, :] = jnp.where(lane == to % group, row, a_ref[target, :].astype(F32)).astype(BF16)
-        return carry
 
     for copy in fills:
         copy.wait()
@@ -432,22 +467,32 @@
         if i + 2 < steps:
             for copy in loads[i + 2]:
                 copy.start()
-        lax.fori_loop(table[2, i], table[2, i + 1], fill, 0)
         slot = i % 2
+
+        @pl.when(first)
+        def _(i=i):
+            pl.loop(table[2, i], table[2, i + 1])(lambda j: put(a_ref, j))
+
+        @pl.when(jnp.logical_not(first))
+        def _(i=i):
+            pl.loop(table[2, i], table[2, i + 1])(lambda j: put(d_ref, j))
+
         if i >= 2:
-            copies[i - 2].wait()
-        for c in range(0, cols, wide):
+            for copy in copies[i - 2]:
+                copy.wait()
+        copies.append([])
+        for b, c in enumerate(range(0, cols, wide)):
             at = slice(c, c + wide)
             out_ref[slot, :, at] = (a_ref[here, at].astype(F32) - dot(l_ref[here, :], u_ref[:, at])).astype(BF16)
-        if i == 0:
-
-            @pl.when(first)
-            def _():
-                out_ref[0] = u_ref[...]
-
-        copies.append(pltpu.make_async_copy(out_ref.at[slot], o_ref.at[here], sems.at[slot]))
-        copies[i].start()
-    for copy in copies[-2:]:
+            if i == 0:
+
+                @pl.when(first)
+                def _(at=at):
+                    out_ref[0, :, at] = u_ref[:, at]
+
+            copies[i].append(pltpu.make_async_copy(out_ref.at[slot, :, at], o_ref.at[here, at], sems.at[slot, b]))
+            copies[i][b].start()
+    for copy in sum(copies[-2:], []):
         copy.wait()
 
 
@@ -470,7 +515,7 @@
                 pltpu.VMEM((2 * width, cols), BF16),
                 pltpu.VMEM((2, rows, cols), BF16),
                 pltpu.SemaphoreType.DMA((2, steps)),
-                pltpu.SemaphoreType.DMA((2,)),
+                pltpu.SemaphoreType.DMA((2, pl.cdiv(cols, 512))),
                 pltpu.SemaphoreType.DMA((2 * devices,)),
             ],
         ),
@@ -512,7 +557,7 @@
     own, key, table = tables(pivot_src, pivot_dst, place[None], height, devices, slots)
 
     received, near = lax.optimization_barrier((received, near))
-    sent, small = solve(inverse, own, key, received, width, panels.shape[1])
+    sent, small, fills = solve(inverse, own, key, received, width, panels.shape[1])
 
     small = lax.all_gather(small, "col", axis=0, tiled=True)
 
@@ -536,7 +581,6 @@
         jnp.stack([offset, across, core]).astype(I32),
     )
 
-    fills = received[0, :slots]
     rounds = (table[3, 0] + CAP - 1) // CAP
 
     def fetch(state):

time: 109 us -> 107 us (0.982)
  local copies, waits for them, and re-layouts: 5.35 us -> 2.12 us
    unnamed x14 -> x10, local copies, waits for them, and re-layouts: 2.39 us -> 0.03 us
    pallas_call x1, Pallas kernels: 4.42 us -> 5.8 us  [arrange(): pl.pallas_call(functools.partial(arrange_kernel, width, chips, origins),...]
  transfers between devices with their start and end apart: 11 -> 11, of which waited for: 4 -> 4; matrix products, arithmetic and copies ran while one was open for 2% -> 2% of each run, Pallas kernels for 9% -> 10%
where the time goes in v6:
time: 107 us; the launch traced here: 106 us
  Pallas kernels  39.8 us (37%)
  blocking collectives  35 us (33%)
  starting transfers between devices  20 us (19%)
  waiting for transfers between devices  8.34 us (8%)
  local copies, waits for them, and re-layouts  2.12 us (2%)
    all_gather x1, blocking collectives, per_device(): lax.all_gather(jnp.concatenate([diag_lower[0], diag_lower[1]], axis=1), '...  19.3 us
    all_gather x1, blocking collectives, per_device(): small = lax.all_gather(small, 'col', axis=0, tiled=True)  15.8 us
    pallas_call x1, Pallas kernels, update(): pl.pallas_call(functools.partial(update_kernel, width, rows), out_shape=j...  15.3 us
    all_to_all x2, starting transfers between devices, exchange(): return lax.all_to_all(x, 'row', 0, 0)  12.5 us
    pallas_call x1, Pallas kernels, gather(): pl.pallas_call(functools.partial(gather_kernel, height, chunk, tiles), ou...  9.56 us
    all_to_all x2, waiting for transfers between devices, exchange(): return lax.all_to_all(x, 'row', 0, 0)  7.26 us
    ppermute x4, starting transfers between devices, forward(): lax.ppermute(x, 'col', [(d, (d + 2 * chips_on) % columns) for d in range(...  6.19 us
    pallas_call x1, Pallas kernels, arrange(): pl.pallas_call(functools.partial(arrange_kernel, width, chips, origins),...  5.8 us
  transfers between devices with their start and end apart: 11, of which 4 were waited for; matrix products, arithmetic and copies ran while one was open for 2% of the time, Pallas kernels for 10%

profile of v6, /device:TPU:0, one launch (start us, length us, event | category | flops | bytes accessed | tf_op | source)
XLA Modules:
  0.0 106.5 jit_solution(3647631884079725957)
XLA Ops:
  0.0 9.6 %shard_map.55 = bf16[16,576,128]{2,1,0:T(8,128)(2,1)} custom-call(s32[1]{0:T(128)} %bitcast.2.place, s32[2,256]{1,0:T(2,128)} %src_ref.2, s32[2,256]{1,0:T(2,128)} %dst_ref.2, bf16[2,32,3072]{2,1,0:T(8,128)(2,1)} %refs_0_, bf16[3072,2048]{1,0:T(8,128)(2,1)} %slab_ref.3), custom_call_target="tpu_custom_call" | custom-call | flops 3221225472 | bytes 14680064 | tf_op jit(solution)/shard_map/pallas_call | solution.py:189
  9.6 8.1 %all-to-all-start.1 = ((bf16[16,576,128]{2,1,0:T(8,128)(2,1)}), bf16[16,576,128]{2,1,0:T(8,128)(2,1)}, u32[]{:S(2)}, u32[]{:S(2)}) async-start(bf16[16,576,128]{2,1,0:T(8,128)(2,1)} %shard_map.55), calls=%async_computation.1 | async-start | bytes 4718592 | tf_op jit(solution)/shard_map/all_to_all | solution.py:530
  17.7 3.1 %collective-permute-start.1 = (bf16[2,32,3072]{2,1,0:T(8,128)(2,1)S(1)}, bf16[2,32,3072]{2,1,0:T(8,128)(2,1)S(1)}, u32[]{:S(2)}, u32[]{:S(2)}) collective-permute-start(bf16[2,32,3072]{2,1,0:T(8,128)(2,1)S(1)} %copy-done), channel_id=1, source_target_pairs={{0,6},{1,7},{2,0},{3,1},{4,2},{5,3},{6,4},{7,5},{8,14},{9,15},{10,... | collective-permute-start | bytes 1179656 | tf_op jit(solution)/shard_map/ppermute | solution.py:549
  20.9 19.3 %all_gather.6.d_ref = bf16[256,512]{1,0:T(8,128)(2,1)S(1)} all-gather(bf16[32,512]{1,0:T(8,128)(2,1)S(1)} %pad_maximum_fusion), channel_id=1, replica_groups=mesh['row'=16,'col'=8] {'col'}, dimensions={0}, use_global_device_ids=true | all-gather | bytes 294912 | tf_op jit(solution)/shard_map/all_gather | solution.py:552
  40.1 1.9 %shard_map.56 = (f32[512,1]{1,0:T(8,128)S(1)}, f32[8,512]{1,0:T(8,128)S(1)}, s32[8,512]{1,0:T(8,128)S(1)}) custom-call(s32[1]{0:T(128)} %bitcast.2.place, s32[2,256]{1,0:T(2,128)S(1)} %copy-done.2, s32[2,256]{1,0:T(2,128)S(1)} %copy-done.3), custom_call_target="tpu_custom_call" | custom-call | tf_op jit(solution)/shard_map/pallas_call | solution.py:86
  42.0 0.6 slice.40
  43.2 3.0 %shard_map.57.inv_ref = f32[2,256,256]{2,1,0:T(8,128)S(1)} custom-call(bf16[256,512]{1,0:T(8,128)(2,1)S(1)} %all_gather.6.d_ref), custom_call_target="tpu_custom_call" | custom-call | flops 1048576 | bytes 262144 | tf_op jit(solution)/shard_map/pallas_call | solution.py:252
  46.3 5.1 %all-to-all-done.1.r_hbm = bf16[16,576,128]{2,1,0:T(8,128)(2,1)} async-done(((bf16[16,576,128]{2,1,0:T(8,128)(2,1)}), bf16[16,576,128]{2,1,0:T(8,128)(2,1)}, u32[]{:S(2)}, u32[]{:S(2)}) %all-to-all-start.1) | async-done | bytes 2359328 | tf_op jit(solution)/shard_map/all_to_all | solution.py:530
  51.5 4.2 %shard_map.58 = (bf16[16,576,128]{2,1,0:T(8,128)(2,1)}, bf16[32,512]{1,0:T(8,128)(2,1)S(1)}, bf16[512,128]{1,0:T(8,128)(2,1)S(1)}) custom-call(f32[2,256,256]{2,1,0:T(8,128)S(1)} %shard_map.57.inv_ref, f32[512,1]{1,0:T(8,128)S(1)} %get-tuple-element.100.own_ref, f32[8,512]{1,0:T(8,128)S(1)} %get-tuple-element.101.key_ref, ...), custom_call_target="tpu_custom_call" | custom-call | flops 536870912 | bytes 4194304 | tf_op jit(solution)/shard_map/pallas_call | solution.py:317
  55.7 4.5 %all-to-all-start.2 = ((bf16[16,576,128]{2,1,0:T(8,128)(2,1)}), bf16[16,576,128]{2,1,0:T(8,128)(2,1)}, u32[]{:S(2)}, u32[]{:S(2)}) async-start(bf16[16,576,128]{2,1,0:T(8,128)(2,1)} %get-tuple-element.110), calls=%async_computation.2 | async-start | bytes 4718592 | tf_op jit(solution)/shard_map/all_to_all | solution.py:530
  60.2 0.1 collective-permute-start.4
  60.3 0.7 slice.38
  61.0 0.5 collective-permute-start.5
  61.4 0.7 slice.39
  62.2 3.1 %collective-permute-start.3 = (bf16[1,32,3072]{2,1,0:T(8,128)(2,1)}, bf16[1,32,3072]{2,1,0:T(8,128)(2,1)S(1)}, u32[]{:S(2)}, u32[]{:S(2)}) collective-permute-start(bf16[1,32,3072]{2,1,0:T(8,128)(2,1)} %slice.39), channel_id=1, source_target_pairs={{0,6},{1,7},{2,0},{3,1},{4,2},{5,3},{6,4},{7,5},{8,14},{9,15},{10,... | collective-permute-start | bytes 589832 | tf_op jit(solution)/shard_map/ppermute | solution.py:549
  65.3 0.1 copy.6.land_ref
  65.4 15.8 %all_gather.7 = bf16[256,512]{1,0:T(8,128)(2,1)S(1)} all-gather(bf16[32,512]{1,0:T(8,128)(2,1)S(1)} %get-tuple-element.105), channel_id=1, replica_groups=mesh['row'=16,'col'=8] {'col'}, dimensions={0}, use_global_device_ids=true | all-gather | bytes 294912 | tf_op jit(solution)/shard_map/all_gather | solution.py:562
  81.2 0.4 collective-permute-start.8
  81.6 0.3 collective-permute-start.7
  82.0 0.7 collective-permute-done.8.refs_9_
  82.7 0.4 collective-permute-done.7.refs_8_
  83.0 5.8 %shard_map.59 = (bf16[3072,512]{1,0:T(8,128)(2,1)}, f32[256,256]{1,0:T(8,128)}) custom-call(s32[3]{0:T(128)S(1)} %pad_add_fusion.where, f32[2,256,256]{2,1,0:T(8,128)S(1)} %shard_map.57.inv_ref, bf16[256,256]{1,0:T(8,128)(2,1)S(1)} %get-tuple-element.124.sel_ref, bf16[256,256]{1,0:T(8,128)(2,1)S(1)} %get-tuple-element.123.below_ref, ...), custom_call_target="tpu_custom_call" | custom-call | flops 16777216 | bytes 1048576 | tf_op jit(solution)/shard_map/pallas_call | solution.py:379
  88.8 2.1 %all-to-all-done.2.y_ref = bf16[16,576,128]{2,1,0:T(8,128)(2,1)} async-done(((bf16[16,576,128]{2,1,0:T(8,128)(2,1)}), bf16[16,576,128]{2,1,0:T(8,128)(2,1)}, u32[]{:S(2)}, u32[]{:S(2)}) %all-to-all-start.2) | async-done | bytes 2359328 | tf_op jit(solution)/shard_map/all_to_all | solution.py:530
  90.9 15.3 %shard_map.60 = bf16[3072,2048]{1,0:T(8,128)(2,1)} custom-call(s32[8,512]{1,0:T(8,128)} %copy-done.1, s32[1]{0:T(128)} %bitcast.2.place, f32[256,256]{1,0:T(8,128)} %get-tuple-element.108.w_ref, bf16[3072,2048]{1,0:T(8,128)(2,1)} %slab_ref.3, bf16[3072,512]{1,0:T(8,128)(2,1)} %get-tuple-element.109.l_hbm, bf16[16,576,128]{2,1,0:T(8,128)(2,1)} %all-to-all-done.2.y_ref, ...), custom_call_target="tpu_custom_call" | custom-call | flops 6442450944 | bytes 25165824 | tf_op jit(solution)/shard_map/pallas_call | solution.py:503
  (27 shorter events, 0.2 us)
Async XLA Ops:
  9.6 8.2 %copy-start = (bf16[2,32,3072]{2,1,0:T(8,128)(2,1)S(1)}, bf16[2,32,3072]{2,1,0:T(8,128)(2,1)}, u32[]{:S(2)}) copy-start(bf16[2,32,3072]{2,1,0:T(8,128)(2,1)} %refs_0_) | copy-start | bytes 1179652
  9.6 11.3 %copy-start.4 = (bf16[2,32,256]{2,1,0:T(8,128)(2,1)S(1)}, bf16[2,32,256]{2,1,0:T(8,128)(2,1)}, u32[]{:S(2)}) copy-start(bf16[2,32,256]{2,1,0:T(8,128)(2,1)} %param.9) | copy-start | bytes 98308
  9.6 30.5 %copy-start.2 = (s32[2,256]{1,0:T(2,128)S(1)}, s32[2,256]{1,0:T(2,128)}, u32[]{:S(2)}) copy-start(s32[2,256]{1,0:T(2,128)} %src_ref.2) | copy-start | bytes 6148
  9.6 30.5 %copy-start.3 = (s32[2,256]{1,0:T(2,128)S(1)}, s32[2,256]{1,0:T(2,128)}, u32[]{:S(2)}) copy-start(s32[2,256]{1,0:T(2,128)} %dst_ref.2) | copy-start | bytes 6148
  9.6 41.8 %all-to-all-start.1 = ((bf16[16,576,128]{2,1,0:T(8,128)(2,1)}), bf16[16,576,128]{2,1,0:T(8,128)(2,1)}, u32[]{:S(2)}, u32[]{:S(2)}) async-start(bf16[16,576,128]{2,1,0:T(8,128)(2,1)} %shard_map.55), calls=%async_computation.1 | async-start | bytes 4718592 | tf_op jit(solution)/shard_map/all_to_all | solution.py:530
  17.7 28.6 %collective-permute-start.1 = (bf16[2,32,3072]{2,1,0:T(8,128)(2,1)S(1)}, bf16[2,32,3072]{2,1,0:T(8,128)(2,1)S(1)}, u32[]{:S(2)}, u32[]{:S(2)}) collective-permute-start(bf16[2,32,3072]{2,1,0:T(8,128)(2,1)S(1)} %copy-done), channel_id=1, source_target_pairs={{0,6},{1,7},{2,0},{3,1},{4,2},{5,3},{6,4},{7,5},{8,14},{9,15},{10,... | collective-permute-start | bytes 1179656 | tf_op jit(solution)/shard_map/ppermute | solution.py:549
  20.9 25.5 %collective-permute-start = (bf16[2,32,3072]{2,1,0:T(8,128)(2,1)S(1)}, bf16[2,32,3072]{2,1,0:T(8,128)(2,1)S(1)}, u32[]{:S(2)}, u32[]{:S(2)}) collective-permute-start(bf16[2,32,3072]{2,1,0:T(8,128)(2,1)S(1)} %copy-done), channel_id=1, source_target_pairs={{0,2},{1,3},{2,4},{3,5},{4,6},{5,7},{6,0},{7,1},{8,10},{9,11},{10,... | collective-permute-start | bytes 1179656 | tf_op jit(solution)/shard_map/ppermute | solution.py:549
  42.0 13.7 %copy-start.1 = (s32[8,512]{1,0:T(8,128)}, s32[8,512]{1,0:T(8,128)S(1)}, u32[]{:S(2)}) copy-start(s32[8,512]{1,0:T(8,128)S(1)} %get-tuple-element.98.table) | copy-start | bytes 49156
  55.7 35.2 %all-to-all-start.2 = ((bf16[16,576,128]{2,1,0:T(8,128)(2,1)}), bf16[16,576,128]{2,1,0:T(8,128)(2,1)}, u32[]{:S(2)}, u32[]{:S(2)}) async-start(bf16[16,576,128]{2,1,0:T(8,128)(2,1)} %get-tuple-element.110), calls=%async_computation.2 | async-start | bytes 4718592 | tf_op jit(solution)/shard_map/all_to_all | solution.py:530
  60.2 21.8 %collective-permute-start.4 = (bf16[2,32,3072]{2,1,0:T(8,128)(2,1)S(1)}, bf16[2,32,3072]{2,1,0:T(8,128)(2,1)S(1)}, u32[]{:S(2)}, u32[]{:S(2)}) collective-permute-start(bf16[2,32,3072]{2,1,0:T(8,128)(2,1)S(1)} %copy-done), channel_id=1, source_target_pairs={{0,1},{1,0},{2,3},{3,2},{4,5},{5,4},{6,7},{7,6},{8,9},{9,8},{10,11... | collective-permute-start | bytes 1179656 | tf_op jit(solution)/shard_map/ppermute | solution.py:569
  61.0 21.0 %collective-permute-start.5 = (bf16[2,32,3072]{2,1,0:T(8,128)(2,1)S(1)}, bf16[2,32,3072]{2,1,0:T(8,128)(2,1)S(1)}, u32[]{:S(2)}, u32[]{:S(2)}) collective-permute-start(bf16[2,32,3072]{2,1,0:T(8,128)(2,1)S(1)} %collective-permute-done.refs_1_), channel_id=1, source_target_pairs={{0,1},{1,0},{2,3},{3,2},{4,5},{5,4},{6,7},{7,6},{8,9},{9,8},{10,11... | collective-permute-start | bytes 1179656 | tf_op jit(solution)/shard_map/ppermute | solution.py:569
  62.1 19.8 %collective-permute-start.6 = (bf16[2,32,3072]{2,1,0:T(8,128)(2,1)S(1)}, bf16[2,32,3072]{2,1,0:T(8,128)(2,1)S(1)}, u32[]{:S(2)}, u32[]{:S(2)}) collective-permute-start(bf16[2,32,3072]{2,1,0:T(8,128)(2,1)S(1)} %collective-permute-done.1.refs_2_), channel_id=1, source_target_pairs={{0,1},{1,0},{2,3},{3,2},{4,5},{5,4},{6,7},{7,6},{8,9},{9,8},{10,11... | collective-permute-start | bytes 1179656 | tf_op jit(solution)/shard_map/ppermute | solution.py:569
  62.2 19.1 %collective-permute-start.3 = (bf16[1,32,3072]{2,1,0:T(8,128)(2,1)}, bf16[1,32,3072]{2,1,0:T(8,128)(2,1)S(1)}, u32[]{:S(2)}, u32[]{:S(2)}) collective-permute-start(bf16[1,32,3072]{2,1,0:T(8,128)(2,1)} %slice.39), channel_id=1, source_target_pairs={{0,6},{1,7},{2,0},{3,1},{4,2},{5,3},{6,4},{7,5},{8,14},{9,15},{10,... | collective-permute-start | bytes 589832 | tf_op jit(solution)/shard_map/ppermute | solution.py:549
  65.2 16.4 %collective-permute-start.2 = (bf16[1,32,3072]{2,1,0:T(8,128)(2,1)}, bf16[1,32,3072]{2,1,0:T(8,128)(2,1)S(1)}, u32[]{:S(2)}, u32[]{:S(2)}) collective-permute-start(bf16[1,32,3072]{2,1,0:T(8,128)(2,1)} %slice.38), channel_id=1, source_target_pairs={{0,2},{1,3},{2,4},{3,5},{4,6},{5,7},{6,0},{7,1},{8,10},{9,11},{10,... | collective-permute-start | bytes 589832 | tf_op jit(solution)/shard_map/ppermute | solution.py:549
  81.2 1.4 %collective-permute-start.8 = (bf16[1,32,3072]{2,1,0:T(8,128)(2,1)S(1)}, bf16[1,32,3072]{2,1,0:T(8,128)(2,1)S(1)}, u32[]{:S(2)}, u32[]{:S(2)}) collective-permute-start(bf16[1,32,3072]{2,1,0:T(8,128)(2,1)S(1)} %collective-permute-done.3.refs_4_), channel_id=1, source_target_pairs={{0,1},{1,0},{2,3},{3,2},{4,5},{5,4},{6,7},{7,6},{8,9},{9,8},{10,11... | collective-permute-start | bytes 589832 | tf_op jit(solution)/shard_map/ppermute | solution.py:569
  81.6 1.4 %collective-permute-start.7 = (bf16[1,32,3072]{2,1,0:T(8,128)(2,1)S(1)}, bf16[1,32,3072]{2,1,0:T(8,128)(2,1)S(1)}, u32[]{:S(2)}, u32[]{:S(2)}) collective-permute-start(bf16[1,32,3072]{2,1,0:T(8,128)(2,1)S(1)} %collective-permute-done.2.refs_3_), channel_id=1, source_target_pairs={{0,1},{1,0},{2,3},{3,2},{4,5},{5,4},{6,7},{7,6},{8,9},{9,8},{10,11... | collective-permute-start | bytes 589832 | tf_op jit(solution)/shard_map/ppermute | solution.py:569

commit v7 on v6

--- a/solution.py
+++ b/solution.py
@@ -259,7 +259,7 @@
 
 def apply_inverse(inverse, rows):
     total = None
-    for _ in range(3):
+    for _ in range(2):
         part = inverse.astype(BF16)
         inverse = inverse - part.astype(F32)
         term = dot(part, rows)
@@ -287,11 +287,10 @@
         fills = fill_ref.at[d * CAP : (d + 1) * CAP]
         sends.append(pltpu.make_async_copy(fills, y_ref.at[d, slots:], outs.at[0, d]))
         sends[-1].start()
-    total = jnp.where(own_ref[...] > 0, zero.astype(F32), 0.0)
+    rows = jnp.where(own_ref[...] > 0, zero.astype(F32), 0.0).astype(BF16)
     for s in range(1, devices):
         loads[s].wait()
-        total = total + r_ref[s, :slots, :].astype(F32)
-    rows = total.astype(BF16)
+        rows = rows + r_ref[s, :slots, :]
     for k in range(2):
         here = slice(k * width, (k + 1) * width)
         u_ref[here, :] = apply_inverse(inv_ref[k], rows[here])
@@ -302,10 +301,10 @@
         have = min(part, width - h * part)
         at = slice(slots + h * piece, slots + (h + 1) * piece)
         moving = r_ref[0, at, :have]
-        picked = jnp.where(key_ref[1:2, h * part : h * part + have] > 0, moving.astype(F32), 0.0)
+        picked = jnp.where(key_ref[1:2, h * part : h * part + have] > 0, moving.astype(F32), 0.0).astype(BF16)
         for s in range(1, devices):
-            picked = picked + r_ref[s, at, :have].astype(F32)
-        small_ref[:, h * part : h * part + have] = picked.astype(BF16)
+            picked = picked + r_ref[s, at, :have]
+        small_ref[:, h * part : h * part + have] = picked
         small_ref[:, width + h * part : width + h * part + have] = moving
     for send in sends:
         send.wait()
@@ -404,7 +403,7 @@
 
 
 def update_kernel(
-    width, rows, table, place, w_ref, slab_ref, l_hbm, y_ref, rest_ref, o_ref, a_ref, l_ref, u_ref, d_ref, out_ref, ins, sems, load
+    width, rows, table, place, w_ref, slab_ref, l_hbm, y_ref, rest_ref, o_ref, a_ref, l_ref, u_ref, d_ref, f_ref, out_ref, ins, sems, load
 ):
     devices, _, part = y_ref.shape
     height, cols = a_ref.shape
@@ -424,13 +423,12 @@
                 pltpu.make_async_copy(l_hbm.at[here], l_ref.at[here], ins.at[1, i]),
             )
         )
-    for copy in (*uppers, *fills, *loads[0]):
+    for copy in (*uppers, *fills):
         copy.start()
-    for copy in uppers:
+    for copy in (*uppers, *fills):
         copy.wait()
-    if steps > 1:
-        for copy in loads[1]:
-            copy.start()
+    for copy in sum((list(pair) for pair in loads[:2]), []):
+        copy.start()
     high = w_ref[...].astype(BF16)
     rest = (w_ref[...] - high.astype(F32)).astype(BF16)
     for c in range(0, cols, wide):
@@ -450,16 +448,24 @@
 
     group = 16
 
-    def put(from_ref, j):
-        to, source = table[0, j], table[1, j]
+    def put(row, to):
+        target = pl.ds(pl.multiple_of(to // group * group, group), group)
+        old = a_ref[target, :].astype(F32)
+        lane = lax.broadcasted_iota(I32, old.shape, 0)
+        a_ref[target, :] = jnp.where(lane == to % group, row, old).astype(BF16)
+
+    def put_from(from_ref, j):
+        source = table[1, j]
         taken = from_ref[pl.ds(pl.multiple_of(source // group * group, group), group), :].astype(F32)
         lane = lax.broadcasted_iota(I32, taken.shape, 0)
-        row = jnp.where(lane == source % group, taken, 0.0).sum(0, keepdims=True)
-        target = pl.ds(pl.multiple_of(to // group * group, group), group)
-        a_ref[target, :] = jnp.where(lane == to % group, row, a_ref[target, :].astype(F32)).astype(BF16)
-
-    for copy in fills:
-        copy.wait()
+        put(jnp.where(lane == source % group, taken, 0.0).sum(0, keepdims=True), table[0, j])
+
+    @pl.when(jnp.logical_not(first))
+    def _():
+        f_ref[...] = d_ref[:CAP, :].astype(F32)
+
+    few = table[2, steps] <= CAP
+
     copies = []
     for i, here in enumerate(block):
         for copy in loads[i]:
@@ -471,11 +477,15 @@
 
         @pl.when(first)
         def _(i=i):
-            pl.loop(table[2, i], table[2, i + 1])(lambda j: put(a_ref, j))
-
-        @pl.when(jnp.logical_not(first))
+            pl.loop(table[2, i], table[2, i + 1])(lambda j: put_from(a_ref, j))
+
+        @pl.when(jnp.logical_not(first) & few)
         def _(i=i):
-            pl.loop(table[2, i], table[2, i + 1])(lambda j: put(d_ref, j))
+            pl.loop(table[2, i], table[2, i + 1])(lambda j: put(f_ref[pl.ds(table[1, j], 1), :], table[0, j]))
+
+        @pl.when(jnp.logical_not(first) & jnp.logical_not(few))
+        def _(i=i):
+            pl.loop(table[2, i], table[2, i + 1])(lambda j: put_from(d_ref, j))
 
         if i >= 2:
             for copy in copies[i - 2]:
@@ -513,6 +523,7 @@
                 pltpu.VMEM(lower.shape, BF16),
                 pltpu.VMEM((2 * width, cols), BF16),
                 pltpu.VMEM((2 * width, cols), BF16),
+                pltpu.VMEM((CAP, cols), F32),
                 pltpu.VMEM((2, rows, cols), BF16),
                 pltpu.SemaphoreType.DMA((2, steps)),
                 pltpu.SemaphoreType.DMA((2, pl.cdiv(cols, 512))),

time: 107 us -> 107 us (level)
  no operation moved by 1% of the time
where the time goes in v7:
time: 107 us
  Pallas kernels  40.1 us (37%)
  blocking collectives  35 us (33%)
  starting transfers between devices  19.8 us (19%)
  waiting for transfers between devices  8.51 us (8%)
  local copies, waits for them, and re-layouts  2.12 us (2%)
    all_gather x1, blocking collectives, per_device(): lax.all_gather(jnp.concatenate([diag_lower[0], diag_lower[1]], axis=1), '...  19.3 us
    pallas_call x1, Pallas kernels, update(): pl.pallas_call(functools.partial(update_kernel, width, rows), out_shape=j...  16 us
    all_gather x1, blocking collectives, per_device(): small = lax.all_gather(small, 'col', axis=0, tiled=True)  15.8 us
    all_to_all x2, starting transfers between devices, exchange(): return lax.all_to_all(x, 'row', 0, 0)  12.5 us
    pallas_call x1, Pallas kernels, gather(): pl.pallas_call(functools.partial(gather_kernel, height, chunk, tiles), ou...  9.56 us
    all_to_all x2, waiting for transfers between devices, exchange(): return lax.all_to_all(x, 'row', 0, 0)  7.26 us
    ppermute x4, starting transfers between devices, forward(): lax.ppermute(x, 'col', [(d, (d + 2 * chips_on) % columns) for d in range(...  6.19 us
    pallas_call x1, Pallas kernels, arrange(): pl.pallas_call(functools.partial(arrange_kernel, width, chips, origins),...  5.8 us
  transfers between devices with their start and end apart: 11, of which 4 were waited for; matrix products, arithmetic and copies ran while one was open for 2% of the time, Pallas kernels for 10%

profile of v7, /device:TPU:0, one launch (start us, length us, event | category | flops | bytes accessed | tf_op | source)
XLA Modules:
  0.0 106.7 jit_solution(11606905719683969513)
XLA Ops:
  0.0 9.6 %shard_map.55 = bf16[16,576,128]{2,1,0:T(8,128)(2,1)} custom-call(s32[1]{0:T(128)} %bitcast.2.place, s32[2,256]{1,0:T(2,128)} %src_ref.2, s32[2,256]{1,0:T(2,128)} %dst_ref.2, bf16[2,32,3072]{2,1,0:T(8,128)(2,1)} %refs_0_, bf16[3072,2048]{1,0:T(8,128)(2,1)} %slab_ref.3), custom_call_target="tpu_custom_call" | custom-call | flops 3221225472 | bytes 14680064 | tf_op jit(solution)/shard_map/pallas_call | solution.py:189
  9.6 8.1 %all-to-all-start.1 = ((bf16[16,576,128]{2,1,0:T(8,128)(2,1)}), bf16[16,576,128]{2,1,0:T(8,128)(2,1)}, u32[]{:S(2)}, u32[]{:S(2)}) async-start(bf16[16,576,128]{2,1,0:T(8,128)(2,1)} %shard_map.55), calls=%async_computation.1 | async-start | bytes 4718592 | tf_op jit(solution)/shard_map/all_to_all | solution.py:541
  17.7 3.1 %collective-permute-start.1 = (bf16[2,32,3072]{2,1,0:T(8,128)(2,1)S(1)}, bf16[2,32,3072]{2,1,0:T(8,128)(2,1)S(1)}, u32[]{:S(2)}, u32[]{:S(2)}) collective-permute-start(bf16[2,32,3072]{2,1,0:T(8,128)(2,1)S(1)} %copy-done), channel_id=1, source_target_pairs={{0,6},{1,7},{2,0},{3,1},{4,2},{5,3},{6,4},{7,5},{8,14},{9,15},{10,... | collective-permute-start | bytes 1179656 | tf_op jit(solution)/shard_map/ppermute | solution.py:560
  20.9 19.3 %all_gather.6.d_ref = bf16[256,512]{1,0:T(8,128)(2,1)S(1)} all-gather(bf16[32,512]{1,0:T(8,128)(2,1)S(1)} %pad_maximum_fusion), channel_id=1, replica_groups=mesh['row'=16,'col'=8] {'col'}, dimensions={0}, use_global_device_ids=true | all-gather | bytes 294912 | tf_op jit(solution)/shard_map/all_gather | solution.py:563
  40.1 1.9 %shard_map.56 = (f32[512,1]{1,0:T(8,128)S(1)}, f32[8,512]{1,0:T(8,128)S(1)}, s32[8,512]{1,0:T(8,128)S(1)}) custom-call(s32[1]{0:T(128)} %bitcast.2.place, s32[2,256]{1,0:T(2,128)S(1)} %copy-done.2, s32[2,256]{1,0:T(2,128)S(1)} %copy-done.3), custom_call_target="tpu_custom_call" | custom-call | tf_op jit(solution)/shard_map/pallas_call | solution.py:86
  42.0 0.6 slice.40
  43.2 3.0 %shard_map.57.inv_ref = f32[2,256,256]{2,1,0:T(8,128)S(1)} custom-call(bf16[256,512]{1,0:T(8,128)(2,1)S(1)} %all_gather.6.d_ref), custom_call_target="tpu_custom_call" | custom-call | flops 1048576 | bytes 262144 | tf_op jit(solution)/shard_map/pallas_call | solution.py:252
  46.3 5.1 %all-to-all-done.1.r_hbm = bf16[16,576,128]{2,1,0:T(8,128)(2,1)} async-done(((bf16[16,576,128]{2,1,0:T(8,128)(2,1)}), bf16[16,576,128]{2,1,0:T(8,128)(2,1)}, u32[]{:S(2)}, u32[]{:S(2)}) %all-to-all-start.1) | async-done | bytes 2359328 | tf_op jit(solution)/shard_map/all_to_all | solution.py:541
  51.5 3.8 %shard_map.58 = (bf16[16,576,128]{2,1,0:T(8,128)(2,1)}, bf16[32,512]{1,0:T(8,128)(2,1)S(1)}, bf16[512,128]{1,0:T(8,128)(2,1)S(1)}) custom-call(f32[2,256,256]{2,1,0:T(8,128)S(1)} %shard_map.57.inv_ref, f32[512,1]{1,0:T(8,128)S(1)} %get-tuple-element.100.own_ref, f32[8,512]{1,0:T(8,128)S(1)} %get-tuple-element.101.key_ref, ...), custom_call_target="tpu_custom_call" | custom-call | flops 536870912 | bytes 4194304 | tf_op jit(solution)/shard_map/pallas_call | solution.py:316
  55.3 4.5 %all-to-all-start.2 = ((bf16[16,576,128]{2,1,0:T(8,128)(2,1)}), bf16[16,576,128]{2,1,0:T(8,128)(2,1)}, u32[]{:S(2)}, u32[]{:S(2)}) async-start(bf16[16,576,128]{2,1,0:T(8,128)(2,1)} %get-tuple-element.110), calls=%async_computation.2 | async-start | bytes 4718592 | tf_op jit(solution)/shard_map/all_to_all | solution.py:541
  59.8 0.1 collective-permute-start.4
  59.9 0.7 slice.38
  60.6 0.5 collective-permute-start.5
  61.1 0.7 slice.39
  61.8 3.1 %collective-permute-start.3 = (bf16[1,32,3072]{2,1,0:T(8,128)(2,1)}, bf16[1,32,3072]{2,1,0:T(8,128)(2,1)S(1)}, u32[]{:S(2)}, u32[]{:S(2)}) collective-permute-start(bf16[1,32,3072]{2,1,0:T(8,128)(2,1)} %slice.39), channel_id=1, source_target_pairs={{0,6},{1,7},{2,0},{3,1},{4,2},{5,3},{6,4},{7,5},{8,14},{9,15},{10,... | collective-permute-start | bytes 589832 | tf_op jit(solution)/shard_map/ppermute | solution.py:560
  65.0 0.1 copy.6.land_ref
  65.1 15.8 %all_gather.7 = bf16[256,512]{1,0:T(8,128)(2,1)S(1)} all-gather(bf16[32,512]{1,0:T(8,128)(2,1)S(1)} %get-tuple-element.105), channel_id=1, replica_groups=mesh['row'=16,'col'=8] {'col'}, dimensions={0}, use_global_device_ids=true | all-gather | bytes 294912 | tf_op jit(solution)/shard_map/all_gather | solution.py:573
  80.9 0.4 collective-permute-start.8
  81.2 0.2 collective-permute-start.7
  81.4 0.9 collective-permute-done.8.refs_9_
  82.3 0.4 collective-permute-done.7.refs_8_
  82.7 5.8 %shard_map.59 = (bf16[3072,512]{1,0:T(8,128)(2,1)}, f32[256,256]{1,0:T(8,128)}) custom-call(s32[3]{0:T(128)S(1)} %pad_add_fusion.where, f32[2,256,256]{2,1,0:T(8,128)S(1)} %shard_map.57.inv_ref, bf16[256,256]{1,0:T(8,128)(2,1)S(1)} %get-tuple-element.124.sel_ref, bf16[256,256]{1,0:T(8,128)(2,1)S(1)} %get-tuple-element.123.below_ref, ...), custom_call_target="tpu_custom_call" | custom-call | flops 16777216 | bytes 1048576 | tf_op jit(solution)/shard_map/pallas_call | solution.py:378
  88.5 2.1 %all-to-all-done.2.y_ref = bf16[16,576,128]{2,1,0:T(8,128)(2,1)} async-done(((bf16[16,576,128]{2,1,0:T(8,128)(2,1)}), bf16[16,576,128]{2,1,0:T(8,128)(2,1)}, u32[]{:S(2)}, u32[]{:S(2)}) %all-to-all-start.2) | async-done | bytes 2359328 | tf_op jit(solution)/shard_map/all_to_all | solution.py:541
  90.6 16.0 %shard_map.60 = bf16[3072,2048]{1,0:T(8,128)(2,1)} custom-call(s32[8,512]{1,0:T(8,128)} %copy-done.1, s32[1]{0:T(128)} %bitcast.2.place, f32[256,256]{1,0:T(8,128)} %get-tuple-element.108.w_ref, bf16[3072,2048]{1,0:T(8,128)(2,1)} %slab_ref.3, bf16[3072,512]{1,0:T(8,128)(2,1)} %get-tuple-element.109.l_hbm, bf16[16,576,128]{2,1,0:T(8,128)(2,1)} %all-to-all-done.2.y_ref, ...), custom_call_target="tpu_custom_call" | custom-call | flops 6442450944 | bytes 25165824 | tf_op jit(solution)/shard_map/pallas_call | solution.py:513
  (27 shorter events, 0.2 us)
Async XLA Ops:
  9.6 8.2 %copy-start = (bf16[2,32,3072]{2,1,0:T(8,128)(2,1)S(1)}, bf16[2,32,3072]{2,1,0:T(8,128)(2,1)}, u32[]{:S(2)}) copy-start(bf16[2,32,3072]{2,1,0:T(8,128)(2,1)} %refs_0_) | copy-start | bytes 1179652
  9.6 11.3 %copy-start.4 = (bf16[2,32,256]{2,1,0:T(8,128)(2,1)S(1)}, bf16[2,32,256]{2,1,0:T(8,128)(2,1)}, u32[]{:S(2)}) copy-start(bf16[2,32,256]{2,1,0:T(8,128)(2,1)} %param.9) | copy-start | bytes 98308
  9.6 30.5 %copy-start.2 = (s32[2,256]{1,0:T(2,128)S(1)}, s32[2,256]{1,0:T(2,128)}, u32[]{:S(2)}) copy-start(s32[2,256]{1,0:T(2,128)} %src_ref.2) | copy-start | bytes 6148
  9.6 30.5 %copy-start.3 = (s32[2,256]{1,0:T(2,128)S(1)}, s32[2,256]{1,0:T(2,128)}, u32[]{:S(2)}) copy-start(s32[2,256]{1,0:T(2,128)} %dst_ref.2) | copy-start | bytes 6148
  9.6 41.8 %all-to-all-start.1 = ((bf16[16,576,128]{2,1,0:T(8,128)(2,1)}), bf16[16,576,128]{2,1,0:T(8,128)(2,1)}, u32[]{:S(2)}, u32[]{:S(2)}) async-start(bf16[16,576,128]{2,1,0:T(8,128)(2,1)} %shard_map.55), calls=%async_computation.1 | async-start | bytes 4718592 | tf_op jit(solution)/shard_map/all_to_all | solution.py:541
  17.7 28.6 %collective-permute-start.1 = (bf16[2,32,3072]{2,1,0:T(8,128)(2,1)S(1)}, bf16[2,32,3072]{2,1,0:T(8,128)(2,1)S(1)}, u32[]{:S(2)}, u32[]{:S(2)}) collective-permute-start(bf16[2,32,3072]{2,1,0:T(8,128)(2,1)S(1)} %copy-done), channel_id=1, source_target_pairs={{0,6},{1,7},{2,0},{3,1},{4,2},{5,3},{6,4},{7,5},{8,14},{9,15},{10,... | collective-permute-start | bytes 1179656 | tf_op jit(solution)/shard_map/ppermute | solution.py:560
  20.9 25.5 %collective-permute-start = (bf16[2,32,3072]{2,1,0:T(8,128)(2,1)S(1)}, bf16[2,32,3072]{2,1,0:T(8,128)(2,1)S(1)}, u32[]{:S(2)}, u32[]{:S(2)}) collective-permute-start(bf16[2,32,3072]{2,1,0:T(8,128)(2,1)S(1)} %copy-done), channel_id=1, source_target_pairs={{0,2},{1,3},{2,4},{3,5},{4,6},{5,7},{6,0},{7,1},{8,10},{9,11},{10,... | collective-permute-start | bytes 1179656 | tf_op jit(solution)/shard_map/ppermute | solution.py:560
  42.0 13.3 %copy-start.1 = (s32[8,512]{1,0:T(8,128)}, s32[8,512]{1,0:T(8,128)S(1)}, u32[]{:S(2)}) copy-start(s32[8,512]{1,0:T(8,128)S(1)} %get-tuple-element.98.table) | copy-start | bytes 49156
  55.3 35.2 %all-to-all-start.2 = ((bf16[16,576,128]{2,1,0:T(8,128)(2,1)}), bf16[16,576,128]{2,1,0:T(8,128)(2,1)}, u32[]{:S(2)}, u32[]{:S(2)}) async-start(bf16[16,576,128]{2,1,0:T(8,128)(2,1)} %get-tuple-element.110), calls=%async_computation.2 | async-start | bytes 4718592 | tf_op jit(solution)/shard_map/all_to_all | solution.py:541
  59.8 21.6 %collective-permute-start.4 = (bf16[2,32,3072]{2,1,0:T(8,128)(2,1)S(1)}, bf16[2,32,3072]{2,1,0:T(8,128)(2,1)S(1)}, u32[]{:S(2)}, u32[]{:S(2)}) collective-permute-start(bf16[2,32,3072]{2,1,0:T(8,128)(2,1)S(1)} %copy-done), channel_id=1, source_target_pairs={{0,1},{1,0},{2,3},{3,2},{4,5},{5,4},{6,7},{7,6},{8,9},{9,8},{10,11... | collective-permute-start | bytes 1179656 | tf_op jit(solution)/shard_map/ppermute | solution.py:580
  60.6 20.8 %collective-permute-start.5 = (bf16[2,32,3072]{2,1,0:T(8,128)(2,1)S(1)}, bf16[2,32,3072]{2,1,0:T(8,128)(2,1)S(1)}, u32[]{:S(2)}, u32[]{:S(2)}) collective-permute-start(bf16[2,32,3072]{2,1,0:T(8,128)(2,1)S(1)} %collective-permute-done.refs_1_), channel_id=1, source_target_pairs={{0,1},{1,0},{2,3},{3,2},{4,5},{5,4},{6,7},{7,6},{8,9},{9,8},{10,11... | collective-permute-start | bytes 1179656 | tf_op jit(solution)/shard_map/ppermute | solution.py:580
  61.8 19.7 %collective-permute-start.6 = (bf16[2,32,3072]{2,1,0:T(8,128)(2,1)S(1)}, bf16[2,32,3072]{2,1,0:T(8,128)(2,1)S(1)}, u32[]{:S(2)}, u32[]{:S(2)}) collective-permute-start(bf16[2,32,3072]{2,1,0:T(8,128)(2,1)S(1)} %collective-permute-done.1.refs_2_), channel_id=1, source_target_pairs={{0,1},{1,0},{2,3},{3,2},{4,5},{5,4},{6,7},{7,6},{8,9},{9,8},{10,11... | collective-permute-start | bytes 1179656 | tf_op jit(solution)/shard_map/ppermute | solution.py:580
  61.8 19.1 %collective-permute-start.3 = (bf16[1,32,3072]{2,1,0:T(8,128)(2,1)}, bf16[1,32,3072]{2,1,0:T(8,128)(2,1)S(1)}, u32[]{:S(2)}, u32[]{:S(2)}) collective-permute-start(bf16[1,32,3072]{2,1,0:T(8,128)(2,1)} %slice.39), channel_id=1, source_target_pairs={{0,6},{1,7},{2,0},{3,1},{4,2},{5,3},{6,4},{7,5},{8,14},{9,15},{10,... | collective-permute-start | bytes 589832 | tf_op jit(solution)/shard_map/ppermute | solution.py:560
  64.9 16.4 %collective-permute-start.2 = (bf16[1,32,3072]{2,1,0:T(8,128)(2,1)}, bf16[1,32,3072]{2,1,0:T(8,128)(2,1)S(1)}, u32[]{:S(2)}, u32[]{:S(2)}) collective-permute-start(bf16[1,32,3072]{2,1,0:T(8,128)(2,1)} %slice.38), channel_id=1, source_target_pairs={{0,2},{1,3},{2,4},{3,5},{4,6},{5,7},{6,0},{7,1},{8,10},{9,11},{10,... | collective-permute-start | bytes 589832 | tf_op jit(solution)/shard_map/ppermute | solution.py:560
  80.9 1.4 %collective-permute-start.8 = (bf16[1,32,3072]{2,1,0:T(8,128)(2,1)S(1)}, bf16[1,32,3072]{2,1,0:T(8,128)(2,1)S(1)}, u32[]{:S(2)}, u32[]{:S(2)}) collective-permute-start(bf16[1,32,3072]{2,1,0:T(8,128)(2,1)S(1)} %collective-permute-done.3.refs_4_), channel_id=1, source_target_pairs={{0,1},{1,0},{2,3},{3,2},{4,5},{5,4},{6,7},{7,6},{8,9},{9,8},{10,11... | collective-permute-start | bytes 589832 | tf_op jit(solution)/shard_map/ppermute | solution.py:580
  81.2 1.4 %collective-permute-start.7 = (bf16[1,32,3072]{2,1,0:T(8,128)(2,1)S(1)}, bf16[1,32,3072]{2,1,0:T(8,128)(2,1)S(1)}, u32[]{:S(2)}, u32[]{:S(2)}) collective-permute-start(bf16[1,32,3072]{2,1,0:T(8,128)(2,1)S(1)} %collective-permute-done.2.refs_3_), channel_id=1, source_target_pairs={{0,1},{1,0},{2,3},{3,2},{4,5},{5,4},{6,7},{7,6},{8,9},{9,8},{10,11... | collective-permute-start | bytes 589832 | tf_op jit(solution)/shard_map/ppermute | solution.py:580

commit v8 on v7

--- a/solution.py
+++ b/solution.py
@@ -181,7 +181,7 @@
     height, cols = slab.shape
     width = pivot_src.shape[1]
     slots, part = 2 * width, cols // devices
-    chunk = min(LANES, slots)
+    chunk = min(64, slots)
     most = slots // chunk
     tiles = min(4, devices)
     piece = panels.shape[1]
@@ -423,11 +423,12 @@
                 pltpu.make_async_copy(l_hbm.at[here], l_ref.at[here], ins.at[1, i]),
             )
         )
-    for copy in (*uppers, *fills):
+    ahead = 3
+    for copy in (*uppers, *fills, *loads[0]):
         copy.start()
     for copy in (*uppers, *fills):
         copy.wait()
-    for copy in sum((list(pair) for pair in loads[:2]), []):
+    for copy in sum((list(pair) for pair in loads[1:ahead]), []):
         copy.start()
     high = w_ref[...].astype(BF16)
     rest = (w_ref[...] - high.astype(F32)).astype(BF16)
@@ -470,8 +471,8 @@
     for i, here in enumerate(block):
         for copy in loads[i]:
             copy.wait()
-        if i + 2 < steps:
-            for copy in loads[i + 2]:
+        if i + ahead < steps:
+            for copy in loads[i + ahead]:
                 copy.start()
         slot = i % 2
 

time: 107 us -> 107 us (level)
  no operation moved by 1% of the time
where the time goes in v8:
time: 107 us
  Pallas kernels  40.2 us (38%)
  blocking collectives  35 us (33%)
  starting transfers between devices  19.8 us (19%)
  waiting for transfers between devices  8.51 us (8%)
  local copies, waits for them, and re-layouts  2.12 us (2%)
    all_gather x1, blocking collectives, per_device(): lax.all_gather(jnp.concatenate([diag_lower[0], diag_lower[1]], axis=1), '...  19.3 us
    pallas_call x1, Pallas kernels, update(): pl.pallas_call(functools.partial(update_kernel, width, rows), out_shape=j...  16.1 us
    all_gather x1, blocking collectives, per_device(): small = lax.all_gather(small, 'col', axis=0, tiled=True)  15.8 us
    all_to_all x2, starting transfers between devices, exchange(): return lax.all_to_all(x, 'row', 0, 0)  12.6 us
    pallas_call x1, Pallas kernels, gather(): pl.pallas_call(functools.partial(gather_kernel, height, chunk, tiles), ou...  9.61 us
    all_to_all x2, waiting for transfers between devices, exchange(): return lax.all_to_all(x, 'row', 0, 0)  7.26 us
    ppermute x4, starting transfers between devices, forward(): lax.ppermute(x, 'col', [(d, (d + 2 * chips_on) % columns) for d in range(...  6.13 us
    pallas_call x1, Pallas kernels, arrange(): pl.pallas_call(functools.partial(arrange_kernel, width, chips, origins),...  5.8 us
  transfers between devices with their start and end apart: 11, of which 4 were waited for; matrix products, arithmetic and copies ran while one was open for 2% of the time, Pallas kernels for 10%

profile of v8, /device:TPU:0, one launch (start us, length us, event | category | flops | bytes accessed | tf_op | source)
XLA Modules:
  0.0 106.9 jit_solution(13213780040347185126)
XLA Ops:
  0.0 9.6 %shard_map.55 = bf16[16,576,128]{2,1,0:T(8,128)(2,1)} custom-call(s32[1]{0:T(128)} %bitcast.2.place, s32[2,256]{1,0:T(2,128)} %src_ref.2, s32[2,256]{1,0:T(2,128)} %dst_ref.2, bf16[2,32,3072]{2,1,0:T(8,128)(2,1)} %refs_0_, bf16[3072,2048]{1,0:T(8,128)(2,1)} %slab_ref.3), custom_call_target="tpu_custom_call" | custom-call | flops 3221225472 | bytes 14680064 | tf_op jit(solution)/shard_map/pallas_call | solution.py:189
  9.7 8.1 %all-to-all-start.1 = ((bf16[16,576,128]{2,1,0:T(8,128)(2,1)}), bf16[16,576,128]{2,1,0:T(8,128)(2,1)}, u32[]{:S(2)}, u32[]{:S(2)}) async-start(bf16[16,576,128]{2,1,0:T(8,128)(2,1)} %shard_map.55), calls=%async_computation.1 | async-start | bytes 4718592 | tf_op jit(solution)/shard_map/all_to_all | solution.py:542
  17.8 3.1 %collective-permute-start.1 = (bf16[2,32,3072]{2,1,0:T(8,128)(2,1)S(1)}, bf16[2,32,3072]{2,1,0:T(8,128)(2,1)S(1)}, u32[]{:S(2)}, u32[]{:S(2)}) collective-permute-start(bf16[2,32,3072]{2,1,0:T(8,128)(2,1)S(1)} %copy-done), channel_id=1, source_target_pairs={{0,6},{1,7},{2,0},{3,1},{4,2},{5,3},{6,4},{7,5},{8,14},{9,15},{10,... | collective-permute-start | bytes 1179656 | tf_op jit(solution)/shard_map/ppermute | solution.py:561
  20.9 19.3 %all_gather.6.d_ref = bf16[256,512]{1,0:T(8,128)(2,1)S(1)} all-gather(bf16[32,512]{1,0:T(8,128)(2,1)S(1)} %pad_maximum_fusion), channel_id=1, replica_groups=mesh['row'=16,'col'=8] {'col'}, dimensions={0}, use_global_device_ids=true | all-gather | bytes 294912 | tf_op jit(solution)/shard_map/all_gather | solution.py:564
  40.2 1.9 %shard_map.56 = (f32[512,1]{1,0:T(8,128)S(1)}, f32[8,512]{1,0:T(8,128)S(1)}, s32[8,512]{1,0:T(8,128)S(1)}) custom-call(s32[1]{0:T(128)} %bitcast.2.place, s32[2,256]{1,0:T(2,128)S(1)} %copy-done.2, s32[2,256]{1,0:T(2,128)S(1)} %copy-done.3), custom_call_target="tpu_custom_call" | custom-call | tf_op jit(solution)/shard_map/pallas_call | solution.py:86
  42.1 0.6 slice.40
  43.3 3.0 %shard_map.57.inv_ref = f32[2,256,256]{2,1,0:T(8,128)S(1)} custom-call(bf16[256,512]{1,0:T(8,128)(2,1)S(1)} %all_gather.6.d_ref), custom_call_target="tpu_custom_call" | custom-call | flops 1048576 | bytes 262144 | tf_op jit(solution)/shard_map/pallas_call | solution.py:252
  46.4 5.2 %all-to-all-done.1.r_hbm = bf16[16,576,128]{2,1,0:T(8,128)(2,1)} async-done(((bf16[16,576,128]{2,1,0:T(8,128)(2,1)}), bf16[16,576,128]{2,1,0:T(8,128)(2,1)}, u32[]{:S(2)}, u32[]{:S(2)}) %all-to-all-start.1) | async-done | bytes 2359328 | tf_op jit(solution)/shard_map/all_to_all | solution.py:542
  51.5 3.8 %shard_map.58 = (bf16[16,576,128]{2,1,0:T(8,128)(2,1)}, bf16[32,512]{1,0:T(8,128)(2,1)S(1)}, bf16[512,128]{1,0:T(8,128)(2,1)S(1)}) custom-call(f32[2,256,256]{2,1,0:T(8,128)S(1)} %shard_map.57.inv_ref, f32[512,1]{1,0:T(8,128)S(1)} %get-tuple-element.100.own_ref, f32[8,512]{1,0:T(8,128)S(1)} %get-tuple-element.101.key_ref, ...), custom_call_target="tpu_custom_call" | custom-call | flops 536870912 | bytes 4194304 | tf_op jit(solution)/shard_map/pallas_call | solution.py:316
  55.4 4.5 %all-to-all-start.2 = ((bf16[16,576,128]{2,1,0:T(8,128)(2,1)}), bf16[16,576,128]{2,1,0:T(8,128)(2,1)}, u32[]{:S(2)}, u32[]{:S(2)}) async-start(bf16[16,576,128]{2,1,0:T(8,128)(2,1)} %get-tuple-element.110), calls=%async_computation.2 | async-start | bytes 4718592 | tf_op jit(solution)/shard_map/all_to_all | solution.py:542
  59.9 0.1 collective-permute-start.4
  60.0 0.7 slice.38
  60.7 0.5 collective-permute-start.5
  61.2 0.7 slice.39
  61.9 3.0 %collective-permute-start.3 = (bf16[1,32,3072]{2,1,0:T(8,128)(2,1)}, bf16[1,32,3072]{2,1,0:T(8,128)(2,1)S(1)}, u32[]{:S(2)}, u32[]{:S(2)}) collective-permute-start(bf16[1,32,3072]{2,1,0:T(8,128)(2,1)} %slice.39), channel_id=1, source_target_pairs={{0,6},{1,7},{2,0},{3,1},{4,2},{5,3},{6,4},{7,5},{8,14},{9,15},{10,... | collective-permute-start | bytes 589832 | tf_op jit(solution)/shard_map/ppermute | solution.py:561
  65.0 0.1 copy.6.land_ref
  65.2 15.8 %all_gather.7 = bf16[256,512]{1,0:T(8,128)(2,1)S(1)} all-gather(bf16[32,512]{1,0:T(8,128)(2,1)S(1)} %get-tuple-element.105), channel_id=1, replica_groups=mesh['row'=16,'col'=8] {'col'}, dimensions={0}, use_global_device_ids=true | all-gather | bytes 294912 | tf_op jit(solution)/shard_map/all_gather | solution.py:574
  81.0 0.4 collective-permute-start.8
  81.3 0.2 collective-permute-start.7
  81.5 0.9 collective-permute-done.8.refs_9_
  82.4 0.4 collective-permute-done.7.refs_8_
  82.8 5.8 %shard_map.59 = (bf16[3072,512]{1,0:T(8,128)(2,1)}, f32[256,256]{1,0:T(8,128)}) custom-call(s32[3]{0:T(128)S(1)} %pad_add_fusion.where, f32[2,256,256]{2,1,0:T(8,128)S(1)} %shard_map.57.inv_ref, bf16[256,256]{1,0:T(8,128)(2,1)S(1)} %get-tuple-element.124.sel_ref, bf16[256,256]{1,0:T(8,128)(2,1)S(1)} %get-tuple-element.123.below_ref, ...), custom_call_target="tpu_custom_call" | custom-call | flops 16777216 | bytes 1048576 | tf_op jit(solution)/shard_map/pallas_call | solution.py:378
  88.6 2.1 %all-to-all-done.2.y_ref = bf16[16,576,128]{2,1,0:T(8,128)(2,1)} async-done(((bf16[16,576,128]{2,1,0:T(8,128)(2,1)}), bf16[16,576,128]{2,1,0:T(8,128)(2,1)}, u32[]{:S(2)}, u32[]{:S(2)}) %all-to-all-start.2) | async-done | bytes 2359328 | tf_op jit(solution)/shard_map/all_to_all | solution.py:542
  90.7 16.1 %shard_map.60 = bf16[3072,2048]{1,0:T(8,128)(2,1)} custom-call(s32[8,512]{1,0:T(8,128)} %copy-done.1, s32[1]{0:T(128)} %bitcast.2.place, f32[256,256]{1,0:T(8,128)} %get-tuple-element.108.w_ref, bf16[3072,2048]{1,0:T(8,128)(2,1)} %slab_ref.3, bf16[3072,512]{1,0:T(8,128)(2,1)} %get-tuple-element.109.l_hbm, bf16[16,576,128]{2,1,0:T(8,128)(2,1)} %all-to-all-done.2.y_ref, ...), custom_call_target="tpu_custom_call" | custom-call | flops 6442450944 | bytes 25165824 | tf_op jit(solution)/shard_map/pallas_call | solution.py:514
  (27 shorter events, 0.2 us)
Async XLA Ops:
  9.6 8.2 %copy-start = (bf16[2,32,3072]{2,1,0:T(8,128)(2,1)S(1)}, bf16[2,32,3072]{2,1,0:T(8,128)(2,1)}, u32[]{:S(2)}) copy-start(bf16[2,32,3072]{2,1,0:T(8,128)(2,1)} %refs_0_) | copy-start | bytes 1179652
  9.6 11.3 %copy-start.4 = (bf16[2,32,256]{2,1,0:T(8,128)(2,1)S(1)}, bf16[2,32,256]{2,1,0:T(8,128)(2,1)}, u32[]{:S(2)}) copy-start(bf16[2,32,256]{2,1,0:T(8,128)(2,1)} %param.9) | copy-start | bytes 98308
  9.6 30.6 %copy-start.2 = (s32[2,256]{1,0:T(2,128)S(1)}, s32[2,256]{1,0:T(2,128)}, u32[]{:S(2)}) copy-start(s32[2,256]{1,0:T(2,128)} %src_ref.2) | copy-start | bytes 6148
  9.7 30.5 %copy-start.3 = (s32[2,256]{1,0:T(2,128)S(1)}, s32[2,256]{1,0:T(2,128)}, u32[]{:S(2)}) copy-start(s32[2,256]{1,0:T(2,128)} %dst_ref.2) | copy-start | bytes 6148
  9.7 41.9 %all-to-all-start.1 = ((bf16[16,576,128]{2,1,0:T(8,128)(2,1)}), bf16[16,576,128]{2,1,0:T(8,128)(2,1)}, u32[]{:S(2)}, u32[]{:S(2)}) async-start(bf16[16,576,128]{2,1,0:T(8,128)(2,1)} %shard_map.55), calls=%async_computation.1 | async-start | bytes 4718592 | tf_op jit(solution)/shard_map/all_to_all | solution.py:542
  17.8 28.5 %collective-permute-start.1 = (bf16[2,32,3072]{2,1,0:T(8,128)(2,1)S(1)}, bf16[2,32,3072]{2,1,0:T(8,128)(2,1)S(1)}, u32[]{:S(2)}, u32[]{:S(2)}) collective-permute-start(bf16[2,32,3072]{2,1,0:T(8,128)(2,1)S(1)} %copy-done), channel_id=1, source_target_pairs={{0,6},{1,7},{2,0},{3,1},{4,2},{5,3},{6,4},{7,5},{8,14},{9,15},{10,... | collective-permute-start | bytes 1179656 | tf_op jit(solution)/shard_map/ppermute | solution.py:561
  20.9 25.5 %collective-permute-start = (bf16[2,32,3072]{2,1,0:T(8,128)(2,1)S(1)}, bf16[2,32,3072]{2,1,0:T(8,128)(2,1)S(1)}, u32[]{:S(2)}, u32[]{:S(2)}) collective-permute-start(bf16[2,32,3072]{2,1,0:T(8,128)(2,1)S(1)} %copy-done), channel_id=1, source_target_pairs={{0,2},{1,3},{2,4},{3,5},{4,6},{5,7},{6,0},{7,1},{8,10},{9,11},{10,... | collective-permute-start | bytes 1179656 | tf_op jit(solution)/shard_map/ppermute | solution.py:561
  42.1 13.3 %copy-start.1 = (s32[8,512]{1,0:T(8,128)}, s32[8,512]{1,0:T(8,128)S(1)}, u32[]{:S(2)}) copy-start(s32[8,512]{1,0:T(8,128)S(1)} %get-tuple-element.98.table) | copy-start | bytes 49156
  55.4 35.2 %all-to-all-start.2 = ((bf16[16,576,128]{2,1,0:T(8,128)(2,1)}), bf16[16,576,128]{2,1,0:T(8,128)(2,1)}, u32[]{:S(2)}, u32[]{:S(2)}) async-start(bf16[16,576,128]{2,1,0:T(8,128)(2,1)} %get-tuple-element.110), calls=%async_computation.2 | async-start | bytes 4718592 | tf_op jit(solution)/shard_map/all_to_all | solution.py:542
  59.9 21.6 %collective-permute-start.4 = (bf16[2,32,3072]{2,1,0:T(8,128)(2,1)S(1)}, bf16[2,32,3072]{2,1,0:T(8,128)(2,1)S(1)}, u32[]{:S(2)}, u32[]{:S(2)}) collective-permute-start(bf16[2,32,3072]{2,1,0:T(8,128)(2,1)S(1)} %copy-done), channel_id=1, source_target_pairs={{0,1},{1,0},{2,3},{3,2},{4,5},{5,4},{6,7},{7,6},{8,9},{9,8},{10,11... | collective-permute-start | bytes 1179656 | tf_op jit(solution)/shard_map/ppermute | solution.py:581
  60.7 20.8 %collective-permute-start.5 = (bf16[2,32,3072]{2,1,0:T(8,128)(2,1)S(1)}, bf16[2,32,3072]{2,1,0:T(8,128)(2,1)S(1)}, u32[]{:S(2)}, u32[]{:S(2)}) collective-permute-start(bf16[2,32,3072]{2,1,0:T(8,128)(2,1)S(1)} %collective-permute-done.refs_1_), channel_id=1, source_target_pairs={{0,1},{1,0},{2,3},{3,2},{4,5},{5,4},{6,7},{7,6},{8,9},{9,8},{10,11... | collective-permute-start | bytes 1179656 | tf_op jit(solution)/shard_map/ppermute | solution.py:581
  61.9 19.7 %collective-permute-start.6 = (bf16[2,32,3072]{2,1,0:T(8,128)(2,1)S(1)}, bf16[2,32,3072]{2,1,0:T(8,128)(2,1)S(1)}, u32[]{:S(2)}, u32[]{:S(2)}) collective-permute-start(bf16[2,32,3072]{2,1,0:T(8,128)(2,1)S(1)} %collective-permute-done.1.refs_2_), channel_id=1, source_target_pairs={{0,1},{1,0},{2,3},{3,2},{4,5},{5,4},{6,7},{7,6},{8,9},{9,8},{10,11... | collective-permute-start | bytes 1179656 | tf_op jit(solution)/shard_map/ppermute | solution.py:581
  61.9 19.0 %collective-permute-start.3 = (bf16[1,32,3072]{2,1,0:T(8,128)(2,1)}, bf16[1,32,3072]{2,1,0:T(8,128)(2,1)S(1)}, u32[]{:S(2)}, u32[]{:S(2)}) collective-permute-start(bf16[1,32,3072]{2,1,0:T(8,128)(2,1)} %slice.39), channel_id=1, source_target_pairs={{0,6},{1,7},{2,0},{3,1},{4,2},{5,3},{6,4},{7,5},{8,14},{9,15},{10,... | collective-permute-start | bytes 589832 | tf_op jit(solution)/shard_map/ppermute | solution.py:561
  64.9 16.4 %collective-permute-start.2 = (bf16[1,32,3072]{2,1,0:T(8,128)(2,1)}, bf16[1,32,3072]{2,1,0:T(8,128)(2,1)S(1)}, u32[]{:S(2)}, u32[]{:S(2)}) collective-permute-start(bf16[1,32,3072]{2,1,0:T(8,128)(2,1)} %slice.38), channel_id=1, source_target_pairs={{0,2},{1,3},{2,4},{3,5},{4,6},{5,7},{6,0},{7,1},{8,10},{9,11},{10,... | collective-permute-start | bytes 589832 | tf_op jit(solution)/shard_map/ppermute | solution.py:561
  81.0 1.4 %collective-permute-start.8 = (bf16[1,32,3072]{2,1,0:T(8,128)(2,1)S(1)}, bf16[1,32,3072]{2,1,0:T(8,128)(2,1)S(1)}, u32[]{:S(2)}, u32[]{:S(2)}) collective-permute-start(bf16[1,32,3072]{2,1,0:T(8,128)(2,1)S(1)} %collective-permute-done.3.refs_4_), channel_id=1, source_target_pairs={{0,1},{1,0},{2,3},{3,2},{4,5},{5,4},{6,7},{7,6},{8,9},{9,8},{10,11... | collective-permute-start | bytes 589832 | tf_op jit(solution)/shard_map/ppermute | solution.py:581
  81.3 1.4 %collective-permute-start.7 = (bf16[1,32,3072]{2,1,0:T(8,128)(2,1)S(1)}, bf16[1,32,3072]{2,1,0:T(8,128)(2,1)S(1)}, u32[]{:S(2)}, u32[]{:S(2)}) collective-permute-start(bf16[1,32,3072]{2,1,0:T(8,128)(2,1)S(1)} %collective-permute-done.2.refs_3_), channel_id=1, source_target_pairs={{0,1},{1,0},{2,3},{3,2},{4,5},{5,4},{6,7},{7,6},{8,9},{9,8},{10,11... | collective-permute-start | bytes 589832 | tf_op jit(solution)/shard_map/ppermute | solution.py:581

commit v9 on v6

--- a/solution.py
+++ b/solution.py
@@ -259,7 +259,7 @@
 
 def apply_inverse(inverse, rows):
     total = None
-    for _ in range(3):
+    for _ in range(2):
         part = inverse.astype(BF16)
         inverse = inverse - part.astype(F32)
         term = dot(part, rows)
@@ -287,11 +287,10 @@
         fills = fill_ref.at[d * CAP : (d + 1) * CAP]
         sends.append(pltpu.make_async_copy(fills, y_ref.at[d, slots:], outs.at[0, d]))
         sends[-1].start()
-    total = jnp.where(own_ref[...] > 0, zero.astype(F32), 0.0)
+    rows = jnp.where(own_ref[...] > 0, zero.astype(F32), 0.0).astype(BF16)
     for s in range(1, devices):
         loads[s].wait()
-        total = total + r_ref[s, :slots, :].astype(F32)
-    rows = total.astype(BF16)
+        rows = rows + r_ref[s, :slots, :]
     for k in range(2):
         here = slice(k * width, (k + 1) * width)
         u_ref[here, :] = apply_inverse(inv_ref[k], rows[here])
@@ -302,10 +301,10 @@
         have = min(part, width - h * part)
         at = slice(slots + h * piece, slots + (h + 1) * piece)
         moving = r_ref[0, at, :have]
-        picked = jnp.where(key_ref[1:2, h * part : h * part + have] > 0, moving.astype(F32), 0.0)
+        picked = jnp.where(key_ref[1:2, h * part : h * part + have] > 0, moving.astype(F32), 0.0).astype(BF16)
         for s in range(1, devices):
-            picked = picked + r_ref[s, at, :have].astype(F32)
-        small_ref[:, h * part : h * part + have] = picked.astype(BF16)
+            picked = picked + r_ref[s, at, :have]
+        small_ref[:, h * part : h * part + have] = picked
         small_ref[:, width + h * part : width + h * part + have] = moving
     for send in sends:
         send.wait()

time: 107 us -> 106 us (level)
  no operation moved by 1% of the time
where the time goes in v9:
time: 106 us
  Pallas kernels  39.2 us (37%)
  blocking collectives  35 us (33%)
  starting transfers between devices  19.8 us (19%)
  waiting for transfers between devices  8.51 us (8%)
  local copies, waits for them, and re-layouts  2.12 us (2%)
  between operations  1.06 us (1%)
    all_gather x1, blocking collectives, per_device(): lax.all_gather(jnp.concatenate([diag_lower[0], diag_lower[1]], axis=1), '...  19.3 us
    all_gather x1, blocking collectives, per_device(): small = lax.all_gather(small, 'col', axis=0, tiled=True)  15.8 us
    pallas_call x1, Pallas kernels, update(): pl.pallas_call(functools.partial(update_kernel, width, rows), out_shape=j...  15.1 us
    all_to_all x2, starting transfers between devices, exchange(): return lax.all_to_all(x, 'row', 0, 0)  12.5 us
    pallas_call x1, Pallas kernels, gather(): pl.pallas_call(functools.partial(gather_kernel, height, chunk, tiles), ou...  9.56 us
    all_to_all x2, waiting for transfers between devices, exchange(): return lax.all_to_all(x, 'row', 0, 0)  7.26 us
    ppermute x4, starting transfers between devices, forward(): lax.ppermute(x, 'col', [(d, (d + 2 * chips_on) % columns) for d in range(...  6.19 us
    pallas_call x1, Pallas kernels, arrange(): pl.pallas_call(functools.partial(arrange_kernel, width, chips, origins),...  5.8 us
  transfers between devices with their start and end apart: 11, of which 4 were waited for; matrix products, arithmetic and copies ran while one was open for 2% of the time, Pallas kernels for 10%

profile of v9, /device:TPU:0, one launch (start us, length us, event | category | flops | bytes accessed | tf_op | source)
XLA Modules:
  0.0 105.9 jit_solution(6185082175854546575)
XLA Ops:
  0.0 9.6 %shard_map.55 = bf16[16,576,128]{2,1,0:T(8,128)(2,1)} custom-call(s32[1]{0:T(128)} %bitcast.2.place, s32[2,256]{1,0:T(2,128)} %src_ref.2, s32[2,256]{1,0:T(2,128)} %dst_ref.2, bf16[2,32,3072]{2,1,0:T(8,128)(2,1)} %refs_0_, bf16[3072,2048]{1,0:T(8,128)(2,1)} %slab_ref.3), custom_call_target="tpu_custom_call" | custom-call | flops 3221225472 | bytes 14680064 | tf_op jit(solution)/shard_map/pallas_call | solution.py:189
  9.6 8.1 %all-to-all-start.1 = ((bf16[16,576,128]{2,1,0:T(8,128)(2,1)}), bf16[16,576,128]{2,1,0:T(8,128)(2,1)}, u32[]{:S(2)}, u32[]{:S(2)}) async-start(bf16[16,576,128]{2,1,0:T(8,128)(2,1)} %shard_map.55), calls=%async_computation.1 | async-start | bytes 4718592 | tf_op jit(solution)/shard_map/all_to_all | solution.py:529
  17.7 3.1 %collective-permute-start.1 = (bf16[2,32,3072]{2,1,0:T(8,128)(2,1)S(1)}, bf16[2,32,3072]{2,1,0:T(8,128)(2,1)S(1)}, u32[]{:S(2)}, u32[]{:S(2)}) collective-permute-start(bf16[2,32,3072]{2,1,0:T(8,128)(2,1)S(1)} %copy-done), channel_id=1, source_target_pairs={{0,6},{1,7},{2,0},{3,1},{4,2},{5,3},{6,4},{7,5},{8,14},{9,15},{10,... | collective-permute-start | bytes 1179656 | tf_op jit(solution)/shard_map/ppermute | solution.py:548
  20.9 19.3 %all_gather.6.d_ref = bf16[256,512]{1,0:T(8,128)(2,1)S(1)} all-gather(bf16[32,512]{1,0:T(8,128)(2,1)S(1)} %pad_maximum_fusion), channel_id=1, replica_groups=mesh['row'=16,'col'=8] {'col'}, dimensions={0}, use_global_device_ids=true | all-gather | bytes 294912 | tf_op jit(solution)/shard_map/all_gather | solution.py:551
  40.1 1.9 %shard_map.56 = (f32[512,1]{1,0:T(8,128)S(1)}, f32[8,512]{1,0:T(8,128)S(1)}, s32[8,512]{1,0:T(8,128)S(1)}) custom-call(s32[1]{0:T(128)} %bitcast.2.place, s32[2,256]{1,0:T(2,128)S(1)} %copy-done.2, s32[2,256]{1,0:T(2,128)S(1)} %copy-done.3), custom_call_target="tpu_custom_call" | custom-call | tf_op jit(solution)/shard_map/pallas_call | solution.py:86
  42.0 0.6 slice.40
  43.2 3.0 %shard_map.57.inv_ref = f32[2,256,256]{2,1,0:T(8,128)S(1)} custom-call(bf16[256,512]{1,0:T(8,128)(2,1)S(1)} %all_gather.6.d_ref), custom_call_target="tpu_custom_call" | custom-call | flops 1048576 | bytes 262144 | tf_op jit(solution)/shard_map/pallas_call | solution.py:252
  46.3 5.1 %all-to-all-done.1.r_hbm = bf16[16,576,128]{2,1,0:T(8,128)(2,1)} async-done(((bf16[16,576,128]{2,1,0:T(8,128)(2,1)}), bf16[16,576,128]{2,1,0:T(8,128)(2,1)}, u32[]{:S(2)}, u32[]{:S(2)}) %all-to-all-start.1) | async-done | bytes 2359328 | tf_op jit(solution)/shard_map/all_to_all | solution.py:529
  51.5 3.8 %shard_map.58 = (bf16[16,576,128]{2,1,0:T(8,128)(2,1)}, bf16[32,512]{1,0:T(8,128)(2,1)S(1)}, bf16[512,128]{1,0:T(8,128)(2,1)S(1)}) custom-call(f32[2,256,256]{2,1,0:T(8,128)S(1)} %shard_map.57.inv_ref, f32[512,1]{1,0:T(8,128)S(1)} %get-tuple-element.100.own_ref, f32[8,512]{1,0:T(8,128)S(1)} %get-tuple-element.101.key_ref, ...), custom_call_target="tpu_custom_call" | custom-call | flops 536870912 | bytes 4194304 | tf_op jit(solution)/shard_map/pallas_call | solution.py:316
  55.3 4.5 %all-to-all-start.2 = ((bf16[16,576,128]{2,1,0:T(8,128)(2,1)}), bf16[16,576,128]{2,1,0:T(8,128)(2,1)}, u32[]{:S(2)}, u32[]{:S(2)}) async-start(bf16[16,576,128]{2,1,0:T(8,128)(2,1)} %get-tuple-element.110), calls=%async_computation.2 | async-start | bytes 4718592 | tf_op jit(solution)/shard_map/all_to_all | solution.py:529
  59.8 0.1 collective-permute-start.4
  59.9 0.7 slice.38
  60.6 0.5 collective-permute-start.5
  61.1 0.7 slice.39
  61.8 3.1 %collective-permute-start.3 = (bf16[1,32,3072]{2,1,0:T(8,128)(2,1)}, bf16[1,32,3072]{2,1,0:T(8,128)(2,1)S(1)}, u32[]{:S(2)}, u32[]{:S(2)}) collective-permute-start(bf16[1,32,3072]{2,1,0:T(8,128)(2,1)} %slice.39), channel_id=1, source_target_pairs={{0,6},{1,7},{2,0},{3,1},{4,2},{5,3},{6,4},{7,5},{8,14},{9,15},{10,... | collective-permute-start | bytes 589832 | tf_op jit(solution)/shard_map/ppermute | solution.py:548
  65.0 0.1 copy.6.land_ref
  65.1 15.8 %all_gather.7 = bf16[256,512]{1,0:T(8,128)(2,1)S(1)} all-gather(bf16[32,512]{1,0:T(8,128)(2,1)S(1)} %get-tuple-element.105), channel_id=1, replica_groups=mesh['row'=16,'col'=8] {'col'}, dimensions={0}, use_global_device_ids=true | all-gather | bytes 294912 | tf_op jit(solution)/shard_map/all_gather | solution.py:561
  80.9 0.4 collective-permute-start.8
  81.2 0.2 collective-permute-start.7
  81.4 0.9 collective-permute-done.8.refs_9_
  82.3 0.4 collective-permute-done.7.refs_8_
  82.7 5.8 %shard_map.59 = (bf16[3072,512]{1,0:T(8,128)(2,1)}, f32[256,256]{1,0:T(8,128)}) custom-call(s32[3]{0:T(128)S(1)} %pad_add_fusion.where, f32[2,256,256]{2,1,0:T(8,128)S(1)} %shard_map.57.inv_ref, bf16[256,256]{1,0:T(8,128)(2,1)S(1)} %get-tuple-element.124.sel_ref, bf16[256,256]{1,0:T(8,128)(2,1)S(1)} %get-tuple-element.123.below_ref, ...), custom_call_target="tpu_custom_call" | custom-call | flops 16777216 | bytes 1048576 | tf_op jit(solution)/shard_map/pallas_call | solution.py:378
  88.5 2.1 %all-to-all-done.2.y_ref = bf16[16,576,128]{2,1,0:T(8,128)(2,1)} async-done(((bf16[16,576,128]{2,1,0:T(8,128)(2,1)}), bf16[16,576,128]{2,1,0:T(8,128)(2,1)}, u32[]{:S(2)}, u32[]{:S(2)}) %all-to-all-start.2) | async-done | bytes 2359328 | tf_op jit(solution)/shard_map/all_to_all | solution.py:529
  90.6 15.1 %shard_map.60 = bf16[3072,2048]{1,0:T(8,128)(2,1)} custom-call(s32[8,512]{1,0:T(8,128)} %copy-done.1, s32[1]{0:T(128)} %bitcast.2.place, f32[256,256]{1,0:T(8,128)} %get-tuple-element.108.w_ref, bf16[3072,2048]{1,0:T(8,128)(2,1)} %slab_ref.3, bf16[3072,512]{1,0:T(8,128)(2,1)} %get-tuple-element.109.l_hbm, bf16[16,576,128]{2,1,0:T(8,128)(2,1)} %all-to-all-done.2.y_ref, ...), custom_call_target="tpu_custom_call" | custom-call | flops 6442450944 | bytes 25165824 | tf_op jit(solution)/shard_map/pallas_call | solution.py:502
  (27 shorter events, 0.2 us)
Async XLA Ops:
  9.6 8.2 %copy-start = (bf16[2,32,3072]{2,1,0:T(8,128)(2,1)S(1)}, bf16[2,32,3072]{2,1,0:T(8,128)(2,1)}, u32[]{:S(2)}) copy-start(bf16[2,32,3072]{2,1,0:T(8,128)(2,1)} %refs_0_) | copy-start | bytes 1179652
  9.6 11.3 %copy-start.4 = (bf16[2,32,256]{2,1,0:T(8,128)(2,1)S(1)}, bf16[2,32,256]{2,1,0:T(8,128)(2,1)}, u32[]{:S(2)}) copy-start(bf16[2,32,256]{2,1,0:T(8,128)(2,1)} %param.9) | copy-start | bytes 98308
  9.6 30.5 %copy-start.2 = (s32[2,256]{1,0:T(2,128)S(1)}, s32[2,256]{1,0:T(2,128)}, u32[]{:S(2)}) copy-start(s32[2,256]{1,0:T(2,128)} %src_ref.2) | copy-start | bytes 6148
  9.6 30.5 %copy-start.3 = (s32[2,256]{1,0:T(2,128)S(1)}, s32[2,256]{1,0:T(2,128)}, u32[]{:S(2)}) copy-start(s32[2,256]{1,0:T(2,128)} %dst_ref.2) | copy-start | bytes 6148
  9.6 41.8 %all-to-all-start.1 = ((bf16[16,576,128]{2,1,0:T(8,128)(2,1)}), bf16[16,576,128]{2,1,0:T(8,128)(2,1)}, u32[]{:S(2)}, u32[]{:S(2)}) async-start(bf16[16,576,128]{2,1,0:T(8,128)(2,1)} %shard_map.55), calls=%async_computation.1 | async-start | bytes 4718592 | tf_op jit(solution)/shard_map/all_to_all | solution.py:529
  17.7 28.6 %collective-permute-start.1 = (bf16[2,32,3072]{2,1,0:T(8,128)(2,1)S(1)}, bf16[2,32,3072]{2,1,0:T(8,128)(2,1)S(1)}, u32[]{:S(2)}, u32[]{:S(2)}) collective-permute-start(bf16[2,32,3072]{2,1,0:T(8,128)(2,1)S(1)} %copy-done), channel_id=1, source_target_pairs={{0,6},{1,7},{2,0},{3,1},{4,2},{5,3},{6,4},{7,5},{8,14},{9,15},{10,... | collective-permute-start | bytes 1179656 | tf_op jit(solution)/shard_map/ppermute | solution.py:548
  20.9 25.5 %collective-permute-start = (bf16[2,32,3072]{2,1,0:T(8,128)(2,1)S(1)}, bf16[2,32,3072]{2,1,0:T(8,128)(2,1)S(1)}, u32[]{:S(2)}, u32[]{:S(2)}) collective-permute-start(bf16[2,32,3072]{2,1,0:T(8,128)(2,1)S(1)} %copy-done), channel_id=1, source_target_pairs={{0,2},{1,3},{2,4},{3,5},{4,6},{5,7},{6,0},{7,1},{8,10},{9,11},{10,... | collective-permute-start | bytes 1179656 | tf_op jit(solution)/shard_map/ppermute | solution.py:548
  42.0 13.3 %copy-start.1 = (s32[8,512]{1,0:T(8,128)}, s32[8,512]{1,0:T(8,128)S(1)}, u32[]{:S(2)}) copy-start(s32[8,512]{1,0:T(8,128)S(1)} %get-tuple-element.98.table) | copy-start | bytes 49156
  55.3 35.2 %all-to-all-start.2 = ((bf16[16,576,128]{2,1,0:T(8,128)(2,1)}), bf16[16,576,128]{2,1,0:T(8,128)(2,1)}, u32[]{:S(2)}, u32[]{:S(2)}) async-start(bf16[16,576,128]{2,1,0:T(8,128)(2,1)} %get-tuple-element.110), calls=%async_computation.2 | async-start | bytes 4718592 | tf_op jit(solution)/shard_map/all_to_all | solution.py:529
  59.8 21.6 %collective-permute-start.4 = (bf16[2,32,3072]{2,1,0:T(8,128)(2,1)S(1)}, bf16[2,32,3072]{2,1,0:T(8,128)(2,1)S(1)}, u32[]{:S(2)}, u32[]{:S(2)}) collective-permute-start(bf16[2,32,3072]{2,1,0:T(8,128)(2,1)S(1)} %copy-done), channel_id=1, source_target_pairs={{0,1},{1,0},{2,3},{3,2},{4,5},{5,4},{6,7},{7,6},{8,9},{9,8},{10,11... | collective-permute-start | bytes 1179656 | tf_op jit(solution)/shard_map/ppermute | solution.py:568
  60.6 20.8 %collective-permute-start.5 = (bf16[2,32,3072]{2,1,0:T(8,128)(2,1)S(1)}, bf16[2,32,3072]{2,1,0:T(8,128)(2,1)S(1)}, u32[]{:S(2)}, u32[]{:S(2)}) collective-permute-start(bf16[2,32,3072]{2,1,0:T(8,128)(2,1)S(1)} %collective-permute-done.refs_1_), channel_id=1, source_target_pairs={{0,1},{1,0},{2,3},{3,2},{4,5},{5,4},{6,7},{7,6},{8,9},{9,8},{10,11... | collective-permute-start | bytes 1179656 | tf_op jit(solution)/shard_map/ppermute | solution.py:568
  61.8 19.7 %collective-permute-start.6 = (bf16[2,32,3072]{2,1,0:T(8,128)(2,1)S(1)}, bf16[2,32,3072]{2,1,0:T(8,128)(2,1)S(1)}, u32[]{:S(2)}, u32[]{:S(2)}) collective-permute-start(bf16[2,32,3072]{2,1,0:T(8,128)(2,1)S(1)} %collective-permute-done.1.refs_2_), channel_id=1, source_target_pairs={{0,1},{1,0},{2,3},{3,2},{4,5},{5,4},{6,7},{7,6},{8,9},{9,8},{10,11... | collective-permute-start | bytes 1179656 | tf_op jit(solution)/shard_map/ppermute | solution.py:568
  61.8 19.1 %collective-permute-start.3 = (bf16[1,32,3072]{2,1,0:T(8,128)(2,1)}, bf16[1,32,3072]{2,1,0:T(8,128)(2,1)S(1)}, u32[]{:S(2)}, u32[]{:S(2)}) collective-permute-start(bf16[1,32,3072]{2,1,0:T(8,128)(2,1)} %slice.39), channel_id=1, source_target_pairs={{0,6},{1,7},{2,0},{3,1},{4,2},{5,3},{6,4},{7,5},{8,14},{9,15},{10,... | collective-permute-start | bytes 589832 | tf_op jit(solution)/shard_map/ppermute | solution.py:548
  64.9 16.4 %collective-permute-start.2 = (bf16[1,32,3072]{2,1,0:T(8,128)(2,1)}, bf16[1,32,3072]{2,1,0:T(8,128)(2,1)S(1)}, u32[]{:S(2)}, u32[]{:S(2)}) collective-permute-start(bf16[1,32,3072]{2,1,0:T(8,128)(2,1)} %slice.38), channel_id=1, source_target_pairs={{0,2},{1,3},{2,4},{3,5},{4,6},{5,7},{6,0},{7,1},{8,10},{9,11},{10,... | collective-permute-start | bytes 589832 | tf_op jit(solution)/shard_map/ppermute | solution.py:548
  80.9 1.4 %collective-permute-start.8 = (bf16[1,32,3072]{2,1,0:T(8,128)(2,1)S(1)}, bf16[1,32,3072]{2,1,0:T(8,128)(2,1)S(1)}, u32[]{:S(2)}, u32[]{:S(2)}) collective-permute-start(bf16[1,32,3072]{2,1,0:T(8,128)(2,1)S(1)} %collective-permute-done.3.refs_4_), channel_id=1, source_target_pairs={{0,1},{1,0},{2,3},{3,2},{4,5},{5,4},{6,7},{7,6},{8,9},{9,8},{10,11... | collective-permute-start | bytes 589832 | tf_op jit(solution)/shard_map/ppermute | solution.py:568
  81.2 1.4 %collective-permute-start.7 = (bf16[1,32,3072]{2,1,0:T(8,128)(2,1)S(1)}, bf16[1,32,3072]{2,1,0:T(8,128)(2,1)S(1)}, u32[]{:S(2)}, u32[]{:S(2)}) collective-permute-start(bf16[1,32,3072]{2,1,0:T(8,128)(2,1)S(1)} %collective-permute-done.2.refs_3_), channel_id=1, source_target_pairs={{0,1},{1,0},{2,3},{3,2},{4,5},{5,4},{6,7},{7,6},{8,9},{9,8},{10,11... | collective-permute-start | bytes 589832 | tf_op jit(solution)/shard_map/ppermute | solution.py:568
